TPU v7x, 256 devices: a whole 4x4x8 slice. The times are simulated.
256 devices in a mesh: head: 4 (over x_hi, core), blk: 64 (over z, x_lo, y).
Axes of the slice: x: 4 (x_hi: 2, x_lo: 2; x = x_hi * 2 + x_lo), y: 4, z: 8, core: 2. Of those that a mesh axis runs over, the one named last changes fastest.
Arguments:
- query: bfloat16 [32768, 8192], P(('blk', 'head'))
- key: bfloat16 [32768, 1024], P(('blk', 'head'))
- value: bfloat16 [32768, 1024], P(('blk', 'head')), may hold values from -6 to 6
- output_gradient: bfloat16 [32768, 8192], P(('blk', 'head')), may hold values from -6 to 6
- pair_codes: int32 [64, 8, 8], P('blk'), may hold values from 0 to 15
- pair_counts: int32 [64, 8], P('blk'), may hold values from 1 to 8
Outputs:
- attn_out: bfloat16 [32768, 8192], P(('blk', 'head'))
- grad_query: bfloat16 [32768, 8192], P(('blk', 'head'))
- key_gradient: bfloat16 [32768, 1024], P(('blk', 'head'))
- value_gradient: bfloat16 [32768, 1024], P(('blk', 'head'))
All inputs are finite; a program needn't handle non-finite values.
Results may differ from a plain program's by a relative error of at most 0.015.
Values may be sent and summed in bfloat16 or wider, within the bound.
No kernel may reach another device: no remote copies, remote signals or barrier semaphores. Data moves between devices by JAX's collectives and lax.ppermute only.
A program may use at most 128 MiB of HBM per device.

v0:
```python
import jax
import jax.numpy as jnp
from jax import lax
from jax.sharding import PartitionSpec as P

QUERY_HEADS = 64
KEY_VALUE_HEADS = 8
HEAD_SIZE = 128
BLOCK = 128


NEGATIVE_FILL = -1e30


def from_behind(block, axis, distance):
    devices = range(lax.axis_size(axis))
    route = [((i - distance) % len(devices), i) for i in devices]
    return lax.ppermute(block, axis, route)


def block_scores(q_blk, k_blk, query_block, key_block, first_step, score_scale):
    scores = (
        jnp.einsum("qhgd,khd->hgqk", q_blk, k_blk, preferred_element_type=jnp.float32) * score_scale
    )
    if first_step:
        rows_at = lax.broadcasted_iota(jnp.int32, scores.shape, 2)
        cols_at = lax.broadcasted_iota(jnp.int32, scores.shape, 3)
        allowed = jnp.logical_or(key_block != query_block, cols_at <= rows_at)
        scores = jnp.where(allowed, scores, NEGATIVE_FILL)
    return scores


def forward_pairs(loop_state, queries, kv_pair, codes, count, first_step, score_scale, nblocks):

    def forward_visit(index, carry):
        best, total, acc = carry
        code = codes[index]
        query_block = code // nblocks
        key_block = code % nblocks
        q_blk = lax.dynamic_slice_in_dim(queries, query_block * BLOCK, BLOCK, 0)
        kv_blk = lax.dynamic_slice_in_dim(kv_pair, key_block * BLOCK, BLOCK, 1)
        scores = block_scores(q_blk, kv_blk[0], query_block, key_block, first_step, score_scale)
        best_old = lax.dynamic_slice_in_dim(best, query_block * BLOCK, BLOCK, 2)
        total_old = lax.dynamic_slice_in_dim(total, query_block * BLOCK, BLOCK, 2)
        acc_old = lax.dynamic_slice_in_dim(acc, query_block * BLOCK, BLOCK, 0)
        best_new = jnp.maximum(best_old, jnp.max(scores, axis=-1))
        factor = jnp.exp(best_old - best_new)
        weights = jnp.exp(scores - best_new[..., None])
        total_new = factor * total_old + jnp.sum(weights, axis=-1)
        mixed = jnp.einsum(
            "hgqk,khd->qhgd",
            weights.astype(jnp.bfloat16),
            kv_blk[1],
            preferred_element_type=jnp.float32,
        )
        acc_new = jnp.transpose(factor, (2, 0, 1))[..., None] * acc_old + mixed
        best = lax.dynamic_update_slice_in_dim(best, best_new, query_block * BLOCK, 2)
        total = lax.dynamic_update_slice_in_dim(total, total_new, query_block * BLOCK, 2)
        acc = lax.dynamic_update_slice_in_dim(acc, acc_new, query_block * BLOCK, 0)
        return (best, total, acc)

    return lax.fori_loop(0, count, forward_visit, loop_state)


def backward_pairs(
    loop_state,
    queries,
    grads,
    kv_pair,
    log_total,
    row_dot,
    codes,
    count,
    first_step,
    score_scale,
    nblocks,
):

    def backward_visit(index, carry):
        query_gradient, kv_grad = carry
        code = codes[index]
        query_block = code // nblocks
        key_block = code % nblocks
        q_blk = lax.dynamic_slice_in_dim(queries, query_block * BLOCK, BLOCK, 0)
        g_blk = lax.dynamic_slice_in_dim(grads, query_block * BLOCK, BLOCK, 0)
        kv_blk = lax.dynamic_slice_in_dim(kv_pair, key_block * BLOCK, BLOCK, 1)
        scores = block_scores(q_blk, kv_blk[0], query_block, key_block, first_step, score_scale)
        lse_blk = lax.dynamic_slice_in_dim(log_total, query_block * BLOCK, BLOCK, 2)
        row_blk = lax.dynamic_slice_in_dim(row_dot, query_block * BLOCK, BLOCK, 2)
        prob = jnp.exp(scores - lse_blk[..., None])
        value_part = jnp.einsum(
            "hgqk,qhgd->khd", prob.astype(jnp.bfloat16), g_blk, preferred_element_type=jnp.float32
        )
        dprob = jnp.einsum("qhgd,khd->hgqk", g_blk, kv_blk[1], preferred_element_type=jnp.float32)
        dscore = (prob * (dprob - row_blk[..., None])).astype(jnp.bfloat16)
        query_part = jnp.einsum(
            "hgqk,khd->qhgd", dscore, kv_blk[0], preferred_element_type=jnp.float32
        )
        key_part = jnp.einsum("hgqk,qhgd->khd", dscore, q_blk, preferred_element_type=jnp.float32)
        old_query = lax.dynamic_slice_in_dim(query_gradient, query_block * BLOCK, BLOCK, 0)
        query_gradient = lax.dynamic_update_slice_in_dim(
            query_gradient, old_query + query_part, query_block * BLOCK, 0
        )
        old_kv = lax.dynamic_slice_in_dim(kv_grad, key_block * BLOCK, BLOCK, 1)
        kv_grad = lax.dynamic_update_slice_in_dim(
            kv_grad, old_kv + jnp.stack((key_part, value_part)), key_block * BLOCK, 1
        )
        return (query_gradient, kv_grad)

    return lax.fori_loop(0, count, backward_visit, loop_state)


def body(query, key, value, output_gradient, pair_codes, pair_counts):
    score_scale = HEAD_SIZE ** (-0.5)
    q_rows, k_rows, v_rows, g_rows = (
        lax.all_to_all(query, "head", split_axis=1, concat_axis=0, tiled=True),
        lax.all_to_all(key, "head", split_axis=1, concat_axis=0, tiled=True),
        lax.all_to_all(value, "head", split_axis=1, concat_axis=0, tiled=True),
        lax.all_to_all(output_gradient, "head", split_axis=1, concat_axis=0, tiled=True),
    )
    row_count_local = q_rows.shape[0]
    kv_local = k_rows.shape[1] // HEAD_SIZE
    device_sharding = QUERY_HEADS // KEY_VALUE_HEADS
    nblocks = row_count_local // BLOCK
    queries = q_rows.reshape(row_count_local, kv_local, device_sharding, HEAD_SIZE)
    grads = g_rows.reshape(row_count_local, kv_local, device_sharding, HEAD_SIZE)
    kv_home = jnp.stack(
        (
            k_rows.reshape(row_count_local, kv_local, HEAD_SIZE),
            v_rows.reshape(row_count_local, kv_local, HEAD_SIZE),
        )
    )
    codes = pair_codes[0]
    counts = pair_counts[0]
    nstep = codes.shape[0]
    loop_state = (
        jnp.full((kv_local, device_sharding, row_count_local), NEGATIVE_FILL, jnp.float32),
        jnp.zeros((kv_local, device_sharding, row_count_local), jnp.float32),
        jnp.zeros((row_count_local, kv_local, device_sharding, HEAD_SIZE), jnp.float32),
    )
    seen = []
    kv_now = kv_home
    for step in range(nstep):
        seen.append(kv_now)
        loop_state = forward_pairs(
            loop_state, queries, kv_now, codes[step], counts[step], step == 0, score_scale, nblocks
        )
        if step + 1 < nstep:
            kv_now = from_behind(kv_now, "blk", 1)
    best, total, acc = loop_state
    attn = (acc / jnp.transpose(total, (2, 0, 1))[..., None]).astype(jnp.bfloat16)
    log_total = best + jnp.log(total)
    row_dot = jnp.einsum("qhgd,qhgd->hgq", grads, attn, preferred_element_type=jnp.float32)
    query_gradient = jnp.zeros((row_count_local, kv_local, device_sharding, HEAD_SIZE), jnp.float32)
    empty_key_value = jnp.zeros((2, row_count_local, kv_local, HEAD_SIZE), jnp.float32)
    kv_now = kv_home
    kv_grad = empty_key_value
    for step in range(nstep):
        query_gradient, kv_grad = backward_pairs(
            (query_gradient, kv_grad),
            queries,
            grads,
            kv_now,
            log_total,
            row_dot,
            codes[step],
            counts[step],
            step == 0,
            score_scale,
            nblocks,
        )
        if step + 1 < nstep:
            kv_now = from_behind(kv_now, "blk", 1)
            kv_grad = from_behind(kv_grad, "blk", 1)
    kv_grad = from_behind(kv_grad.astype(jnp.bfloat16), "blk", 1 - nstep).astype(kv_grad.dtype)
    attn_rows = attn.reshape(row_count_local, kv_local * device_sharding * HEAD_SIZE)
    query_rows = (
        (query_gradient * score_scale)
        .astype(jnp.bfloat16)
        .reshape(row_count_local, kv_local * device_sharding * HEAD_SIZE)
    )
    key_rows = (
        (kv_grad[0] * score_scale)
        .astype(jnp.bfloat16)
        .reshape(row_count_local, kv_local * HEAD_SIZE)
    )
    value_rows = kv_grad[1].astype(jnp.bfloat16).reshape(row_count_local, kv_local * HEAD_SIZE)
    attn_out, grad_query, key_gradient, value_gradient = (
        lax.all_to_all(attn_rows, "head", split_axis=0, concat_axis=1, tiled=True),
        lax.all_to_all(query_rows, "head", split_axis=0, concat_axis=1, tiled=True),
        lax.all_to_all(key_rows, "head", split_axis=0, concat_axis=1, tiled=True),
        lax.all_to_all(value_rows, "head", split_axis=0, concat_axis=1, tiled=True),
    )
    return (attn_out, grad_query, key_gradient, value_gradient)


def solution(mesh):
    return jax.shard_map(
        body,
        mesh=mesh,
        in_specs=(
            P(("blk", "head"), None),
            P(("blk", "head"), None),
            P(("blk", "head"), None),
            P(("blk", "head"), None),
            P("blk", None, None),
            P("blk", None),
        ),
        out_specs=(
            P(("blk", "head"), None),
            P(("blk", "head"), None),
            P(("blk", "head"), None),
            P(("blk", "head"), None),
        ),
        check_vma=False,
    )
```

profile of v0, /device:TPU:192, one launch (start us, length us, event | category | flops | bytes accessed | tf_op | source)
XLA Modules:
  0.0 1049.5 jit_solution(12218740734922193370)
XLA Ops:
  2.3 4.3 all-to-all-start
  8.3 5.8 all-to-all-done
  20.7 4.3 all-to-all-done.1
  30.8 15.8 %collective-permute-done = bf16[2,512,2,128]{3,2,1,0:T(2,128)(2,1)S(1)} collective-permute-done((bf16[2,512,2,128]{3,2,1,0:T(2,128)(2,1)S(1)}, bf16[2,512,2,128]{3,2,1,0:T(2,128)(2,1)S(1)}, u32[]{:S(2)}, u32[]{:S(2)}) %collective-permute-start) | collective-permute-done | bytes 524320 | tf_op jit(solution)/shard_map/ppermute | solution.py:18
  52.2 11.0 %collective-permute-done.1 = bf16[2,512,2,128]{3,2,1,0:T(2,128)(2,1)} collective-permute-done((bf16[2,512,2,128]{3,2,1,0:T(2,128)(2,1)S(1)}, bf16[2,512,2,128]{3,2,1,0:T(2,128)(2,1)}, u32[]{:S(2)}, u32[]{:S(2)}) %collective-permute-start.1) | collective-permute-done | bytes 524320 | tf_op jit(solution)/shard_map/ppermute | solution.py:18
  65.1 4.5 all-to-all-start.4
  73.3 48.1 %while.240 = (s32[]{:T(128)}, f32[2,8,512]{2,1,0:T(8,128)S(1)}, f32[2,8,512]{2,1,0:T(8,128)S(1)}, f32[512,2,8,128]{0,3,2,1:T(8,128)}, s32[]{:T(128)}, /*index=5*...) while((s32[]{:T(128)}, f32[2,8,512]{2,1,0:T(8,128)S(1)}, ...), condition=%wide.region_3.4_spmd, body=%wide.region_0.3_spmd.sunk | while | flops 137107488 | bytes 6021660 | solution.py:62
  121.4 24.3 %while.241 = (s32[]{:T(128)}, f32[2,8,512]{2,1,0:T(8,128)S(1)}, f32[2,8,512]{2,1,0:T(8,128)S(1)}, f32[512,2,8,128]{0,3,2,1:T(8,128)}, s32[]{:T(128)}, /*index=5*...) while((s32[]{:T(128)}, f32[2,8,512]{2,1,0:T(8,128)S(1)}, ...), condition=%wide.region_7.8_spmd, body=%wide.region_4.7_spmd.sunk | while | flops 136321056 | bytes 6021650 | solution.py:62
  145.8 32.0 %while.242 = (s32[]{:T(128)}, f32[2,8,512]{2,1,0:T(8,128)S(1)}, f32[2,8,512]{2,1,0:T(8,128)S(1)}, f32[512,2,8,128]{0,3,2,1:T(8,128)}, s32[]{:T(128)}, /*index=5*...) while((s32[]{:T(128)}, f32[2,8,512]{2,1,0:T(8,128)S(1)}, ...), condition=%wide.region_11.12_spmd, body=%wide.region_8.11_spmd.sunk | while | flops 136321056 | bytes 6021650 | solution.py:62
  185.2 24.6 %while.243 = (s32[]{:T(128)}, f32[2,8,512]{2,1,0:T(8,128)S(1)}, f32[2,8,512]{2,1,0:T(8,128)S(1)}, f32[512,2,8,128]{0,3,2,1:T(8,128)}, s32[]{:T(128)}, /*index=5*...) while((s32[]{:T(128)}, f32[2,8,512]{2,1,0:T(8,128)S(1)}, ...), condition=%wide.region_15.16_spmd, body=%wide.region_12.15_spmd.sunk | while | flops 136321056 | bytes 6021650 | solution.py:62
  209.8 15.9 %collective-permute-done.3 = bf16[2,512,2,128]{3,2,1,0:T(2,128)(2,1)} collective-permute-done((bf16[2,512,2,128]{3,2,1,0:T(2,128)(2,1)}, bf16[2,512,2,128]{3,2,1,0:T(2,128)(2,1)}, u32[]{:S(2)}, u32[]{:S(2)}) %collective-permute-start.3) | collective-permute-done | bytes 524320 | tf_op jit(solution)/shard_map/ppermute | solution.py:18
  227.6 8.9 while.244
  236.5 15.6 %collective-permute-done.4 = bf16[2,512,2,128]{3,2,1,0:T(2,128)(2,1)} collective-permute-done((bf16[2,512,2,128]{3,2,1,0:T(2,128)(2,1)}, bf16[2,512,2,128]{3,2,1,0:T(2,128)(2,1)}, u32[]{:S(2)}, u32[]{:S(2)}) %collective-permute-start.4) | collective-permute-done | bytes 524320 | tf_op jit(solution)/shard_map/ppermute | solution.py:18
  254.1 8.6 while.245
  262.7 24.0 %collective-permute-done.5 = bf16[2,512,2,128]{3,2,1,0:T(2,128)(2,1)} collective-permute-done((bf16[2,512,2,128]{3,2,1,0:T(2,128)(2,1)}, bf16[2,512,2,128]{3,2,1,0:T(2,128)(2,1)}, u32[]{:S(2)}, u32[]{:S(2)}) %collective-permute-start.5) | collective-permute-done | bytes 524320 | tf_op jit(solution)/shard_map/ppermute | solution.py:18
  288.6 8.5 while.246
  297.2 8.5 collective-permute-done.6
  307.5 32.0 %while.247 = (s32[]{:T(128)}, f32[2,8,512]{2,1,0:T(8,128)S(1)}, f32[2,8,512]{2,1,0:T(8,128)S(1)}, f32[512,2,8,128]{0,3,2,1:T(8,128)}, s32[]{:T(128)}, /*index=5*...) while((s32[]{:T(128)}, f32[2,8,512]{2,1,0:T(8,128)S(1)}, ...), condition=%wide.region_31.32_spmd, body=%wide.region_28.31_spmd.sunk | while | flops 136321056 | bytes 6021650 | solution.py:62
  339.6 5.6 bitcast_convert_fusion
  345.2 5.4 copy.531
  350.6 4.3 multiply_reduce_fusion
  358.7 76.2 %while.248 = (s32[]{:T(128)}, f32[512,2,8,128]{0,3,2,1:T(8,128)}, f32[2,512,2,128]{1,3,2,0:T(8,128)}, s32[]{:T(128)}, s32[8]{0:T(128)S(1)}, /*index=5*/bf16[2,51...) while((s32[]{:T(128)}, f32[512,2,8,128]{0,3,2,1:T(8,128)}, ...), condition=%wide.region_33.34_spmd, body=%wide.region_32.33_spmd.sunk | while | flops 338296864 | bytes 10207804 | solution.py:110
  435.0 35.6 %collective-permute-done.7 = f32[2,512,2,128]{1,3,2,0:T(8,128)} collective-permute-done((f32[2,512,2,128]{1,3,2,0:T(8,128)}, f32[2,512,2,128]{1,3,2,0:T(8,128)}, u32[]{:S(2)}, u32[]{:S(2)}) %collective-permute-start.7) | collective-permute-done | bytes 1048608 | tf_op jit(solution)/shard_map/ppermute | solution.py:18
  470.7 38.4 %while.249 = (s32[]{:T(128)}, f32[512,2,8,128]{0,3,2,1:T(8,128)}, f32[2,512,2,128]{1,3,2,0:T(8,128)}, s32[]{:T(128)}, s32[8]{0:T(128)S(1)}, /*index=5*/bf16[2,51...) while((s32[]{:T(128)}, f32[512,2,8,128]{0,3,2,1:T(8,128)}, ...), condition=%wide.region_35.36_spmd, body=%wide.region_34.35_spmd.sunk | while | flops 337510432 | bytes 10207794 | solution.py:110
  509.4 27.4 %collective-permute-done.8 = f32[2,512,2,128]{1,3,2,0:T(8,128)} collective-permute-done((f32[2,512,2,128]{1,3,2,0:T(8,128)}, f32[2,512,2,128]{1,3,2,0:T(8,128)}, u32[]{:S(2)}, u32[]{:S(2)}) %collective-permute-start.8) | collective-permute-done | bytes 1048608 | tf_op jit(solution)/shard_map/ppermute | solution.py:18
  536.8 50.7 %while.250 = (s32[]{:T(128)}, f32[512,2,8,128]{0,3,2,1:T(8,128)}, f32[2,512,2,128]{1,3,2,0:T(8,128)}, s32[]{:T(128)}, s32[8]{0:T(128)S(1)}, /*index=5*/bf16[2,51...) while((s32[]{:T(128)}, f32[512,2,8,128]{0,3,2,1:T(8,128)}, ...), condition=%wide.region_37.38_spmd, body=%wide.region_36.37_spmd.sunk | while | flops 337510432 | bytes 10207794 | solution.py:110
  587.5 80.9 %collective-permute-done.9 = f32[2,512,2,128]{1,3,2,0:T(8,128)} collective-permute-done((f32[2,512,2,128]{1,3,2,0:T(8,128)}, f32[2,512,2,128]{1,3,2,0:T(8,128)}, u32[]{:S(2)}, u32[]{:S(2)}) %collective-permute-start.9) | collective-permute-done | bytes 1048608 | tf_op jit(solution)/shard_map/ppermute | solution.py:18
  668.4 38.7 %while.251 = (s32[]{:T(128)}, f32[512,2,8,128]{0,3,2,1:T(8,128)}, f32[2,512,2,128]{1,3,2,0:T(8,128)}, s32[]{:T(128)}, s32[8]{0:T(128)S(1)}, /*index=5*/bf16[2,51...) while((s32[]{:T(128)}, f32[512,2,8,128]{0,3,2,1:T(8,128)}, ...), condition=%wide.region_39.40_spmd, body=%wide.region_38.39_spmd.sunk | while | flops 337510432 | bytes 10207794 | solution.py:110
  707.2 26.0 %collective-permute-done.10 = f32[2,512,2,128]{1,3,2,0:T(8,128)} collective-permute-done((f32[2,512,2,128]{1,3,2,0:T(8,128)}, f32[2,512,2,128]{1,3,2,0:T(8,128)}, u32[]{:S(2)}, u32[]{:S(2)}) %collective-permute-start.10) | collective-permute-done | bytes 1048608 | tf_op jit(solution)/shard_map/ppermute | solution.py:18
  733.2 13.1 %while.252 = (s32[]{:T(128)}, f32[512,2,8,128]{0,3,2,1:T(8,128)}, f32[2,512,2,128]{1,3,2,0:T(8,128)}, s32[]{:T(128)}, s32[8]{0:T(128)S(1)}, /*index=5*/bf16[2,51...) while((s32[]{:T(128)}, f32[512,2,8,128]{0,3,2,1:T(8,128)}, ...), condition=%wide.region_41.42_spmd, body=%wide.region_40.41_spmd.sunk | while | flops 337510432 | bytes 10207794 | solution.py:110
  746.3 10.0 collective-permute-start.11
  756.3 47.7 %collective-permute-done.11 = f32[2,512,2,128]{1,3,2,0:T(8,128)} collective-permute-done((f32[2,512,2,128]{1,3,2,0:T(8,128)}, f32[2,512,2,128]{1,3,2,0:T(8,128)}, u32[]{:S(2)}, u32[]{:S(2)}) %collective-permute-start.11) | collective-permute-done | bytes 1048608 | tf_op jit(solution)/shard_map/ppermute | solution.py:18
  804.0 13.3 %while.253 = (s32[]{:T(128)}, f32[512,2,8,128]{0,3,2,1:T(8,128)}, f32[2,512,2,128]{1,3,2,0:T(8,128)}, s32[]{:T(128)}, s32[8]{0:T(128)S(1)}, /*index=5*/bf16[2,51...) while((s32[]{:T(128)}, f32[512,2,8,128]{0,3,2,1:T(8,128)}, ...), condition=%wide.region_43.44_spmd, body=%wide.region_42.43_spmd.sunk | while | flops 337510432 | bytes 10207794 | solution.py:110
  817.3 33.9 %collective-permute-done.12 = f32[2,512,2,128]{1,3,2,0:T(8,128)} collective-permute-done((f32[2,512,2,128]{1,3,2,0:T(8,128)}, f32[2,512,2,128]{1,3,2,0:T(8,128)}, u32[]{:S(2)}, u32[]{:S(2)}) %collective-permute-start.12) | collective-permute-done | bytes 1048608 | tf_op jit(solution)/shard_map/ppermute | solution.py:18
  851.2 13.2 %while.254 = (s32[]{:T(128)}, f32[512,2,8,128]{0,3,2,1:T(8,128)}, f32[2,512,2,128]{1,3,2,0:T(8,128)}, s32[]{:T(128)}, s32[8]{0:T(128)S(1)}, /*index=5*/bf16[2,51...) while((s32[]{:T(128)}, f32[512,2,8,128]{0,3,2,1:T(8,128)}, ...), condition=%wide.region_45.46_spmd, body=%wide.region_44.45_spmd.sunk | while | flops 337510432 | bytes 10207794 | solution.py:110
  865.3 4.0 reshape.182
  869.2 4.3 copy.565
  873.5 4.5 all-to-all-start.3
  877.9 45.0 %collective-permute-done.13 = f32[2,512,2,128]{1,3,2,0:T(8,128)} collective-permute-done((f32[2,512,2,128]{1,3,2,0:T(8,128)}, f32[2,512,2,128]{1,3,2,0:T(8,128)}, u32[]{:S(2)}, u32[]{:S(2)}) %collective-permute-start.13) | collective-permute-done | bytes 1048608 | tf_op jit(solution)/shard_map/ppermute | solution.py:18
  923.0 50.6 %while.255 = (s32[]{:T(128)}, f32[512,2,8,128]{0,3,2,1:T(8,128)}, f32[2,512,2,128]{1,3,2,0:T(8,128)}, s32[]{:T(128)}, s32[8]{0:T(128)S(1)}, /*index=5*/bf16[2,51...) while((s32[]{:T(128)}, f32[512,2,8,128]{0,3,2,1:T(8,128)}, ...), condition=%wide.region_47.48_spmd, body=%wide.region_46.47_spmd.sunk | while | flops 337510432 | bytes 10207794 | solution.py:110
  975.0 11.3 %collective-permute-done.14 = bf16[2,512,2,128]{1,3,2,0:T(8,128)(2,1)S(1)} collective-permute-done((bf16[2,512,2,128]{1,3,2,0:T(8,128)(2,1)S(1)}, bf16[2,512,2,128]{1,3,2,0:T(8,128)(2,1)S(1)}, u32[]{:S(2)}, u32[]{:S(2)}) %collective-permute-start.14) | collective-permute-done | bytes 524320 | tf_op jit(solution)/shard_map/ppermute | solution.py:18
  991.6 6.5 all-to-all-done.6
  1006.4 4.4 copy.566
  1010.7 4.8 all-to-all-start.5
  1015.5 3.9 copy.386
  1019.4 4.1 copy.418
  1025.6 17.1 %all-to-all-done.5 = bf16[4,128,2048]{2,1,0:T(8,128)(2,1)S(1)} async-done(((bf16[4,128,2048]{2,1,0:T(8,128)(2,1)}), bf16[4,128,2048]{2,1,0:T(8,128)(2,1)S(1)}, u32[]{:S(2)}, u32[]{:S(2)}) %all-to-all-start.5) | async-done | bytes 2097184 | tf_op jit(solution)/shard_map/all_to_all | solution.py:190
  1045.2 4.1 copy.419
  (394 shorter events, 386.1 us)
Async XLA Ops:
  2.3 11.8 %all-to-all-start = ((bf16[128,4,256]{2,0,1:T(8,128)(2,1)}), bf16[128,4,256]{2,0,1:T(8,128)(2,1)S(1)}, u32[]{:S(2)}, u32[]{:S(2)}) async-start(bf16[128,4,256]{2,0,1:T(8,128)(2,1)} %bitcast.728), calls=%async_computation | async-start | bytes 524288 | tf_op jit(solution)/shard_map/all_to_all | solution.py:117
  14.1 10.9 %all-to-all-start.1 = ((bf16[128,4,256]{2,0,1:T(8,128)(2,1)}), bf16[128,4,256]{2,0,1:T(8,128)(2,1)S(1)}, u32[]{:S(2)}, u32[]{:S(2)}) async-start(bf16[128,4,256]{2,0,1:T(8,128)(2,1)} %bitcast.727), calls=%async_computation.1 | async-start | bytes 524288 | tf_op jit(solution)/shard_map/all_to_all | solution.py:118
  25.0 40.1 %all-to-all-start.2 = ((bf16[128,4,2048]{2,0,1:T(8,128)(2,1)}), bf16[128,4,2048]{2,0,1:T(8,128)(2,1)S(1)}, u32[]{:S(2)}, u32[]{:S(2)}) async-start(bf16[128,4,2048]{2,0,1:T(8,128)(2,1)} %bitcast.988), calls=%async_computation.2 | async-start | bytes 4194304 | tf_op jit(solution)/shard_map/all_to_all | solution.py:116
  28.6 21.2 %copy-start.1 = (s32[1,8]{1,0:T(1,128)S(1)}, s32[1,8]{1,0:T(1,128)}, u32[]{:S(2)}) copy-start(s32[1,8]{1,0:T(1,128)} %param.43) | copy-start | bytes 100
  28.6 21.9 %copy-start.2 = (s32[1,8,8]{2,1,0:T(8,128)S(1)}, s32[1,8,8]{2,1,0:T(8,128)}, u32[]{:S(2)}) copy-start(s32[1,8,8]{2,1,0:T(8,128)} %param.42) | copy-start | bytes 772
  29.2 17.5 %collective-permute-start = (bf16[2,512,2,128]{3,2,1,0:T(2,128)(2,1)S(1)}, bf16[2,512,2,128]{3,2,1,0:T(2,128)(2,1)S(1)}, u32[]{:S(2)}, u32[]{:S(2)}) collective-permute-start(bf16[2,512,2,128]{3,2,1,0:T(2,128)(2,1)S(1)} %constant_dynamic-update-slice_fusion.8), channel_id=1, source_target_pairs={{63,0},{0,1},{1,2},{2,3},{3,4},{4,5},{5,6},{6,7},{7,8},{8,9},{9,10... | collective-permute-start | bytes 1572872 | tf_op jit(solution)/shard_map/ppermute | solution.py:18
  46.6 16.6 %collective-permute-start.1 = (bf16[2,512,2,128]{3,2,1,0:T(2,128)(2,1)S(1)}, bf16[2,512,2,128]{3,2,1,0:T(2,128)(2,1)}, u32[]{:S(2)}, u32[]{:S(2)}) collective-permute-start(bf16[2,512,2,128]{3,2,1,0:T(2,128)(2,1)S(1)} %collective-permute-done), channel_id=1, source_target_pairs={{63,0},{0,1},{1,2},{2,3},{3,4},{4,5},{5,6},{6,7},{7,8},{8,9},{9,10... | collective-permute-start | bytes 1572872 | tf_op jit(solution)/shard_map/ppermute | solution.py:18
  65.1 118.1 %collective-permute-start.2 = (bf16[2,512,2,128]{3,2,1,0:T(2,128)(2,1)}, bf16[2,512,2,128]{3,2,1,0:T(2,128)(2,1)}, u32[]{:S(2)}, u32[]{:S(2)}) collective-permute-start(bf16[2,512,2,128]{3,2,1,0:T(2,128)(2,1)} %collective-permute-done.1), channel_id=1, source_target_pairs={{63,0},{0,1},{1,2},{2,3},{3,4},{4,5},{5,6},{6,7},{7,8},{8,9},{9,10... | collective-permute-start | bytes 1572872 | tf_op jit(solution)/shard_map/ppermute | solution.py:18
  65.1 112.6 %all-to-all-start.4 = ((bf16[128,4,2048]{2,0,1:T(8,128)(2,1)}), bf16[128,4,2048]{2,0,1:T(8,128)(2,1)}, u32[]{:S(2)}, u32[]{:S(2)}) async-start(bf16[128,4,2048]{2,0,1:T(8,128)(2,1)} %bitcast.725), calls=%async_computation.4 | async-start | bytes 4194304 | tf_op jit(solution)/shard_map/all_to_all | solution.py:119
  180.0 1.3 copy-start
  185.2 40.5 %collective-permute-start.3 = (bf16[2,512,2,128]{3,2,1,0:T(2,128)(2,1)}, bf16[2,512,2,128]{3,2,1,0:T(2,128)(2,1)}, u32[]{:S(2)}, u32[]{:S(2)}) collective-permute-start(bf16[2,512,2,128]{3,2,1,0:T(2,128)(2,1)} %collective-permute-done.2), channel_id=1, source_target_pairs={{63,0},{0,1},{1,2},{2,3},{3,4},{4,5},{5,6},{6,7},{7,8},{8,9},{9,10... | collective-permute-start | bytes 1572872 | tf_op jit(solution)/shard_map/ppermute | solution.py:18
  227.6 24.6 %collective-permute-start.4 = (bf16[2,512,2,128]{3,2,1,0:T(2,128)(2,1)}, bf16[2,512,2,128]{3,2,1,0:T(2,128)(2,1)}, u32[]{:S(2)}, u32[]{:S(2)}) collective-permute-start(bf16[2,512,2,128]{3,2,1,0:T(2,128)(2,1)} %collective-permute-done.3), channel_id=1, source_target_pairs={{63,0},{0,1},{1,2},{2,3},{3,4},{4,5},{5,6},{6,7},{7,8},{8,9},{9,10... | collective-permute-start | bytes 1572872 | tf_op jit(solution)/shard_map/ppermute | solution.py:18
  254.1 32.6 %collective-permute-start.5 = (bf16[2,512,2,128]{3,2,1,0:T(2,128)(2,1)}, bf16[2,512,2,128]{3,2,1,0:T(2,128)(2,1)}, u32[]{:S(2)}, u32[]{:S(2)}) collective-permute-start(bf16[2,512,2,128]{3,2,1,0:T(2,128)(2,1)} %collective-permute-done.4), channel_id=1, source_target_pairs={{63,0},{0,1},{1,2},{2,3},{3,4},{4,5},{5,6},{6,7},{7,8},{8,9},{9,10... | collective-permute-start | bytes 1572872 | tf_op jit(solution)/shard_map/ppermute | solution.py:18
  288.6 17.0 %collective-permute-start.6 = (bf16[2,512,2,128]{3,2,1,0:T(2,128)(2,1)}, bf16[2,512,2,128]{3,2,1,0:T(2,128)(2,1)}, u32[]{:S(2)}, u32[]{:S(2)}) collective-permute-start(bf16[2,512,2,128]{3,2,1,0:T(2,128)(2,1)} %collective-permute-done.5), channel_id=1, source_target_pairs={{63,0},{0,1},{1,2},{2,3},{3,4},{4,5},{5,6},{6,7},{7,8},{8,9},{9,10... | collective-permute-start | bytes 1572872 | tf_op jit(solution)/shard_map/ppermute | solution.py:18
  434.9 35.7 %collective-permute-start.7 = (f32[2,512,2,128]{1,3,2,0:T(8,128)}, f32[2,512,2,128]{1,3,2,0:T(8,128)}, u32[]{:S(2)}, u32[]{:S(2)}) collective-permute-start(f32[2,512,2,128]{1,3,2,0:T(8,128)} %get-tuple-element.1957), channel_id=1, source_target_pairs={{63,0},{0,1},{1,2},{2,3},{3,4},{4,5},{5,6},{6,7},{7,8},{8,9},{9,10... | collective-permute-start | bytes 3145736 | tf_op jit(solution)/shard_map/ppermute | solution.py:18
  509.1 27.7 %collective-permute-start.8 = (f32[2,512,2,128]{1,3,2,0:T(8,128)}, f32[2,512,2,128]{1,3,2,0:T(8,128)}, u32[]{:S(2)}, u32[]{:S(2)}) collective-permute-start(f32[2,512,2,128]{1,3,2,0:T(8,128)} %get-tuple-element.1959), channel_id=1, source_target_pairs={{63,0},{0,1},{1,2},{2,3},{3,4},{4,5},{5,6},{6,7},{7,8},{8,9},{9,10... | collective-permute-start | bytes 3145736 | tf_op jit(solution)/shard_map/ppermute | solution.py:18
  587.5 81.0 %collective-permute-start.9 = (f32[2,512,2,128]{1,3,2,0:T(8,128)}, f32[2,512,2,128]{1,3,2,0:T(8,128)}, u32[]{:S(2)}, u32[]{:S(2)}) collective-permute-start(f32[2,512,2,128]{1,3,2,0:T(8,128)} %get-tuple-element.1961), channel_id=1, source_target_pairs={{63,0},{0,1},{1,2},{2,3},{3,4},{4,5},{5,6},{6,7},{7,8},{8,9},{9,10... | collective-permute-start | bytes 3145736 | tf_op jit(solution)/shard_map/ppermute | solution.py:18
  707.1 26.0 %collective-permute-start.10 = (f32[2,512,2,128]{1,3,2,0:T(8,128)}, f32[2,512,2,128]{1,3,2,0:T(8,128)}, u32[]{:S(2)}, u32[]{:S(2)}) collective-permute-start(f32[2,512,2,128]{1,3,2,0:T(8,128)} %get-tuple-element.1963), channel_id=1, source_target_pairs={{63,0},{0,1},{1,2},{2,3},{3,4},{4,5},{5,6},{6,7},{7,8},{8,9},{9,10... | collective-permute-start | bytes 3145736 | tf_op jit(solution)/shard_map/ppermute | solution.py:18
  746.3 57.6 %collective-permute-start.11 = (f32[2,512,2,128]{1,3,2,0:T(8,128)}, f32[2,512,2,128]{1,3,2,0:T(8,128)}, u32[]{:S(2)}, u32[]{:S(2)}) collective-permute-start(f32[2,512,2,128]{1,3,2,0:T(8,128)} %get-tuple-element.1965), channel_id=1, source_target_pairs={{63,0},{0,1},{1,2},{2,3},{3,4},{4,5},{5,6},{6,7},{7,8},{8,9},{9,10... | collective-permute-start | bytes 3145736 | tf_op jit(solution)/shard_map/ppermute | solution.py:18
  817.2 34.0 %collective-permute-start.12 = (f32[2,512,2,128]{1,3,2,0:T(8,128)}, f32[2,512,2,128]{1,3,2,0:T(8,128)}, u32[]{:S(2)}, u32[]{:S(2)}) collective-permute-start(f32[2,512,2,128]{1,3,2,0:T(8,128)} %get-tuple-element.1967), channel_id=1, source_target_pairs={{63,0},{0,1},{1,2},{2,3},{3,4},{4,5},{5,6},{6,7},{7,8},{8,9},{9,10... | collective-permute-start | bytes 3145736 | tf_op jit(solution)/shard_map/ppermute | solution.py:18
  864.4 58.5 %collective-permute-start.13 = (f32[2,512,2,128]{1,3,2,0:T(8,128)}, f32[2,512,2,128]{1,3,2,0:T(8,128)}, u32[]{:S(2)}, u32[]{:S(2)}) collective-permute-start(f32[2,512,2,128]{1,3,2,0:T(8,128)} %get-tuple-element.1969), channel_id=1, source_target_pairs={{63,0},{0,1},{1,2},{2,3},{3,4},{4,5},{5,6},{6,7},{7,8},{8,9},{9,10... | collective-permute-start | bytes 3145736 | tf_op jit(solution)/shard_map/ppermute | solution.py:18
  873.5 113.8 %all-to-all-start.3 = ((bf16[4,128,2048]{2,1,0:T(8,128)(2,1)}), bf16[4,128,2048]{2,1,0:T(8,128)(2,1)}, u32[]{:S(2)}, u32[]{:S(2)}) async-start(bf16[4,128,2048]{2,1,0:T(8,128)(2,1)} %copy.565), calls=%async_computation.3 | async-start | bytes 4194304 | tf_op jit(solution)/shard_map/all_to_all | solution.py:189
  974.9 11.4 %collective-permute-start.14 = (bf16[2,512,2,128]{1,3,2,0:T(8,128)(2,1)S(1)}, bf16[2,512,2,128]{1,3,2,0:T(8,128)(2,1)S(1)}, u32[]{:S(2)}, u32[]{:S(2)}) collective-permute-start(bf16[2,512,2,128]{1,3,2,0:T(8,128)(2,1)S(1)} %convert_element_type.170), channel_id=1, source_target_pairs={{7,0},{8,1},{9,2},{10,3},{11,4},{12,5},{13,6},{14,7},{15,8},{16,9}... | collective-permute-start | bytes 1572872 | tf_op jit(solution)/shard_map/ppermute | solution.py:18
  987.3 10.9 %all-to-all-start.6 = ((bf16[4,128,256]{2,1,0:T(8,128)(2,1)}), bf16[4,128,256]{2,1,0:T(8,128)(2,1)S(1)}, u32[]{:S(2)}, u32[]{:S(2)}) async-start(bf16[4,128,256]{2,1,0:T(8,128)(2,1)} %copy.567), calls=%async_computation.6 | async-start | bytes 524288 | tf_op jit(solution)/shard_map/all_to_all | solution.py:191
  998.1 12.6 %all-to-all-start.7 = ((bf16[4,128,256]{2,1,0:T(8,128)(2,1)}), bf16[4,128,256]{2,1,0:T(8,128)(2,1)S(1)}, u32[]{:S(2)}, u32[]{:S(2)}) async-start(bf16[4,128,256]{2,1,0:T(8,128)(2,1)} %copy.568), calls=%async_computation.7 | async-start | bytes 524288 | tf_op jit(solution)/shard_map/all_to_all | solution.py:192
  1010.7 31.9 %all-to-all-start.5 = ((bf16[4,128,2048]{2,1,0:T(8,128)(2,1)}), bf16[4,128,2048]{2,1,0:T(8,128)(2,1)S(1)}, u32[]{:S(2)}, u32[]{:S(2)}) async-start(bf16[4,128,2048]{2,1,0:T(8,128)(2,1)} %copy.566), calls=%async_computation.5 | async-start | bytes 4194304 | tf_op jit(solution)/shard_map/all_to_all | solution.py:190
where the time goes:
time: 1070 us; the launch traced here: 1050 us
  waiting for transfers between devices  432 us (40%)
  matrix products  248 us (23%)
  loops' own time  162 us (15%)
  local copies, waits for them, and re-layouts  103 us (10%)
  other arithmetic  58 us (5%)
  starting transfers between devices  45 us (4%)
    ppermute x15, waiting for transfers between devices, from_behind(): return lax.ppermute(block, axis, route)  398 us
    another operation x8, loops' own time, forward_pairs(): return lax.fori_loop(0, count, forward_visit, loop_state)  81 us
    another operation x8, loops' own time, backward_pairs(): return lax.fori_loop(0, count, backward_visit, loop_state)  80.9 us
    dot_general x23, matrix products, forward_visit(): jnp.einsum('hgqk,khd->qhgd', weights.astype(jnp.bfloat16), kv_blk[1], pre...  61.5 us
    dot_general x23, matrix products, backward_visit(): jnp.einsum('hgqk,khd->qhgd', dscore, kv_blk[0], preferred_element_type=jn...  61.3 us
    dot_general x46, matrix products, block_scores(): jnp.einsum('qhgd,khd->hgqk', q_blk, k_blk, preferred_element_type=jnp.flo...  53.7 us
    dynamic_update_slice x23, other arithmetic, backward_visit(): lax.dynamic_update_slice_in_dim(kv_grad, old_kv + jnp.stack((key_part, va...  39.5 us
    dot_general x23, matrix products, backward_visit(): jnp.einsum('qhgd,khd->hgqk', g_blk, kv_blk[1], preferred_element_type=jnp...  32.1 us
  transfers between devices with their start and end apart: 23, of which 18 were waited for; matrix products, arithmetic and copies ran while one was open for 17% of the time, Pallas kernels for 0%

commit v1 on v0

v1 whole, which is shorter than its diff:
```python
import functools

import jax
import jax.numpy as jnp
from jax import lax
from jax.experimental import pallas as pl
from jax.experimental.pallas import tpu as pltpu
from jax.sharding import PartitionSpec as P

QUERY_HEADS = 64
KEY_VALUE_HEADS = 8
HEAD_SIZE = 128
BLOCK = 128
NSTEP = 8
NB = 4
QUAD = 4
GROUP = QUERY_HEADS // KEY_VALUE_HEADS
WIDE = GROUP * BLOCK
MOST = NSTEP * NB
NEGATIVE_FILL = -1e30
SCALE = HEAD_SIZE ** (-0.5)
SCALE_LOG2 = SCALE * 1.4426950408889634
TILE = 256
F32 = jnp.float32
BF16 = jnp.bfloat16

OWN, PREV = 0, 1
NEAR = {1: 2, 2: 4, 3: 3}
FAR = {1: 5, 2: 7, 3: 6}


def dot(a, b):
    return lax.dot_general(a, b, (((1,), (0,)), ((), ())), preferred_element_type=F32)


def attend(codes, counts, place, qd_ref, *refs):
    kv_refs = refs[:NSTEP]
    out_ref, own_ref = refs[NSTEP], refs[NSTEP + 1]
    part_refs = refs[NSTEP + 2 : 2 * NSTEP + 1]
    (
        pairs, filled, kvs, dkv, masks, q_t, q_s, g_t, g_s, scores, weights, top, total, row, turned, dsc,
    ) = refs[2 * NSTEP + 1 :]
    t = pl.program_id(0)

    @pl.when(t == 0)
    def _():
        y = place[0]
        for b in range(NB):
            pairs[b, 0] = b
            filled[b] = 1
        for s in range(NSTEP):
            d = s % QUAD
            if d == 0:
                slot = OWN if s == 0 else PREV
            elif s < QUAD:
                slot = jnp.where(y >= d, FAR[d], NEAR[d])
            else:
                slot = jnp.where(y >= d, NEAR[d], FAR[d])

            def add(i, carry, s=s, slot=slot):
                code = codes[s, i]
                b = lax.shift_right_logical(code, 2)
                c = jnp.bitwise_and(code, 3)

                def put():
                    n = filled[b]
                    pairs[b, n] = slot * NB + c
                    filled[b] = n + 1

                if s == 0:
                    pl.when(b != c)(put)
                else:
                    put()
                return carry

            lax.fori_loop(0, counts[s], add, 0)
        for b in range(NB):
            pairs[b, filled[b]] = b
        for s in range(NSTEP):
            for c in range(NB):
                kvs[s * NB + c] = kv_refs[s][pl.ds(c * BLOCK, BLOCK), :]
        dkv[...] = jnp.zeros_like(dkv)
        keys_at = lax.broadcasted_iota(jnp.int32, (BLOCK, BLOCK), 0)
        rows_at = lax.broadcasted_iota(jnp.int32, (BLOCK, BLOCK), 1)
        masks[0] = jnp.zeros((BLOCK, BLOCK), F32)
        masks[1] = jnp.where(keys_at <= rows_at, 0.0, NEGATIVE_FILL)
        masks[2] = jnp.full((BLOCK, BLOCK), NEGATIVE_FILL, F32)

    for h in range(GROUP):
        at = pl.ds(h * BLOCK, BLOCK)
        q = qd_ref[0, :, at]
        q_s[at, :] = q
        q_t[:, at] = q.T
        g_t[:, at] = qd_ref[1, :, at].T

    n = filled[t]
    trips = lax.shift_right_logical(n + 1, 1)
    top[...] = jnp.full_like(top, NEGATIVE_FILL)
    total[...] = jnp.zeros_like(total)
    turned[...] = jnp.zeros_like(turned)

    def two(i, lo):
        a, b = pairs[t, 2 * i], pairs[t, 2 * i + 1]
        return jnp.concatenate([kvs[a, :, pl.ds(lo, HEAD_SIZE)], kvs[b, :, pl.ds(lo, HEAD_SIZE)]], axis=0)

    def score_visit(i, carry):
        k = two(i, 0)
        first = masks[jnp.where(i == 0, 1, 0)]
        second = masks[jnp.where(2 * i + 1 >= n, 2, 0)]
        mask = jnp.concatenate([first, second], axis=0)
        mask = jnp.concatenate([mask, mask], axis=1)
        for w in range(WIDE // TILE):
            at = pl.ds(w * TILE, TILE)
            s = dot(k, q_t[:, at]) * SCALE_LOG2 + mask
            scores[pl.ds(2 * i, 2), :, at] = s.reshape(2, BLOCK, TILE)
            top[:, at] = jnp.maximum(top[:, at], jnp.max(s.reshape(2 * BLOCK // 8, 8, TILE), axis=0))
        return carry

    lax.fori_loop(0, trips, score_visit, 0)
    top[...] = jnp.broadcast_to(jnp.max(top[...], axis=0, keepdims=True), top.shape)

    def weight_visit(i, carry):
        v_t = two(i, HEAD_SIZE).T
        for w in range(WIDE // TILE):
            at = pl.ds(w * TILE, TILE)
            s = scores[pl.ds(2 * i, 2), :, at].reshape(2 * BLOCK // 8, 8, TILE)
            p = jnp.exp2(s - top[:, at][None])
            total[:, at] += jnp.sum(p, axis=0)
            low = p.reshape(2 * BLOCK, TILE).astype(BF16)
            weights[pl.ds(2 * i, 2), :, at] = low.reshape(2, BLOCK, TILE)
            turned[:, at] += dot(v_t, low)
        return carry

    lax.fori_loop(0, trips, weight_visit, 0)

    for h in range(GROUP):
        at = pl.ds(h * BLOCK, BLOCK)
        inverse = 1.0 / jnp.sum(total[:, at], axis=0, keepdims=True)
        attn = (turned[:, at] * inverse).astype(BF16)
        out_ref[0, :, at] = attn.T
        grad = (g_t[:, at].astype(F32) * inverse).astype(BF16)
        g_t[:, at] = grad
        g_s[at, :] = grad.T
        row[:, at] = jnp.broadcast_to(
            jnp.sum(grad.astype(F32) * attn.astype(F32), axis=0, keepdims=True), (8, BLOCK)
        )
    turned[...] = jnp.zeros_like(turned)

    def back_visit(i, carry):
        k = two(i, 0)
        v = two(i, HEAD_SIZE)
        k_t = k.T
        for w in range(WIDE // TILE):
            at = pl.ds(w * TILE, TILE)
            p = weights[pl.ds(2 * i, 2), :, at].reshape(2 * BLOCK, TILE).astype(F32)
            dp = dot(v, g_t[:, at])
            ds = p.reshape(2 * BLOCK // 8, 8, TILE) * (dp.reshape(2 * BLOCK // 8, 8, TILE) - row[:, at][None])
            ds = ds.reshape(2 * BLOCK, TILE).astype(BF16)
            dsc[:, at] = ds
            turned[:, at] += dot(k_t, ds)
        dk = dot(dsc[...], q_s[...])
        dv = dot(weights[pl.ds(2 * i, 2)].reshape(2 * BLOCK, WIDE), g_s[...])
        for half in range(2):
            a = pairs[t, 2 * i + half]
            rows = slice(half * BLOCK, (half + 1) * BLOCK)
            dkv[a, :, pl.ds(0, HEAD_SIZE)] += dk[rows]
            dkv[a, :, pl.ds(HEAD_SIZE, HEAD_SIZE)] += dv[rows]
        return carry

    lax.fori_loop(0, trips, back_visit, 0)

    for h in range(GROUP):
        at = pl.ds(h * BLOCK, BLOCK)
        out_ref[1, :, at] = (turned[:, at] * SCALE).astype(BF16).T

    @pl.when(t == NB - 1)
    def _():
        left, right = pl.ds(0, HEAD_SIZE), pl.ds(HEAD_SIZE, HEAD_SIZE)
        for c in range(NB):
            rows = pl.ds(c * BLOCK, BLOCK)
            own_ref[rows, left] = dkv[c, :, left] * SCALE
            own_ref[rows, right] = dkv[c, :, right]
            for s in range(1, NSTEP):
                part_refs[s - 1][rows, left] = (dkv[s * NB + c, :, left] * SCALE).astype(BF16)
                part_refs[s - 1][rows, right] = dkv[s * NB + c, :, right].astype(BF16)


def attend_call(codes, counts, place, qd, kv):
    rows = NB * BLOCK
    whole = pl.BlockSpec((rows, 2 * HEAD_SIZE), lambda t, *_: (0, 0))
    block = pl.BlockSpec((None, 2, BLOCK, WIDE), lambda t, *_: (t, 0, 0, 0))
    small = (rows, 2 * HEAD_SIZE)
    return pl.pallas_call(
        attend,
        grid_spec=pltpu.PrefetchScalarGridSpec(
            num_scalar_prefetch=3,
            grid=(NB,),
            in_specs=[block] + [whole] * NSTEP,
            out_specs=[block] + [whole] * NSTEP,
            scratch_shapes=[
                pltpu.SMEM((NB, MOST + 8), jnp.int32),
                pltpu.SMEM((NB,), jnp.int32),
                pltpu.VMEM((MOST, BLOCK, 2 * HEAD_SIZE), BF16),
                pltpu.VMEM((MOST, BLOCK, 2 * HEAD_SIZE), F32),
                pltpu.VMEM((3, BLOCK, BLOCK), F32),
                pltpu.VMEM((HEAD_SIZE, WIDE), BF16),
                pltpu.VMEM((WIDE, HEAD_SIZE), BF16),
                pltpu.VMEM((HEAD_SIZE, WIDE), BF16),
                pltpu.VMEM((WIDE, HEAD_SIZE), BF16),
                pltpu.VMEM((MOST, BLOCK, WIDE), F32),
                pltpu.VMEM((MOST, BLOCK, WIDE), BF16),
                pltpu.VMEM((8, WIDE), F32),
                pltpu.VMEM((8, WIDE), F32),
                pltpu.VMEM((8, WIDE), F32),
                pltpu.VMEM((HEAD_SIZE, WIDE), F32),
                pltpu.VMEM((2 * BLOCK, WIDE), BF16),
            ],
        ),
        out_shape=[jax.ShapeDtypeStruct(qd.shape, BF16), jax.ShapeDtypeStruct(small, F32)]
        + [jax.ShapeDtypeStruct(small, BF16)] * (NSTEP - 1),
        compiler_params=pltpu.CompilerParams(
            dimension_semantics=("arbitrary",), vmem_limit_bytes=58 * 1024 * 1024
        ),
    )(codes, counts, place, qd, *kv)


def shifted(x, distance):
    n = lax.axis_size("blk")
    return lax.ppermute(x, "blk", [((i - distance) % n, i) for i in range(n)])


def hop(x, moves):
    quads = lax.axis_size("blk") // QUAD
    return lax.ppermute(x, "blk", [(q * QUAD + a, q * QUAD + b) for q in range(quads) for a, b in moves])


UP = [(y, (y + 1) % QUAD) for y in range(QUAD)]
DOWN = [(y, (y - 1) % QUAD) for y in range(QUAD)]


def flipped(moves):
    return [(b, a) for a, b in moves]


NEAR_UP, NEAR_DOWN = [(3, 0), (0, 1)], [(3, 2), (0, 3)]
FAR_UP, FAR_DOWN = [(1, 2), (2, 3)], [(1, 0), (2, 1)]


def spread(own, y):
    prev = shifted(own, QUAD)
    back = shifted(own, 2 * QUAD)
    near_1 = hop(prev, UP)
    near_3 = hop(prev, DOWN)
    far_1 = hop(jnp.where(y == QUAD - 1, back, own), UP)
    far_3 = hop(jnp.where(y == 0, own, back), DOWN)
    near_2 = jnp.where(y < 2, hop(near_1, NEAR_UP), hop(near_3, NEAR_DOWN))
    far_2 = jnp.where(y >= 2, hop(far_1, FAR_UP), hop(far_3, FAR_DOWN))
    return (own, prev, near_1, near_3, near_2, far_1, far_3, far_2)


def plus(a, b):
    return (a.astype(F32) + b.astype(F32)).astype(BF16)


def gathered(own, parts, y):
    prev, near_1, near_3, near_2, far_1, far_3, far_2 = parts
    near_1 = plus(near_1, hop(near_2, flipped(NEAR_UP)))
    near_3 = plus(near_3, hop(near_2, flipped(NEAR_DOWN)))
    far_1 = plus(far_1, hop(far_2, flipped(FAR_UP)))
    far_3 = plus(far_3, hop(far_2, flipped(FAR_DOWN)))
    near_1 = hop(near_1, flipped(UP)).astype(F32)
    near_3 = hop(near_3, flipped(DOWN)).astype(F32)
    far_1 = hop(far_1, flipped(UP)).astype(F32)
    far_3 = hop(far_3, flipped(DOWN)).astype(F32)
    prev = (prev.astype(F32) + near_1 + near_3).astype(BF16)
    back = (jnp.where(y == QUAD - 1, far_1, 0.0) + jnp.where(y == 0, 0.0, far_3)).astype(BF16)
    own = own + jnp.where(y == QUAD - 1, 0.0, far_1) + jnp.where(y == 0, far_3, 0.0)
    return own + shifted(prev, -QUAD).astype(F32) + shifted(back, -2 * QUAD).astype(F32)


def swap(x):
    return lax.all_to_all(x, "head", split_axis=0, concat_axis=0, tiled=True)


def body(query, key, value, output_gradient, pair_codes, pair_counts):
    ranks = lax.axis_size("head")
    tokens = query.shape[0]
    held = KEY_VALUE_HEADS // ranks
    y = lax.axis_index("blk") % QUAD
    place = jnp.full((1,), y, jnp.int32)
    codes, counts = pair_codes[0], pair_counts[0]
    q_all = query.reshape(tokens, ranks, held, WIDE)
    g_all = output_gradient.reshape(tokens, ranks, held, WIDE)
    k_all = key.reshape(tokens, ranks, held, HEAD_SIZE)
    v_all = value.reshape(tokens, ranks, held, HEAD_SIZE)
    windows, rows = [], []
    for j in range(held):
        kv = jnp.concatenate([k_all[:, :, j], v_all[:, :, j]], axis=-1)
        kv = swap(jnp.transpose(kv, (1, 0, 2))).reshape(ranks * tokens, 2 * HEAD_SIZE)
        windows.append(spread(kv, y))
    for j in range(held):
        qd = jnp.stack([q_all[:, :, j], g_all[:, :, j]])
        rows.append(swap(jnp.transpose(qd, (2, 0, 1, 3))))
    outs, sums = [], []
    for j in range(held):
        both, own, *parts = attend_call(codes, counts, place, rows[j], windows[j])
        outs.append(swap(both))
        kv_sum = gathered(own, parts, y).astype(BF16)
        sums.append(swap(kv_sum.reshape(ranks, tokens, 2 * HEAD_SIZE)))
    wide = jnp.stack(outs, axis=3)
    attn_out = jnp.transpose(wide[:, 0], (1, 0, 2, 3)).reshape(query.shape)
    grad_query = jnp.transpose(wide[:, 1], (1, 0, 2, 3)).reshape(query.shape)
    small = jnp.transpose(jnp.stack(sums, axis=2), (1, 0, 2, 3))
    key_gradient = small[..., :HEAD_SIZE].reshape(key.shape)
    value_gradient = small[..., HEAD_SIZE:].reshape(value.shape)
    return attn_out, grad_query, key_gradient, value_gradient


def solution(mesh):
    rows = P(("blk", "head"), None)
    return jax.shard_map(
        body,
        mesh=mesh,
        in_specs=(rows, rows, rows, rows, P("blk", None, None), P("blk", None)),
        out_specs=(rows, rows, rows, rows),
        check_vma=False,
    )
```

time: 1070 us -> 353 us (0.33)
  the two profiles are of different devices: /device:TPU:192 before, /device:TPU:1 now
where the time goes in v1:
time: 353 us; the launch traced here: 347 us
  starting transfers between devices  129 us (37%)
  waiting for transfers between devices  67.1 us (19%)
  Pallas kernels  57.5 us (16%)
  blocking collectives  40.6 us (12%)
  local copies, waits for them, and re-layouts  35.7 us (10%)
  other arithmetic  16.5 us (5%)
    ppermute x32, starting transfers between devices, hop(): lax.ppermute(x, 'blk', [(q * QUAD + a, q * QUAD + b) for q in range(quads...  59.1 us
    pallas_call x2, Pallas kernels, attend_call(): pl.pallas_call(attend, grid_spec=pltpu.PrefetchScalarGridSpec(num_scalar_...  57.5 us
    all_to_all x6, waiting for transfers between devices, swap(): return lax.all_to_all(x, 'head', split_axis=0, concat_axis=0, tiled=True)  45.4 us
    all_to_all x6, starting transfers between devices, swap(): return lax.all_to_all(x, 'head', split_axis=0, concat_axis=0, tiled=True)  43 us
    all_to_all x2, blocking collectives, swap(): return lax.all_to_all(x, 'head', split_axis=0, concat_axis=0, tiled=True)  40.6 us
    ppermute x8, starting transfers between devices, shifted(): return lax.ppermute(x, 'blk', [((i - distance) % n, i) for i in range(n)])  26.6 us
    unnamed x58, local copies, waits for them, and re-layouts  20.2 us
    ppermute x32, waiting for transfers between devices, hop(): lax.ppermute(x, 'blk', [(q * QUAD + a, q * QUAD + b) for q in range(quads...  19.5 us
  transfers between devices with their start and end apart: 46, of which 10 were waited for; matrix products, arithmetic and copies ran while one was open for 9% of the time, Pallas kernels for 17%

profile of v1, /device:TPU:1, one launch (start us, length us, event | category | flops | bytes accessed | tf_op | source)
XLA Modules:
  0.0 347.3 jit_solution(793396721624295587)
XLA Ops:
  5.1 7.2 %all-to-all-start.1 = ((bf16[4,128,256]{2,1,0:T(8,128)(2,1)}), bf16[4,128,256]{2,1,0:T(8,128)(2,1)}, u32[]{:S(2)}, u32[]{:S(2)}) async-start(bf16[4,128,256]{2,1,0:T(8,128)(2,1)} %maximum_bitcast_fusion.3), calls=%async_computation.1 | async-start | bytes 524288 | tf_op jit(solution)/shard_map/all_to_all | solution.py:282
  12.3 3.2 copy.18
  17.4 3.3 copy.20
  21.4 4.8 %all-to-all-start.4 = ((bf16[4,128,256]{2,1,0:T(8,128)(2,1)}), bf16[4,128,256]{2,1,0:T(8,128)(2,1)S(1)}, u32[]{:S(2)}, u32[]{:S(2)}) async-start(bf16[4,128,256]{2,1,0:T(8,128)(2,1)} %maximum_bitcast_fusion.4), calls=%async_computation.4 | async-start | bytes 524288 | tf_op jit(solution)/shard_map/all_to_all | solution.py:282
  26.2 1.5 fusion.18
  27.7 1.6 copy.34
  30.6 2.7 maximum_bitcast_fusion
  33.3 4.8 %all-to-all-start = ((bf16[4,2,128,1024]{3,2,1,0:T(8,128)(2,1)}), bf16[4,2,128,1024]{3,2,1,0:T(8,128)(2,1)S(1)}, u32[]{:S(2)}, u32[]{:S(2)}) async-start(bf16[4,2,128,1024]{3,2,1,0:T(8,128)(2,1)} %maximum_bitcast_fusion), calls=%async_computation | async-start | bytes 4194304 | tf_op jit(solution)/shard_map/all_to_all | solution.py:282
  39.6 2.4 copy.39
  42.0 2.7 maximum_bitcast_fusion.1
  45.7 1.6 collective-permute-start.15
  47.3 1.9 collective-permute-start.10
  49.2 15.2 %all-to-all-done.qd_ref = bf16[4,2,128,1024]{3,2,1,0:T(8,128)(2,1)S(1)} async-done(((bf16[4,2,128,1024]{3,2,1,0:T(8,128)(2,1)}), bf16[4,2,128,1024]{3,2,1,0:T(8,128)(2,1)S(1)}, u32[]{:S(2)}, u32[]{:S(2)}) %all-to-all-start) | async-done | bytes 2097184 | tf_op jit(solution)/shard_map/all_to_all | solution.py:282
  65.7 5.8 %all-to-all-start.3 = ((bf16[4,2,128,1024]{3,2,1,0:T(8,128)(2,1)}), bf16[4,2,128,1024]{3,2,1,0:T(8,128)(2,1)}, u32[]{:S(2)}, u32[]{:S(2)}) async-start(bf16[4,2,128,1024]{3,2,1,0:T(8,128)(2,1)} %maximum_bitcast_fusion.1), calls=%async_computation.3 | async-start | bytes 4194304 | tf_op jit(solution)/shard_map/all_to_all | solution.py:282
  72.7 2.7 collective-permute-start.7
  75.4 2.7 collective-permute-start.2
  78.3 3.6 %collective-permute-done.6.refs_5_ = bf16[512,256]{1,0:T(8,128)(2,1)S(1)} collective-permute-done((bf16[512,256]{1,0:T(8,128)(2,1)S(1)}, bf16[512,256]{1,0:T(8,128)(2,1)S(1)}, u32[]{:S(2)}, u32[]{:S(2)}) %collective-permute-start.6) | collective-permute-done | bytes 262176 | tf_op jit(solution)/shard_map/ppermute | solution.py:234
  82.0 1.4 collective-permute-start.11
  83.3 4.0 %collective-permute-done.1.refs_2_ = bf16[512,256]{1,0:T(8,128)(2,1)S(1)} collective-permute-done((bf16[512,256]{1,0:T(8,128)(2,1)}, bf16[512,256]{1,0:T(8,128)(2,1)S(1)}, u32[]{:S(2)}, u32[]{:S(2)}) %collective-permute-start.1) | collective-permute-done | bytes 262176 | tf_op jit(solution)/shard_map/ppermute | solution.py:234
  89.3 3.7 %collective-permute-done.16.refs_5_ = bf16[512,256]{1,0:T(8,128)(2,1)S(1)} collective-permute-done((bf16[512,256]{1,0:T(8,128)(2,1)S(1)}, bf16[512,256]{1,0:T(8,128)(2,1)S(1)}, u32[]{:S(2)}, u32[]{:S(2)}) %collective-permute-start.16) | collective-permute-done | bytes 262176 | tf_op jit(solution)/shard_map/ppermute | solution.py:234
  93.2 3.3 collective-permute-start.3
  96.5 2.2 collective-permute-done.11.refs_2_
  98.7 2.0 collective-permute-start.4
  103.5 7.2 %collective-permute-start.13 = (bf16[512,256]{1,0:T(8,128)(2,1)S(1)}, bf16[512,256]{1,0:T(8,128)(2,1)S(1)}, u32[]{:S(2)}, u32[]{:S(2)}) collective-permute-start(bf16[512,256]{1,0:T(8,128)(2,1)S(1)} %collective-permute-done.11.refs_2_), channel_id=1, source_target_pairs={{3,0},{0,1},{7,4},{4,5},{11,8},{8,9},{15,12},{12,13},{19,16},{16,1... | collective-permute-start | bytes 786440 | tf_op jit(solution)/shard_map/ppermute | solution.py:234
  112.8 28.8 %shard_map.93 = (bf16[4,2,128,1024]{3,2,1,0:T(8,128)(2,1)}, f32[512,256]{1,0:T(8,128)}, bf16[512,256]{1,0:T(8,128)(2,1)}, bf16[512,256]{1,0:T(8,128)(2,1)}, bf16...) custom-call(s32[8,8]{1,0:T(8,128)} %bitcast.64, ...), custom_call_target="tpu_custom_call" | custom-call | tf_op jit(solution)/shard_map/pallas_call | solution.py:193
  141.5 7.2 %collective-permute-start.24 = (bf16[512,256]{1,0:T(8,128)(2,1)}, bf16[512,256]{1,0:T(8,128)(2,1)S(1)}, u32[]{:S(2)}, u32[]{:S(2)}) collective-permute-start(bf16[512,256]{1,0:T(8,128)(2,1)} %get-tuple-element.30), channel_id=1, source_target_pairs={{0,3},{1,0},{4,7},{5,4},{8,11},{9,8},{12,15},{13,12},{16,19},{17,1... | collective-permute-start | bytes 786440 | tf_op jit(solution)/shard_map/ppermute | solution.py:234
  151.5 1.4 collective-permute-start.22
  153.7 28.7 %shard_map.94 = (bf16[4,2,128,1024]{3,2,1,0:T(8,128)(2,1)}, f32[512,256]{1,0:T(8,128)}, bf16[512,256]{1,0:T(8,128)(2,1)}, bf16[512,256]{1,0:T(8,128)(2,1)}, bf16...) custom-call(s32[8,8]{1,0:T(8,128)} %bitcast.65, ...), custom_call_target="tpu_custom_call" | custom-call | tf_op jit(solution)/shard_map/pallas_call | solution.py:193
  182.4 9.2 %collective-permute-start.34 = (bf16[512,256]{1,0:T(8,128)(2,1)}, bf16[512,256]{1,0:T(8,128)(2,1)S(1)}, u32[]{:S(2)}, u32[]{:S(2)}) collective-permute-start(bf16[512,256]{1,0:T(8,128)(2,1)} %get-tuple-element.38), channel_id=1, source_target_pairs={{0,3},{1,0},{4,7},{5,4},{8,11},{9,8},{12,15},{13,12},{16,19},{17,1... | collective-permute-start | bytes 786440 | tf_op jit(solution)/shard_map/ppermute | solution.py:234
  193.9 1.4 collective-permute-start.32
  195.4 3.4 collective-permute-start.25
  200.2 3.0 collective-permute-start.21
  203.9 2.6 collective-permute-start.37
  206.8 4.8 %collective-permute-done.23 = bf16[512,256]{1,0:T(8,128)(2,1)S(1)} collective-permute-done((bf16[512,256]{1,0:T(8,128)(2,1)S(1)}, bf16[512,256]{1,0:T(8,128)(2,1)S(1)}, u32[]{:S(2)}, u32[]{:S(2)}) %collective-permute-start.23) | collective-permute-done | bytes 262176 | tf_op jit(solution)/shard_map/ppermute | solution.py:234
  212.9 16.9 %collective-permute-start.28 = (bf16[512,256]{1,0:T(8,128)(2,1)S(1)}, bf16[512,256]{1,0:T(8,128)(2,1)S(1)}, u32[]{:S(2)}, u32[]{:S(2)}) collective-permute-start(bf16[512,256]{1,0:T(8,128)(2,1)S(1)} %add_convert_fusion.5), channel_id=1, source_target_pairs={{4,0},{5,1},{6,2},{7,3},{8,4},{9,5},{10,6},{11,7},{12,8},{13,9},{1... | collective-permute-start | bytes 786440 | tf_op jit(solution)/shard_map/ppermute | solution.py:229
  231.2 3.2 collective-permute-start.38
  235.2 2.1 collective-permute-done.29
  238.2 14.9 %all-to-all-start.6 = ((bf16[4,128,256]{2,1,0:T(8,128)(2,1)}), bf16[4,128,256]{2,1,0:T(8,128)(2,1)S(1)}, u32[]{:S(2)}, u32[]{:S(2)}) async-start(bf16[4,128,256]{2,1,0:T(8,128)(2,1)} %bitcast.27), calls=%async_computation.6 | async-start | bytes 524288 | tf_op jit(solution)/shard_map/all_to_all | solution.py:282
  253.4 6.3 %all-to-all-done.6 = bf16[4,128,256]{2,1,0:T(8,128)(2,1)S(1)} async-done(((bf16[4,128,256]{2,1,0:T(8,128)(2,1)}), bf16[4,128,256]{2,1,0:T(8,128)(2,1)S(1)}, u32[]{:S(2)}, u32[]{:S(2)}) %all-to-all-start.6) | async-done | bytes 262176 | tf_op jit(solution)/shard_map/all_to_all | solution.py:282
  259.7 9.8 %all_to_all.40 = bf16[4,128,256]{2,1,0:T(8,128)(2,1)S(1)} all-to-all(bf16[4,128,256]{2,1,0:T(8,128)(2,1)S(1)} %bitcast.61), channel_id=1, replica_groups=mesh['head'=4,'blk'=64] {'head'}, dimensions={0} | all-to-all | bytes 524288 | tf_op jit(solution)/shard_map/all_to_all | solution.py:282
  269.5 30.7 %all_to_all.41 = bf16[4,2,128,1024]{3,2,1,0:T(8,128)(2,1)S(1)} all-to-all(bf16[4,2,128,1024]{3,2,1,0:T(8,128)(2,1)} %get-tuple-element.22), channel_id=1, replica_groups=mesh['head'=4,'blk'=64] {'head'}, dimensions={0} | all-to-all | bytes 4194304 | tf_op jit(solution)/shard_map/all_to_all | solution.py:282
  300.3 5.4 %all-to-all-start.5 = ((bf16[4,2,128,1024]{3,2,1,0:T(8,128)(2,1)}), bf16[4,2,128,1024]{3,2,1,0:T(8,128)(2,1)}, u32[]{:S(2)}, u32[]{:S(2)}) async-start(bf16[4,2,128,1024]{3,2,1,0:T(8,128)(2,1)} %get-tuple-element.23), calls=%async_computation.5 | async-start | bytes 4194304 | tf_op jit(solution)/shard_map/all_to_all | solution.py:282
  308.2 23.9 %all-to-all-done.5 = bf16[4,2,128,1024]{3,2,1,0:T(8,128)(2,1)} async-done(((bf16[4,2,128,1024]{3,2,1,0:T(8,128)(2,1)}), bf16[4,2,128,1024]{3,2,1,0:T(8,128)(2,1)}, u32[]{:S(2)}, u32[]{:S(2)}) %all-to-all-start.5) | async-done | bytes 2097184 | tf_op jit(solution)/shard_map/all_to_all | solution.py:282
  332.0 3.4 fusion.2
  335.4 3.0 copy.28
  338.4 2.9 copy.32
  341.3 3.0 copy.29
  344.4 2.9 copy.33
  (147 shorter events, 35.5 us)
Async XLA Ops:
  5.1 16.3 %all-to-all-start.1 = ((bf16[4,128,256]{2,1,0:T(8,128)(2,1)}), bf16[4,128,256]{2,1,0:T(8,128)(2,1)}, u32[]{:S(2)}, u32[]{:S(2)}) async-start(bf16[4,128,256]{2,1,0:T(8,128)(2,1)} %maximum_bitcast_fusion.3), calls=%async_computation.1 | async-start | bytes 524288 | tf_op jit(solution)/shard_map/all_to_all | solution.py:282
  21.4 11.9 %all-to-all-start.4 = ((bf16[4,128,256]{2,1,0:T(8,128)(2,1)}), bf16[4,128,256]{2,1,0:T(8,128)(2,1)S(1)}, u32[]{:S(2)}, u32[]{:S(2)}) async-start(bf16[4,128,256]{2,1,0:T(8,128)(2,1)} %maximum_bitcast_fusion.4), calls=%async_computation.4 | async-start | bytes 524288 | tf_op jit(solution)/shard_map/all_to_all | solution.py:282
  33.3 31.1 %all-to-all-start = ((bf16[4,2,128,1024]{3,2,1,0:T(8,128)(2,1)}), bf16[4,2,128,1024]{3,2,1,0:T(8,128)(2,1)S(1)}, u32[]{:S(2)}, u32[]{:S(2)}) async-start(bf16[4,2,128,1024]{3,2,1,0:T(8,128)(2,1)} %maximum_bitcast_fusion), calls=%async_computation | async-start | bytes 4194304 | tf_op jit(solution)/shard_map/all_to_all | solution.py:282
  38.1 33.5 %collective-permute-start.5 = (bf16[512,256]{1,0:T(8,128)(2,1)}, bf16[512,256]{1,0:T(8,128)(2,1)}, u32[]{:S(2)}, u32[]{:S(2)}) collective-permute-start(bf16[512,256]{1,0:T(8,128)(2,1)} %bitcast.11.refs_0_), channel_id=1, source_target_pairs={{56,0},{57,1},{58,2},{59,3},{60,4},{61,5},{62,6},{63,7},{0,8},{1,9... | collective-permute-start | bytes 786440 | tf_op jit(solution)/shard_map/ppermute | solution.py:229
  44.7 30.7 %collective-permute-start = (bf16[512,256]{1,0:T(8,128)(2,1)}, bf16[512,256]{1,0:T(8,128)(2,1)}, u32[]{:S(2)}, u32[]{:S(2)}) collective-permute-start(bf16[512,256]{1,0:T(8,128)(2,1)} %bitcast.11.refs_0_), channel_id=1, source_target_pairs={{60,0},{61,1},{62,2},{63,3},{0,4},{1,5},{2,6},{3,7},{4,8},{5,9},{6... | collective-permute-start | bytes 786440 | tf_op jit(solution)/shard_map/ppermute | solution.py:229
  45.7 29.8 %collective-permute-start.15 = (bf16[512,256]{1,0:T(8,128)(2,1)S(1)}, bf16[512,256]{1,0:T(8,128)(2,1)S(1)}, u32[]{:S(2)}, u32[]{:S(2)}) collective-permute-start(bf16[512,256]{1,0:T(8,128)(2,1)S(1)} %bitcast.58), channel_id=1, source_target_pairs={{56,0},{57,1},{58,2},{59,3},{60,4},{61,5},{62,6},{63,7},{0,8},{1,9... | collective-permute-start | bytes 786440 | tf_op jit(solution)/shard_map/ppermute | solution.py:229
  47.3 30.9 %collective-permute-start.10 = (bf16[512,256]{1,0:T(8,128)(2,1)S(1)}, bf16[512,256]{1,0:T(8,128)(2,1)}, u32[]{:S(2)}, u32[]{:S(2)}) collective-permute-start(bf16[512,256]{1,0:T(8,128)(2,1)S(1)} %bitcast.59), channel_id=1, source_target_pairs={{60,0},{61,1},{62,2},{63,3},{0,4},{1,5},{2,6},{3,7},{4,8},{5,9},{6... | collective-permute-start | bytes 786440 | tf_op jit(solution)/shard_map/ppermute | solution.py:229
  65.7 87.9 %all-to-all-start.3 = ((bf16[4,2,128,1024]{3,2,1,0:T(8,128)(2,1)}), bf16[4,2,128,1024]{3,2,1,0:T(8,128)(2,1)}, u32[]{:S(2)}, u32[]{:S(2)}) async-start(bf16[4,2,128,1024]{3,2,1,0:T(8,128)(2,1)} %maximum_bitcast_fusion.1), calls=%async_computation.3 | async-start | bytes 4194304 | tf_op jit(solution)/shard_map/all_to_all | solution.py:282
  72.7 9.2 %collective-permute-start.6 = (bf16[512,256]{1,0:T(8,128)(2,1)S(1)}, bf16[512,256]{1,0:T(8,128)(2,1)S(1)}, u32[]{:S(2)}, u32[]{:S(2)}) collective-permute-start(bf16[512,256]{1,0:T(8,128)(2,1)S(1)} %get-tuple-element.55), channel_id=1, source_target_pairs={{0,1},{1,2},{2,3},{3,0},{4,5},{5,6},{6,7},{7,4},{8,9},{9,10},{10,1... | collective-permute-start | bytes 786440 | tf_op jit(solution)/shard_map/ppermute | solution.py:234
  72.7 9.2 %collective-permute-start.7 = (bf16[512,256]{1,0:T(8,128)(2,1)S(1)}, bf16[512,256]{1,0:T(8,128)(2,1)S(1)}, u32[]{:S(2)}, u32[]{:S(2)}) collective-permute-start(bf16[512,256]{1,0:T(8,128)(2,1)S(1)} %get-tuple-element.54), channel_id=1, source_target_pairs={{0,3},{1,0},{2,1},{3,2},{4,7},{5,4},{6,5},{7,6},{8,11},{9,8},{10,9... | collective-permute-start | bytes 786440 | tf_op jit(solution)/shard_map/ppermute | solution.py:234
  75.4 12.0 %collective-permute-start.1 = (bf16[512,256]{1,0:T(8,128)(2,1)}, bf16[512,256]{1,0:T(8,128)(2,1)S(1)}, u32[]{:S(2)}, u32[]{:S(2)}) collective-permute-start(bf16[512,256]{1,0:T(8,128)(2,1)} %collective-permute-done.refs_1_), channel_id=1, source_target_pairs={{0,1},{1,2},{2,3},{3,0},{4,5},{5,6},{6,7},{7,4},{8,9},{9,10},{10,1... | collective-permute-start | bytes 786440 | tf_op jit(solution)/shard_map/ppermute | solution.py:234
  75.4 12.6 %collective-permute-start.2 = (bf16[512,256]{1,0:T(8,128)(2,1)}, bf16[512,256]{1,0:T(8,128)(2,1)}, u32[]{:S(2)}, u32[]{:S(2)}) collective-permute-start(bf16[512,256]{1,0:T(8,128)(2,1)} %collective-permute-done.refs_1_), channel_id=1, source_target_pairs={{0,3},{1,0},{2,1},{3,2},{4,7},{5,4},{6,5},{7,6},{8,11},{9,8},{10,9... | collective-permute-start | bytes 786440 | tf_op jit(solution)/shard_map/ppermute | solution.py:234
  78.2 14.9 %collective-permute-start.16 = (bf16[512,256]{1,0:T(8,128)(2,1)S(1)}, bf16[512,256]{1,0:T(8,128)(2,1)S(1)}, u32[]{:S(2)}, u32[]{:S(2)}) collective-permute-start(bf16[512,256]{1,0:T(8,128)(2,1)S(1)} %get-tuple-element.53), channel_id=1, source_target_pairs={{0,1},{1,2},{2,3},{3,0},{4,5},{5,6},{6,7},{7,4},{8,9},{9,10},{10,1... | collective-permute-start | bytes 786440 | tf_op jit(solution)/shard_map/ppermute | solution.py:234
  81.9 11.3 %collective-permute-start.17 = (bf16[512,256]{1,0:T(8,128)(2,1)S(1)}, bf16[512,256]{1,0:T(8,128)(2,1)S(1)}, u32[]{:S(2)}, u32[]{:S(2)}) collective-permute-start(bf16[512,256]{1,0:T(8,128)(2,1)S(1)} %get-tuple-element.52), channel_id=1, source_target_pairs={{0,3},{1,0},{2,1},{3,2},{4,7},{5,4},{6,5},{7,6},{8,11},{9,8},{10,9... | collective-permute-start | bytes 786440 | tf_op jit(solution)/shard_map/ppermute | solution.py:234
  82.0 16.7 %collective-permute-start.11 = (bf16[512,256]{1,0:T(8,128)(2,1)}, bf16[512,256]{1,0:T(8,128)(2,1)S(1)}, u32[]{:S(2)}, u32[]{:S(2)}) collective-permute-start(bf16[512,256]{1,0:T(8,128)(2,1)} %collective-permute-done.10.refs_1_), channel_id=1, source_target_pairs={{0,1},{1,2},{2,3},{3,0},{4,5},{5,6},{6,7},{7,4},{8,9},{9,10},{10,1... | collective-permute-start | bytes 786440 | tf_op jit(solution)/shard_map/ppermute | solution.py:234
  87.4 13.4 %collective-permute-start.8 = (bf16[512,256]{1,0:T(8,128)(2,1)S(1)}, bf16[512,256]{1,0:T(8,128)(2,1)S(1)}, u32[]{:S(2)}, u32[]{:S(2)}) collective-permute-start(bf16[512,256]{1,0:T(8,128)(2,1)S(1)} %collective-permute-done.6.refs_5_), channel_id=1, source_target_pairs={{1,2},{2,3},{5,6},{6,7},{9,10},{10,11},{13,14},{14,15},{17,18},{18... | collective-permute-start | bytes 786440 | tf_op jit(solution)/shard_map/ppermute | solution.py:234
  88.0 13.4 %collective-permute-start.9 = (bf16[512,256]{1,0:T(8,128)(2,1)S(1)}, bf16[512,256]{1,0:T(8,128)(2,1)S(1)}, u32[]{:S(2)}, u32[]{:S(2)}) collective-permute-start(bf16[512,256]{1,0:T(8,128)(2,1)S(1)} %collective-permute-done.7.refs_6_), channel_id=1, source_target_pairs={{1,0},{2,1},{5,4},{6,5},{9,8},{10,9},{13,12},{14,13},{17,16},{18,1... | collective-permute-start | bytes 786440 | tf_op jit(solution)/shard_map/ppermute | solution.py:234
  93.1 48.4 %copy-start.18 = (bf16[512,256]{1,0:T(8,128)(2,1)}, bf16[512,256]{1,0:T(8,128)(2,1)S(1)}, u32[]{:S(2)}) copy-start(bf16[512,256]{1,0:T(8,128)(2,1)S(1)} %collective-permute-done.16.refs_5_) | copy-start | bytes 786436
  93.1 10.4 %collective-permute-start.12 = (bf16[512,256]{1,0:T(8,128)(2,1)}, bf16[512,256]{1,0:T(8,128)(2,1)S(1)}, u32[]{:S(2)}, u32[]{:S(2)}) collective-permute-start(bf16[512,256]{1,0:T(8,128)(2,1)} %collective-permute-done.10.refs_1_), channel_id=1, source_target_pairs={{0,3},{1,0},{2,1},{3,2},{4,7},{5,4},{6,5},{7,6},{8,11},{9,8},{10,9... | collective-permute-start | bytes 786440 | tf_op jit(solution)/shard_map/ppermute | solution.py:234
  93.2 48.3 %copy-start.19 = (bf16[512,256]{1,0:T(8,128)(2,1)}, bf16[512,256]{1,0:T(8,128)(2,1)S(1)}, u32[]{:S(2)}) copy-start(bf16[512,256]{1,0:T(8,128)(2,1)S(1)} %collective-permute-done.17.refs_6_) | copy-start | bytes 786436
  93.2 17.5 %collective-permute-start.3 = (bf16[512,256]{1,0:T(8,128)(2,1)S(1)}, bf16[512,256]{1,0:T(8,128)(2,1)S(1)}, u32[]{:S(2)}, u32[]{:S(2)}) collective-permute-start(bf16[512,256]{1,0:T(8,128)(2,1)S(1)} %collective-permute-done.1.refs_2_), channel_id=1, source_target_pairs={{3,0},{0,1},{7,4},{4,5},{11,8},{8,9},{15,12},{12,13},{19,16},{16,1... | collective-permute-start | bytes 786440 | tf_op jit(solution)/shard_map/ppermute | solution.py:234
  98.7 13.3 %collective-permute-start.4 = (bf16[512,256]{1,0:T(8,128)(2,1)}, bf16[512,256]{1,0:T(8,128)(2,1)S(1)}, u32[]{:S(2)}, u32[]{:S(2)}) collective-permute-start(bf16[512,256]{1,0:T(8,128)(2,1)} %collective-permute-done.2.refs_3_), channel_id=1, source_target_pairs={{3,2},{0,3},{7,6},{4,7},{11,10},{8,11},{15,14},{12,15},{19,18},{16... | collective-permute-start | bytes 786440 | tf_op jit(solution)/shard_map/ppermute | solution.py:234
  100.7 48.0 %collective-permute-start.18 = (bf16[512,256]{1,0:T(8,128)(2,1)S(1)}, bf16[512,256]{1,0:T(8,128)(2,1)S(1)}, u32[]{:S(2)}, u32[]{:S(2)}) collective-permute-start(bf16[512,256]{1,0:T(8,128)(2,1)S(1)} %collective-permute-done.16.refs_5_), channel_id=1, source_target_pairs={{1,2},{2,3},{5,6},{6,7},{9,10},{10,11},{13,14},{14,15},{17,18},{18... | collective-permute-start | bytes 786440 | tf_op jit(solution)/shard_map/ppermute | solution.py:234
  101.4 47.3 %collective-permute-start.19 = (bf16[512,256]{1,0:T(8,128)(2,1)S(1)}, bf16[512,256]{1,0:T(8,128)(2,1)S(1)}, u32[]{:S(2)}, u32[]{:S(2)}) collective-permute-start(bf16[512,256]{1,0:T(8,128)(2,1)S(1)} %collective-permute-done.17.refs_6_), channel_id=1, source_target_pairs={{1,0},{2,1},{5,4},{6,5},{9,8},{10,9},{13,12},{14,13},{17,16},{18,1... | collective-permute-start | bytes 786440 | tf_op jit(solution)/shard_map/ppermute | solution.py:234
  103.5 47.3 %collective-permute-start.13 = (bf16[512,256]{1,0:T(8,128)(2,1)S(1)}, bf16[512,256]{1,0:T(8,128)(2,1)S(1)}, u32[]{:S(2)}, u32[]{:S(2)}) collective-permute-start(bf16[512,256]{1,0:T(8,128)(2,1)S(1)} %collective-permute-done.11.refs_2_), channel_id=1, source_target_pairs={{3,0},{0,1},{7,4},{4,5},{11,8},{8,9},{15,12},{12,13},{19,16},{16,1... | collective-permute-start | bytes 786440 | tf_op jit(solution)/shard_map/ppermute | solution.py:234
  110.7 40.1 %collective-permute-start.14 = (bf16[512,256]{1,0:T(8,128)(2,1)S(1)}, bf16[512,256]{1,0:T(8,128)(2,1)S(1)}, u32[]{:S(2)}, u32[]{:S(2)}) collective-permute-start(bf16[512,256]{1,0:T(8,128)(2,1)S(1)} %collective-permute-done.12.refs_3_), channel_id=1, source_target_pairs={{3,2},{0,3},{7,6},{4,7},{11,10},{8,11},{15,14},{12,15},{19,18},{16... | collective-permute-start | bytes 786440 | tf_op jit(solution)/shard_map/ppermute | solution.py:234
  141.5 50.0 %collective-permute-start.24 = (bf16[512,256]{1,0:T(8,128)(2,1)}, bf16[512,256]{1,0:T(8,128)(2,1)S(1)}, u32[]{:S(2)}, u32[]{:S(2)}) collective-permute-start(bf16[512,256]{1,0:T(8,128)(2,1)} %get-tuple-element.30), channel_id=1, source_target_pairs={{0,3},{1,0},{4,7},{5,4},{8,11},{9,8},{12,15},{13,12},{16,19},{17,1... | collective-permute-start | bytes 786440 | tf_op jit(solution)/shard_map/ppermute | solution.py:234
  149.5 43.5 %collective-permute-start.26 = (bf16[512,256]{1,0:T(8,128)(2,1)}, bf16[512,256]{1,0:T(8,128)(2,1)S(1)}, u32[]{:S(2)}, u32[]{:S(2)}) collective-permute-start(bf16[512,256]{1,0:T(8,128)(2,1)} %get-tuple-element.30), channel_id=1, source_target_pairs={{2,3},{3,0},{6,7},{7,4},{10,11},{11,8},{14,15},{15,12},{18,19},{19... | collective-permute-start | bytes 786440 | tf_op jit(solution)/shard_map/ppermute | solution.py:234
  151.5 42.4 %collective-permute-start.22 = (bf16[512,256]{1,0:T(8,128)(2,1)}, bf16[512,256]{1,0:T(8,128)(2,1)S(1)}, u32[]{:S(2)}, u32[]{:S(2)}) collective-permute-start(bf16[512,256]{1,0:T(8,128)(2,1)} %get-tuple-element.26), channel_id=1, source_target_pairs={{0,1},{1,2},{4,5},{5,6},{8,9},{9,10},{12,13},{13,14},{16,17},{17,1... | collective-permute-start | bytes 786440 | tf_op jit(solution)/shard_map/ppermute | solution.py:234
  153.0 42.5 %collective-permute-start.20 = (bf16[512,256]{1,0:T(8,128)(2,1)}, bf16[512,256]{1,0:T(8,128)(2,1)S(1)}, u32[]{:S(2)}, u32[]{:S(2)}) collective-permute-start(bf16[512,256]{1,0:T(8,128)(2,1)} %get-tuple-element.26), channel_id=1, source_target_pairs={{2,1},{3,2},{6,5},{7,6},{10,9},{11,10},{14,13},{15,14},{18,17},{19... | collective-permute-start | bytes 786440 | tf_op jit(solution)/shard_map/ppermute | solution.py:234
  182.4 16.5 %collective-permute-start.34 = (bf16[512,256]{1,0:T(8,128)(2,1)}, bf16[512,256]{1,0:T(8,128)(2,1)S(1)}, u32[]{:S(2)}, u32[]{:S(2)}) collective-permute-start(bf16[512,256]{1,0:T(8,128)(2,1)} %get-tuple-element.38), channel_id=1, source_target_pairs={{0,3},{1,0},{4,7},{5,4},{8,11},{9,8},{12,15},{13,12},{16,19},{17,1... | collective-permute-start | bytes 786440 | tf_op jit(solution)/shard_map/ppermute | solution.py:234
  191.6 8.5 %collective-permute-start.36 = (bf16[512,256]{1,0:T(8,128)(2,1)}, bf16[512,256]{1,0:T(8,128)(2,1)S(1)}, u32[]{:S(2)}, u32[]{:S(2)}) collective-permute-start(bf16[512,256]{1,0:T(8,128)(2,1)} %get-tuple-element.38), channel_id=1, source_target_pairs={{2,3},{3,0},{6,7},{7,4},{10,11},{11,8},{14,15},{15,12},{18,19},{19... | collective-permute-start | bytes 786440 | tf_op jit(solution)/shard_map/ppermute | solution.py:234
  193.0 7.2 %collective-permute-start.30 = (bf16[512,256]{1,0:T(8,128)(2,1)}, bf16[512,256]{1,0:T(8,128)(2,1)S(1)}, u32[]{:S(2)}, u32[]{:S(2)}) collective-permute-start(bf16[512,256]{1,0:T(8,128)(2,1)} %get-tuple-element.34), channel_id=1, source_target_pairs={{2,1},{3,2},{6,5},{7,6},{10,9},{11,10},{14,13},{15,14},{18,17},{19... | collective-permute-start | bytes 786440 | tf_op jit(solution)/shard_map/ppermute | solution.py:234
  193.9 9.4 %collective-permute-start.32 = (bf16[512,256]{1,0:T(8,128)(2,1)}, bf16[512,256]{1,0:T(8,128)(2,1)S(1)}, u32[]{:S(2)}, u32[]{:S(2)}) collective-permute-start(bf16[512,256]{1,0:T(8,128)(2,1)} %get-tuple-element.34), channel_id=1, source_target_pairs={{0,1},{1,2},{4,5},{5,6},{8,9},{9,10},{12,13},{13,14},{16,17},{17,1... | collective-permute-start | bytes 786440 | tf_op jit(solution)/shard_map/ppermute | solution.py:234
  195.4 8.5 %collective-permute-start.25 = (bf16[512,256]{1,0:T(8,128)(2,1)S(1)}, bf16[512,256]{1,0:T(8,128)(2,1)S(1)}, u32[]{:S(2)}, u32[]{:S(2)}) collective-permute-start(bf16[512,256]{1,0:T(8,128)(2,1)S(1)} %add_convert_fusion.7), channel_id=1, source_target_pairs={{1,0},{2,1},{3,2},{0,3},{5,4},{6,5},{7,6},{4,7},{9,8},{10,9},{11,1... | collective-permute-start | bytes 786440 | tf_op jit(solution)/shard_map/ppermute | solution.py:234
  198.9 7.7 %collective-permute-start.27 = (bf16[512,256]{1,0:T(8,128)(2,1)S(1)}, bf16[512,256]{1,0:T(8,128)(2,1)S(1)}, u32[]{:S(2)}, u32[]{:S(2)}) collective-permute-start(bf16[512,256]{1,0:T(8,128)(2,1)S(1)} %add_convert_fusion.6), channel_id=1, source_target_pairs={{3,0},{0,1},{1,2},{2,3},{7,4},{4,5},{5,6},{6,7},{11,8},{8,9},{9,10... | collective-permute-start | bytes 786440 | tf_op jit(solution)/shard_map/ppermute | solution.py:234
  200.1 11.5 %collective-permute-start.23 = (bf16[512,256]{1,0:T(8,128)(2,1)S(1)}, bf16[512,256]{1,0:T(8,128)(2,1)S(1)}, u32[]{:S(2)}, u32[]{:S(2)}) collective-permute-start(bf16[512,256]{1,0:T(8,128)(2,1)S(1)} %add_convert_fusion.8), channel_id=1, source_target_pairs={{3,0},{0,1},{1,2},{2,3},{7,4},{4,5},{5,6},{6,7},{11,8},{8,9},{9,10... | collective-permute-start | bytes 786440 | tf_op jit(solution)/shard_map/ppermute | solution.py:234
  200.2 12.7 %collective-permute-start.21 = (bf16[512,256]{1,0:T(8,128)(2,1)S(1)}, bf16[512,256]{1,0:T(8,128)(2,1)S(1)}, u32[]{:S(2)}, u32[]{:S(2)}) collective-permute-start(bf16[512,256]{1,0:T(8,128)(2,1)S(1)} %add_convert_fusion.9), channel_id=1, source_target_pairs={{1,0},{2,1},{3,2},{0,3},{5,4},{6,5},{7,6},{4,7},{9,8},{10,9},{11,1... | collective-permute-start | bytes 786440 | tf_op jit(solution)/shard_map/ppermute | solution.py:234
  203.3 26.7 %collective-permute-start.35 = (bf16[512,256]{1,0:T(8,128)(2,1)S(1)}, bf16[512,256]{1,0:T(8,128)(2,1)S(1)}, u32[]{:S(2)}, u32[]{:S(2)}) collective-permute-start(bf16[512,256]{1,0:T(8,128)(2,1)S(1)} %add_convert_fusion.2), channel_id=1, source_target_pairs={{1,0},{2,1},{3,2},{0,3},{5,4},{6,5},{7,6},{4,7},{9,8},{10,9},{11,1... | collective-permute-start | bytes 786440 | tf_op jit(solution)/shard_map/ppermute | solution.py:234
  203.9 27.1 %collective-permute-start.37 = (bf16[512,256]{1,0:T(8,128)(2,1)S(1)}, bf16[512,256]{1,0:T(8,128)(2,1)S(1)}, u32[]{:S(2)}, u32[]{:S(2)}) collective-permute-start(bf16[512,256]{1,0:T(8,128)(2,1)S(1)} %add_convert_fusion.1), channel_id=1, source_target_pairs={{3,0},{0,1},{1,2},{2,3},{7,4},{4,5},{5,6},{6,7},{11,8},{8,9},{9,10... | collective-permute-start | bytes 786440 | tf_op jit(solution)/shard_map/ppermute | solution.py:234
  206.6 27.8 %collective-permute-start.31 = (bf16[512,256]{1,0:T(8,128)(2,1)S(1)}, bf16[512,256]{1,0:T(8,128)(2,1)S(1)}, u32[]{:S(2)}, u32[]{:S(2)}) collective-permute-start(bf16[512,256]{1,0:T(8,128)(2,1)S(1)} %add_convert_fusion.4), channel_id=1, source_target_pairs={{1,0},{2,1},{3,2},{0,3},{5,4},{6,5},{7,6},{4,7},{9,8},{10,9},{11,1... | collective-permute-start | bytes 786440 | tf_op jit(solution)/shard_map/ppermute | solution.py:234
  211.7 22.7 %collective-permute-start.33 = (bf16[512,256]{1,0:T(8,128)(2,1)S(1)}, bf16[512,256]{1,0:T(8,128)(2,1)S(1)}, u32[]{:S(2)}, u32[]{:S(2)}) collective-permute-start(bf16[512,256]{1,0:T(8,128)(2,1)S(1)} %add_convert_fusion.3), channel_id=1, source_target_pairs={{3,0},{0,1},{1,2},{2,3},{7,4},{4,5},{5,6},{6,7},{11,8},{8,9},{9,10... | collective-permute-start | bytes 786440 | tf_op jit(solution)/shard_map/ppermute | solution.py:234
  212.9 22.3 %collective-permute-start.28 = (bf16[512,256]{1,0:T(8,128)(2,1)S(1)}, bf16[512,256]{1,0:T(8,128)(2,1)S(1)}, u32[]{:S(2)}, u32[]{:S(2)}) collective-permute-start(bf16[512,256]{1,0:T(8,128)(2,1)S(1)} %add_convert_fusion.5), channel_id=1, source_target_pairs={{4,0},{5,1},{6,2},{7,3},{8,4},{9,5},{10,6},{11,7},{12,8},{13,9},{1... | collective-permute-start | bytes 786440 | tf_op jit(solution)/shard_map/ppermute | solution.py:229
  229.9 7.4 %collective-permute-start.29 = (bf16[512,256]{1,0:T(8,128)(2,1)S(1)}, bf16[512,256]{1,0:T(8,128)(2,1)S(1)}, u32[]{:S(2)}, u32[]{:S(2)}) collective-permute-start(bf16[512,256]{1,0:T(8,128)(2,1)S(1)} %fusion.9), channel_id=1, source_target_pairs={{8,0},{9,1},{10,2},{11,3},{12,4},{13,5},{14,6},{15,7},{16,8},{17,9... | collective-permute-start | bytes 786440 | tf_op jit(solution)/shard_map/ppermute | solution.py:229
  231.2 22.0 %collective-permute-start.38 = (bf16[512,256]{1,0:T(8,128)(2,1)S(1)}, bf16[512,256]{1,0:T(8,128)(2,1)S(1)}, u32[]{:S(2)}, u32[]{:S(2)}) collective-permute-start(bf16[512,256]{1,0:T(8,128)(2,1)S(1)} %add_convert_fusion), channel_id=1, source_target_pairs={{4,0},{5,1},{6,2},{7,3},{8,4},{9,5},{10,6},{11,7},{12,8},{13,9},{1... | collective-permute-start | bytes 786440 | tf_op jit(solution)/shard_map/ppermute | solution.py:229
  234.5 18.7 %collective-permute-start.39 = (bf16[512,256]{1,0:T(8,128)(2,1)S(1)}, bf16[512,256]{1,0:T(8,128)(2,1)S(1)}, u32[]{:S(2)}, u32[]{:S(2)}) collective-permute-start(bf16[512,256]{1,0:T(8,128)(2,1)S(1)} %fusion.16), channel_id=1, source_target_pairs={{8,0},{9,1},{10,2},{11,3},{12,4},{13,5},{14,6},{15,7},{16,8},{17,9... | collective-permute-start | bytes 786440 | tf_op jit(solution)/shard_map/ppermute | solution.py:229
  238.2 21.5 %all-to-all-start.6 = ((bf16[4,128,256]{2,1,0:T(8,128)(2,1)}), bf16[4,128,256]{2,1,0:T(8,128)(2,1)S(1)}, u32[]{:S(2)}, u32[]{:S(2)}) async-start(bf16[4,128,256]{2,1,0:T(8,128)(2,1)} %bitcast.27), calls=%async_computation.6 | async-start | bytes 524288 | tf_op jit(solution)/shard_map/all_to_all | solution.py:282
  300.3 31.8 %all-to-all-start.5 = ((bf16[4,2,128,1024]{3,2,1,0:T(8,128)(2,1)}), bf16[4,2,128,1024]{3,2,1,0:T(8,128)(2,1)}, u32[]{:S(2)}, u32[]{:S(2)}) async-start(bf16[4,2,128,1024]{3,2,1,0:T(8,128)(2,1)} %get-tuple-element.23), calls=%async_computation.5 | async-start | bytes 4194304 | tf_op jit(solution)/shard_map/all_to_all | solution.py:282
  (23 other events, 518.6 us)

commit v2 on v1

v2 whole, which is shorter than its diff:
```python
import jax
import jax.numpy as jnp
from jax import lax
from jax.experimental import pallas as pl
from jax.experimental.pallas import tpu as pltpu
from jax.sharding import PartitionSpec as P


QUERY_HEADS = 64
KEY_VALUE_HEADS = 8
HEAD_SIZE = 128
BLOCK = 128
NSTEP = 8
NB = 4
QUAD = 4
GROUP = QUERY_HEADS // KEY_VALUE_HEADS
WIDE = GROUP * BLOCK
MOST = NSTEP * NB
NEGATIVE_FILL = -1e30
SCALE = HEAD_SIZE ** (-0.5)
SCALE_LOG2 = SCALE * 1.4426950408889634
TILE = 256
F32 = jnp.float32
BF16 = jnp.bfloat16


def dot(a, b):
    return lax.dot_general(a, b, (((1,), (0,)), ((), ())), preferred_element_type=F32)


def dot_nt(a, b):
    return lax.dot_general(a, b, (((1,), (1,)), ((), ())), preferred_element_type=F32)


def attend(
    codes, counts, place, qd_ref, own_in, prev_in, near_1, near_2, near_3, out_ref, own_out, prev_out, part_1, part_2, part_3,
    pairs, filled, kvs, dkv, masks, q_t, g_t, scores, weights, top, total, row, turned,
):
    t = pl.program_id(0)

    @pl.when(t == 0)
    def _():
        y = place[0]
        for b in range(NB):
            pairs[b, 0] = b
            filled[b] = 1
        for s in range(NSTEP):
            d = s % QUAD
            if d == 0:
                slot = 0 if s == 0 else 1
            elif s < QUAD:
                slot = 2 * d + jnp.where(y >= d, 1, 0)
            else:
                slot = 2 * d + jnp.where(y >= d, 0, 1)

            def add(i, carry, s=s, slot=slot):
                code = codes[s, i]
                b = lax.shift_right_logical(code, 2)
                c = jnp.bitwise_and(code, 3)

                def put():
                    n = filled[b]
                    pairs[b, n] = slot * NB + c
                    filled[b] = n + 1

                if s == 0:
                    pl.when(b != c)(put)
                else:
                    put()
                return carry

            lax.fori_loop(0, counts[s], add, 0)
        for b in range(NB):
            pairs[b, filled[b]] = b
        kvs[0:NB] = own_in[...]
        kvs[NB : 2 * NB] = prev_in[...]
        for d, ref in enumerate((near_1, near_2, near_3), 1):
            for m in range(2):
                kvs[(2 * d + m) * NB : (2 * d + m + 1) * NB] = ref[m]
        dkv[...] = jnp.zeros_like(dkv)
        keys_at = lax.broadcasted_iota(jnp.int32, (BLOCK, BLOCK), 0)
        rows_at = lax.broadcasted_iota(jnp.int32, (BLOCK, BLOCK), 1)
        masks[0] = jnp.zeros((BLOCK, BLOCK), F32)
        masks[1] = jnp.where(keys_at <= rows_at, 0.0, NEGATIVE_FILL)
        masks[2] = jnp.full((BLOCK, BLOCK), NEGATIVE_FILL, F32)

    for h in range(GROUP):
        at = pl.ds(h * BLOCK, BLOCK)
        q = qd_ref[0, :, at]
        q_t[:, at] = q.T
        g_t[:, at] = qd_ref[1, :, at].T

    n = filled[t]
    trips = lax.shift_right_logical(n + 1, 1)
    top[...] = jnp.full_like(top, NEGATIVE_FILL)
    total[...] = jnp.zeros_like(total)
    turned[...] = jnp.zeros_like(turned)

    def two(i, lo):
        a, b = pairs[t, 2 * i], pairs[t, 2 * i + 1]
        return jnp.concatenate([kvs[a, :, pl.ds(lo, HEAD_SIZE)], kvs[b, :, pl.ds(lo, HEAD_SIZE)]], axis=0)

    def score_visit(i, carry):
        k = two(i, 0)
        first = masks[jnp.where(i == 0, 1, 0)]
        second = masks[jnp.where(2 * i + 1 >= n, 2, 0)]
        mask = jnp.concatenate([first, second], axis=0)
        mask = jnp.concatenate([mask, mask], axis=1)
        for w in range(WIDE // TILE):
            at = pl.ds(w * TILE, TILE)
            s = dot(k, q_t[:, at]) * SCALE_LOG2 + mask
            scores[pl.ds(2 * i, 2), :, at] = s.reshape(2, BLOCK, TILE)
            top[:, at] = jnp.maximum(top[:, at], jnp.max(s.reshape(2 * BLOCK // 8, 8, TILE), axis=0))
        return carry

    lax.fori_loop(0, trips, score_visit, 0)
    top[...] = jnp.broadcast_to(jnp.max(top[...], axis=0, keepdims=True), top.shape)

    def weight_visit(i, carry):
        v_t = two(i, HEAD_SIZE).T
        for w in range(WIDE // TILE):
            at = pl.ds(w * TILE, TILE)
            s = scores[pl.ds(2 * i, 2), :, at].reshape(2 * BLOCK // 8, 8, TILE)
            p = jnp.exp2(s - top[:, at][None])
            total[:, at] += jnp.sum(p, axis=0)
            low = p.reshape(2 * BLOCK, TILE).astype(BF16)
            weights[pl.ds(2 * i, 2), :, at] = low.reshape(2, BLOCK, TILE)
            turned[:, at] += dot(v_t, low)
        return carry

    lax.fori_loop(0, trips, weight_visit, 0)

    for h in range(GROUP):
        at = pl.ds(h * BLOCK, BLOCK)
        inverse = 1.0 / jnp.sum(total[:, at], axis=0, keepdims=True)
        attn = (turned[:, at] * inverse).astype(BF16)
        out_ref[0, :, at] = attn.T
        grad = (g_t[:, at].astype(F32) * inverse).astype(BF16)
        g_t[:, at] = grad
        row[:, at] = jnp.broadcast_to(
            jnp.sum(grad.astype(F32) * attn.astype(F32), axis=0, keepdims=True), (8, BLOCK)
        )
    turned[...] = jnp.zeros_like(turned)

    def back_visit(i, carry):
        k = two(i, 0)
        v = two(i, HEAD_SIZE)
        k_t = k.T
        tiles = [pl.ds(w * TILE, TILE) for w in range(WIDE // TILE)]
        dp = dot(v, g_t[:, tiles[0]])
        dk = dv = None
        for w, at in enumerate(tiles):
            ahead = dot(v, g_t[:, tiles[w + 1]]) if w + 1 < len(tiles) else None
            low = weights[pl.ds(2 * i, 2), :, at].reshape(2 * BLOCK, TILE)
            dv_w = dot_nt(g_t[:, at], low)
            dv = dv_w if dv is None else dv + dv_w
            p = low.astype(F32)
            ds = p.reshape(2 * BLOCK // 8, 8, TILE) * (dp.reshape(2 * BLOCK // 8, 8, TILE) - row[:, at][None])
            ds = ds.reshape(2 * BLOCK, TILE).astype(BF16)
            turned[:, at] += dot(k_t, ds)
            dk_w = dot_nt(q_t[:, at], ds)
            dk = dk_w if dk is None else dk + dk_w
            dp = ahead
        for half in range(2):
            a = pairs[t, 2 * i + half]
            columns = slice(half * BLOCK, (half + 1) * BLOCK)
            dkv[a, pl.ds(0, HEAD_SIZE)] += dk[:, columns]
            dkv[a, pl.ds(HEAD_SIZE, HEAD_SIZE)] += dv[:, columns]
        return carry

    lax.fori_loop(0, trips, back_visit, 0)

    for h in range(GROUP):
        at = pl.ds(h * BLOCK, BLOCK)
        out_ref[1, :, at] = (turned[:, at] * SCALE).astype(BF16).T

    @pl.when(t == NB - 1)
    def _():
        left, right = pl.ds(0, HEAD_SIZE), pl.ds(HEAD_SIZE, HEAD_SIZE)
        for c in range(NB):
            for at, ref in enumerate((own_out, prev_out)):
                ref[c, :, left] = (dkv[at * NB + c, left] * SCALE).T
                ref[c, :, right] = dkv[at * NB + c, right].T
            for d, ref in enumerate((part_1, part_2, part_3), 1):
                for m in range(2):
                    at = (2 * d + m) * NB + c
                    ref[m, c, :, left] = (dkv[at, left] * SCALE).astype(BF16).T
                    ref[m, c, :, right] = dkv[at, right].astype(BF16).T


def attend_call(j, codes, counts, place, qd, own, prev, near):
    mine = pl.BlockSpec((NB, None, BLOCK, 2 * HEAD_SIZE), lambda t, *_: (0, j, 0, 0))
    whole = pl.BlockSpec((2, NB, BLOCK, 2 * HEAD_SIZE), lambda t, *_: (0, 0, 0, 0))
    flat = pl.BlockSpec((NB, BLOCK, 2 * HEAD_SIZE), lambda t, *_: (0, 0, 0))
    block = pl.BlockSpec((None, 2, BLOCK, WIDE), lambda t, *_: (t, 0, 0, 0))
    return pl.pallas_call(
        attend,
        name="attend",
        grid_spec=pltpu.PrefetchScalarGridSpec(
            num_scalar_prefetch=3,
            grid=(NB,),
            in_specs=[block, mine, mine, whole, whole, whole],
            out_specs=[block, flat, flat, whole, whole, whole],
            scratch_shapes=[
                pltpu.SMEM((NB, MOST + 8), jnp.int32),
                pltpu.SMEM((NB,), jnp.int32),
                pltpu.VMEM((MOST, BLOCK, 2 * HEAD_SIZE), BF16),
                pltpu.VMEM((MOST, 2 * HEAD_SIZE, BLOCK), F32),
                pltpu.VMEM((3, BLOCK, BLOCK), F32),
                pltpu.VMEM((HEAD_SIZE, WIDE), BF16),
                pltpu.VMEM((HEAD_SIZE, WIDE), BF16),
                pltpu.VMEM((MOST, BLOCK, WIDE), F32),
                pltpu.VMEM((MOST, BLOCK, WIDE), BF16),
                pltpu.VMEM((8, WIDE), F32),
                pltpu.VMEM((8, WIDE), F32),
                pltpu.VMEM((8, WIDE), F32),
                pltpu.VMEM((HEAD_SIZE, WIDE), F32),
            ],
        ),
        out_shape=[
            jax.ShapeDtypeStruct(qd.shape, BF16),
            jax.ShapeDtypeStruct((NB, BLOCK, 2 * HEAD_SIZE), F32),
            jax.ShapeDtypeStruct((NB, BLOCK, 2 * HEAD_SIZE), F32),
        ]
        + [jax.ShapeDtypeStruct((2, NB, BLOCK, 2 * HEAD_SIZE), BF16)] * 3,
        cost_estimate=pl.CostEstimate(flops=30_000_000_000, bytes_accessed=20_000_000, transcendentals=70_000_000),
        compiler_params=pltpu.CompilerParams(
            dimension_semantics=("arbitrary",), vmem_limit_bytes=58 * 1024 * 1024
        ),
    )(codes, counts, place, qd, own, prev, *near)


def pack_rows(j, query, grad):
    def kernel(q_ref, g_ref, o_ref):
        o_ref[0] = q_ref[...]
        o_ref[1] = g_ref[...]

    tokens = query.shape[0]
    ranks = query.shape[1] // (2 * WIDE)
    column = pl.BlockSpec((tokens, WIDE), lambda r: (0, 2 * r + j))
    return pl.pallas_call(
        kernel,
        name="pack_rows",
        grid=(ranks,),
        in_specs=[column, column],
        out_specs=pl.BlockSpec((None, 2, tokens, WIDE), lambda r: (r, 0, 0, 0)),
        out_shape=jax.ShapeDtypeStruct((ranks, 2, tokens, WIDE), BF16),
    )(query, grad)


def pack_keys(key, value):
    def kernel(k_ref, v_ref, o_ref):
        for r in range(ranks):
            for j in range(2):
                at = pl.ds((2 * r + j) * HEAD_SIZE, HEAD_SIZE)
                o_ref[r, j, :, pl.ds(0, HEAD_SIZE)] = k_ref[:, at]
                o_ref[r, j, :, pl.ds(HEAD_SIZE, HEAD_SIZE)] = v_ref[:, at]

    tokens = key.shape[0]
    ranks = key.shape[1] // (2 * HEAD_SIZE)
    return pl.pallas_call(
        kernel,
        name="pack_keys",
        out_shape=jax.ShapeDtypeStruct((ranks, 2, tokens, 2 * HEAD_SIZE), BF16),
    )(key, value)


def pack_window(place, own, prev, back):
    def kernel(y_ref, own_ref, prev_ref, back_ref, *out_refs):
        for d in range(1, QUAD):
            for j in range(2):
                out = out_refs[2 * (d - 1) + j]
                out[0] = prev_ref[:, j]
                pick = y_ref[0] + d < QUAD

                @pl.when(pick)
                def _(out=out, j=j):
                    out[1] = own_ref[:, j]

                @pl.when(jnp.logical_not(pick))
                def _(out=out, j=j):
                    out[1] = back_ref[:, j]

    shape = (2,) + own.shape[:1] + own.shape[2:]
    vmem = pl.BlockSpec(memory_space=pltpu.VMEM)
    outs = pl.pallas_call(
        kernel,
        name="pack_window",
        in_specs=[pl.BlockSpec(memory_space=pltpu.SMEM), vmem, vmem, vmem],
        out_specs=[vmem] * 6,
        out_shape=[jax.ShapeDtypeStruct(shape, BF16)] * 6,
    )(place, own, prev, back)
    return [outs[j::2] for j in range(2)]


def unpack_rows(j, got, filled):
    def kernel(got_ref, *refs):
        a_ref, g_ref = refs[-2:]
        a_ref[...] = got_ref[0]
        g_ref[...] = got_ref[1]

    ranks, _, tokens, _ = got.shape
    column = pl.BlockSpec((tokens, WIDE), lambda r: (0, 2 * r + j))
    whole = jax.ShapeDtypeStruct((tokens, ranks * 2 * WIDE), BF16)
    given = () if filled is None else filled
    return pl.pallas_call(
        kernel,
        name="unpack_rows",
        grid=(ranks,),
        in_specs=[pl.BlockSpec((None, 2, tokens, WIDE), lambda r: (r, 0, 0, 0))]
        + [pl.BlockSpec(memory_space=pl.ANY)] * len(given),
        out_specs=[column, column],
        out_shape=[whole, whole],
        input_output_aliases={} if filled is None else {1: 0, 2: 1},
    )(got, *given)


def unpack_keys(got):
    def kernel(got_ref, k_ref, v_ref):
        for r in range(ranks):
            for j in range(2):
                at = pl.ds((2 * r + j) * HEAD_SIZE, HEAD_SIZE)
                k_ref[:, at] = got_ref[r, j, :, pl.ds(0, HEAD_SIZE)]
                v_ref[:, at] = got_ref[r, j, :, pl.ds(HEAD_SIZE, HEAD_SIZE)]

    ranks, _, tokens, _ = got.shape
    whole = jax.ShapeDtypeStruct((tokens, ranks * 2 * HEAD_SIZE), BF16)
    return pl.pallas_call(kernel, name="unpack_keys", out_shape=[whole, whole])(got)


def shifted(x, distance):
    n = lax.axis_size("blk")
    return lax.ppermute(x, "blk", [((i - distance) % n, i) for i in range(n)])


def turned_in_quad(x, d):
    n = lax.axis_size("blk")
    return lax.ppermute(x, "blk", [(i, i - i % QUAD + (i + d) % QUAD) for i in range(n)])


def add_parts(place, own, prev, parts):
    def kernel(y_ref, own_ref, prev_ref, *refs):
        part_refs, own_out, prev_out, back_out = refs[:-3], refs[-3], refs[-2], refs[-1]
        mine, before = own_ref[...], prev_ref[...]
        back = jnp.zeros_like(mine)
        for d, ref in enumerate(part_refs, 1):
            before = before + ref[0].astype(F32)
            other = ref[1].astype(F32)
            ahead = (y_ref[0] + d < QUAD).astype(F32)
            mine = mine + ahead * other
            back = back + (1.0 - ahead) * other
        own_out[...] = mine
        prev_out[...] = before.astype(BF16)
        back_out[...] = back.astype(BF16)

    block = (BLOCK, 2 * HEAD_SIZE)
    flat = pl.BlockSpec((None,) + block, lambda c: (c, 0, 0))
    pair = pl.BlockSpec((2, None) + block, lambda c: (0, c, 0, 0))
    return pl.pallas_call(
        kernel,
        name="add_parts",
        grid=(NB,),
        in_specs=[pl.BlockSpec(memory_space=pltpu.SMEM), flat, flat] + [pair] * len(parts),
        out_specs=[flat] * 3,
        out_shape=[
            jax.ShapeDtypeStruct(own.shape, F32),
            jax.ShapeDtypeStruct(own.shape, BF16),
            jax.ShapeDtypeStruct(own.shape, BF16),
        ],
    )(place, own, prev, *parts)


def add_home(sums):
    def kernel(*refs):
        out = refs[-1]
        for j in range(2):
            own, prev, back = (ref[...].astype(F32) for ref in refs[3 * j : 3 * j + 3])
            out[j] = (own + prev + back).astype(BF16)

    block = (BLOCK, 2 * HEAD_SIZE)
    flat = pl.BlockSpec((None,) + block, lambda c: (c, 0, 0))
    return pl.pallas_call(
        kernel,
        name="add_home",
        grid=(NB,),
        in_specs=[flat] * 6,
        out_specs=pl.BlockSpec((None, 2) + block, lambda c: (c, 0, 0, 0)),
        out_shape=jax.ShapeDtypeStruct((NB, 2) + block, BF16),
    )(*sums)


def gathered(place, own, prev, parts):
    got = [turned_in_quad(part, -d) for d, part in enumerate(parts, 1)]
    own, prev, back = add_parts(place, own, prev, got)
    return [own, shifted(prev, -QUAD), shifted(back, -2 * QUAD)]


def swap(x):
    return lax.all_to_all(x, "head", split_axis=0, concat_axis=0, tiled=True)


def layer(query, key, value, output_gradient, pair_codes, pair_counts):
    y = lax.axis_index("blk") % QUAD
    place = jnp.full((1,), y, jnp.int32)
    codes, counts = pair_codes[0], pair_counts[0]
    own = swap(pack_keys(key, value))
    prev, back = shifted(own, QUAD), shifted(own, 2 * QUAD)
    sends = pack_window(place, own, prev, back)
    near, rows = [], []
    for j in range(2):
        near.append([turned_in_quad(sends[j][d - 1], d) for d in range(1, QUAD)])
        packed = pack_rows(j, query, output_gradient)
        rows.append(swap(packed))
    filled, sums = None, []
    for j in range(2):
        both, own_sum, prev_sum, *parts = attend_call(j, codes, counts, place, rows[j], own, prev, near[j])
        got = swap(both)
        filled = unpack_rows(j, got, filled)
        sums += gathered(place, own_sum, prev_sum, parts)
    both = add_home(sums)
    got = swap(both)
    key_gradient, value_gradient = unpack_keys(got)
    return filled[0], filled[1], key_gradient, value_gradient


def solution(mesh):
    rows = P(("blk", "head"), None)
    return jax.shard_map(
        layer,
        mesh=mesh,
        in_specs=(rows, rows, rows, rows, P("blk", None, None), P("blk", None)),
        out_specs=(rows, rows, rows, rows),
        check_vma=False,
    )
```

time: 353 us -> 282 us (0.80)
  the two profiles are of different devices: /device:TPU:1 before, /device:TPU:192 now
where the time goes in v2:
time: 282 us; the launch traced here: 277 us
  waiting for transfers between devices  97.7 us (35%)
  Pallas kernels  77.4 us (27%)
  starting transfers between devices  51 us (18%)
  blocking collectives  45.2 us (16%)
  local copies, waits for them, and re-layouts  4.66 us (2%)
    all_to_all x2, blocking collectives, swap(): return lax.all_to_all(x, 'head', split_axis=0, concat_axis=0, tiled=True)  45.2 us
    pallas_call x2, Pallas kernels, attend_call(): pl.pallas_call(attend, name='attend', grid_spec=pltpu.PrefetchScalarGridS...  44.1 us
    ppermute x6, waiting for transfers between devices, shifted(): return lax.ppermute(x, 'blk', [((i - distance) % n, i) for i in range(n)])  42.2 us
    ppermute x12, starting transfers between devices, turned_in_quad(): lax.ppermute(x, 'blk', [(i, i - i % QUAD + (i + d) % QUAD) for i in range...  29.7 us
    all_to_all x4, waiting for transfers between devices, swap(): return lax.all_to_all(x, 'head', split_axis=0, concat_axis=0, tiled=True)  28 us
    ppermute x12, waiting for transfers between devices, turned_in_quad(): lax.ppermute(x, 'blk', [(i, i - i % QUAD + (i + d) % QUAD) for i in range...  27.6 us
    all_to_all x4, starting transfers between devices, swap(): return lax.all_to_all(x, 'head', split_axis=0, concat_axis=0, tiled=True)  16 us
    pallas_call x2, Pallas kernels, add_parts(): pl.pallas_call(kernel, name='add_parts', grid=(NB,), in_specs=[pl.BlockSp...  7.57 us
  transfers between devices with their start and end apart: 22, of which 10 were waited for; matrix products, arithmetic and copies ran while one was open for 0% of the time, Pallas kernels for 25%

profile of v2, /device:TPU:192, one launch (start us, length us, event | category | flops | bytes accessed | tf_op | source)
XLA Modules:
  0.0 276.7 jit_solution(14061457361704443129)
XLA Ops:
  0.6 1.9 pack_keys.1
  2.5 4.3 %all-to-all-start.1 = ((bf16[4,2,128,256]{3,2,1,0:T(8,128)(2,1)}), bf16[4,2,128,256]{3,2,1,0:T(8,128)(2,1)S(1)}, u32[]{:S(2)}, u32[]{:S(2)}) async-start(bf16[4,2,128,256]{3,2,1,0:T(8,128)(2,1)} %pack_keys.1), calls=%async_computation.1 | async-start | bytes 1048576 | tf_op jit(solution)/shard_map/all_to_all | solution.py:399
  6.8 3.8 %pack_rows.2 = bf16[4,2,128,1024]{3,2,1,0:T(8,128)(2,1)} custom-call(bf16[128,8192]{1,0:T(8,128)(2,1)} %q_ref.3, bf16[128,8192]{1,0:T(8,128)(2,1)} %g_ref.3), custom_call_target="tpu_custom_call" | custom-call | tf_op jit(solution)/shard_map/pack_rows/pallas_call | solution.py:241
  10.6 6.6 %all-to-all-done.1.own_ref.own_in = bf16[4,2,128,256]{3,2,1,0:T(8,128)(2,1)S(1)} async-done(((bf16[4,2,128,256]{3,2,1,0:T(8,128)(2,1)}), bf16[4,2,128,256]{3,2,1,0:T(8,128)(2,1)S(1)}, u32[]{:S(2)}, u32[]{:S(2)}) %all-to-all-start.1) | async-done | bytes 524320 | tf_op jit(solution)/shard_map/all_to_all | solution.py:399
  17.2 3.6 %all-to-all-start = ((bf16[4,2,128,1024]{3,2,1,0:T(8,128)(2,1)}), bf16[4,2,128,1024]{3,2,1,0:T(8,128)(2,1)S(1)}, u32[]{:S(2)}, u32[]{:S(2)}) async-start(bf16[4,2,128,1024]{3,2,1,0:T(8,128)(2,1)} %pack_rows.2), calls=%async_computation | async-start | bytes 4194304 | tf_op jit(solution)/shard_map/all_to_all | solution.py:399
  20.8 0.7 collective-permute-start
  21.5 1.0 collective-permute-start.1
  22.5 33.0 %collective-permute-done.prev_ref.prev_in = bf16[4,2,128,256]{3,2,1,0:T(8,128)(2,1)S(1)} collective-permute-done((bf16[4,2,128,256]{3,2,1,0:T(8,128)(2,1)S(1)}, bf16[4,2,128,256]{3,2,1,0:T(8,128)(2,1)S(1)}, u32[]{:S(2)}, u32[]{:S(2)}) %collective-permute-start) | collective-permute-done | bytes 524320 | tf_op jit(solution)/shard_map/ppermute | solution.py:333
  55.6 0.8 copy-done.4
  56.4 3.2 %pack_window.1 = (bf16[2,4,128,256]{3,2,1,0:T(8,128)(2,1)}, bf16[2,4,128,256]{3,2,1,0:T(8,128)(2,1)}, bf16[2,4,128,256]{3,2,1,0:T(8,128)(2,1)}, bf16[2,4,128,256...) custom-call(s32[1]{0:T(128)} %bitcast.2.y_ref.place, ...), custom_call_target="tpu_custom_call" | custom-call | tf_op jit(solution)/shard_map/pack_window/pallas_call | solution.py:286
  59.6 1.6 collective-permute-start.2
  61.2 2.9 %collective-permute-start.3 = (bf16[2,4,128,256]{3,2,1,0:T(8,128)(2,1)}, bf16[2,4,128,256]{3,2,1,0:T(8,128)(2,1)}, u32[]{:S(2)}, u32[]{:S(2)}) collective-permute-start(bf16[2,4,128,256]{3,2,1,0:T(8,128)(2,1)} %get-tuple-element.35), channel_id=1, source_target_pairs={{0,2},{1,3},{2,0},{3,1},{4,6},{5,7},{6,4},{7,5},{8,10},{9,11},{10,... | collective-permute-start | bytes 1572872 | tf_op jit(solution)/shard_map/ppermute | solution.py:338
  64.1 1.4 collective-permute-start.4
  65.4 3.8 %pack_rows.3 = bf16[4,2,128,1024]{3,2,1,0:T(8,128)(2,1)} custom-call(bf16[128,8192]{1,0:T(8,128)(2,1)} %q_ref.3, bf16[128,8192]{1,0:T(8,128)(2,1)} %g_ref.3), custom_call_target="tpu_custom_call" | custom-call | tf_op jit(solution)/shard_map/pack_rows/pallas_call | solution.py:241
  69.2 0.7 collective-permute-start.5
  69.9 0.8 collective-permute-start.6
  70.7 4.5 %all-to-all-start.3 = ((bf16[4,2,128,1024]{3,2,1,0:T(8,128)(2,1)}), bf16[4,2,128,1024]{3,2,1,0:T(8,128)(2,1)}, u32[]{:S(2)}, u32[]{:S(2)}) async-start(bf16[4,2,128,1024]{3,2,1,0:T(8,128)(2,1)} %pack_rows.3), calls=%async_computation.3 | async-start | bytes 4194304 | tf_op jit(solution)/shard_map/all_to_all | solution.py:399
  75.1 1.7 collective-permute-done.2.near_1
  76.8 0.9 collective-permute-start.7
  77.7 10.7 %collective-permute-done.3.near_2 = bf16[2,4,128,256]{3,2,1,0:T(8,128)(2,1)} collective-permute-done((bf16[2,4,128,256]{3,2,1,0:T(8,128)(2,1)}, bf16[2,4,128,256]{3,2,1,0:T(8,128)(2,1)}, u32[]{:S(2)}, u32[]{:S(2)}) %collective-permute-start.3) | collective-permute-done | bytes 524320 | tf_op jit(solution)/shard_map/ppermute | solution.py:338
  88.5 22.1 %attend.2 = (bf16[4,2,128,1024]{3,2,1,0:T(8,128)(2,1)}, f32[4,128,256]{2,1,0:T(8,128)}, f32[4,128,256]{2,1,0:T(8,128)}, bf16[2,4,128,256]{3,2,1,0:T(8,128)(2,1)}...) custom-call(s32[8,8]{1,0:T(8,128)} %bitcast.3, s32[8]{0:T(128)} %bitcast.5, s32[1]{0:T(128)} %bitcast.2.y_ref.place, ...), custom_call_target="tpu_custom_call" | custom-call | flops 30000001024 | bytes 20000000 | tf_op jit(solution)/shard_map/attend/pallas_call | solution.py:196
  110.5 9.4 %collective-permute-start.13 = (bf16[2,4,128,256]{3,2,1,0:T(8,128)(2,1)}, bf16[2,4,128,256]{3,2,1,0:T(8,128)(2,1)S(1)}, u32[]{:S(2)}, u32[]{:S(2)}) collective-permute-start(bf16[2,4,128,256]{3,2,1,0:T(8,128)(2,1)} %get-tuple-element.56), channel_id=1, source_target_pairs={{0,3},{1,0},{2,1},{3,2},{4,7},{5,4},{6,5},{7,6},{8,11},{9,8},{10,9... | collective-permute-start | bytes 1572872 | tf_op jit(solution)/shard_map/ppermute | solution.py:338
  119.9 1.0 collective-permute-start.15
  120.9 22.1 %attend.3 = (bf16[4,2,128,1024]{3,2,1,0:T(8,128)(2,1)}, f32[4,128,256]{2,1,0:T(8,128)}, f32[4,128,256]{2,1,0:T(8,128)}, bf16[2,4,128,256]{3,2,1,0:T(8,128)(2,1)}...) custom-call(s32[8,8]{1,0:T(8,128)} %bitcast.4, s32[8]{0:T(128)} %bitcast.6, s32[1]{0:T(128)} %bitcast.2.y_ref.place, ...), custom_call_target="tpu_custom_call" | custom-call | flops 30000001024 | bytes 20000000 | tf_op jit(solution)/shard_map/attend/pallas_call | solution.py:196
  143.0 5.4 %collective-permute-start.10 = (bf16[2,4,128,256]{3,2,1,0:T(8,128)(2,1)}, bf16[2,4,128,256]{3,2,1,0:T(8,128)(2,1)S(1)}, u32[]{:S(2)}, u32[]{:S(2)}) collective-permute-start(bf16[2,4,128,256]{3,2,1,0:T(8,128)(2,1)} %get-tuple-element.50), channel_id=1, source_target_pairs={{0,1},{1,2},{2,3},{3,0},{4,5},{5,6},{6,7},{7,4},{8,9},{9,10},{10,1... | collective-permute-start | bytes 1572872 | tf_op jit(solution)/shard_map/ppermute | solution.py:338
  148.4 4.3 %collective-permute-start.8 = (bf16[2,4,128,256]{3,2,1,0:T(8,128)(2,1)}, bf16[2,4,128,256]{3,2,1,0:T(8,128)(2,1)S(1)}, u32[]{:S(2)}, u32[]{:S(2)}) collective-permute-start(bf16[2,4,128,256]{3,2,1,0:T(8,128)(2,1)} %get-tuple-element.48), channel_id=1, source_target_pairs={{0,3},{1,0},{2,1},{3,2},{4,7},{5,4},{6,5},{7,6},{8,11},{9,8},{10,9... | collective-permute-start | bytes 1572872 | tf_op jit(solution)/shard_map/ppermute | solution.py:338
  152.7 1.5 collective-permute-start.9
  154.2 0.8 copy-done.6
  155.2 3.8 %add_parts.3 = (f32[4,128,256]{2,1,0:T(8,128)}, bf16[4,128,256]{2,1,0:T(8,128)(2,1)}, bf16[4,128,256]{2,1,0:T(8,128)(2,1)}) custom-call(s32[1]{0:T(128)} %bitcast.2.y_ref.place, f32[4,128,256]{2,1,0:T(8,128)} %get-tuple-element.54.own_ref, f32[4,128,256]{2,1,0:T(8,128)} %get-tuple-element.55.prev_ref, bf16[2,4,128,256]{3,2,1,0:T(8,128)(2,1)} %copy-done.5, ...), custom_call_target="tpu_custom_call" | custom-call | tf_op jit(solution)/shard_map/add_parts/pallas_call | solution.py:359
  159.0 2.4 collective-permute-start.17
  161.4 3.3 %collective-permute-done.10.refs_2_ = bf16[2,4,128,256]{3,2,1,0:T(8,128)(2,1)S(1)} collective-permute-done((bf16[2,4,128,256]{3,2,1,0:T(8,128)(2,1)}, bf16[2,4,128,256]{3,2,1,0:T(8,128)(2,1)S(1)}, u32[]{:S(2)}, u32[]{:S(2)}) %collective-permute-start.10) | collective-permute-done | bytes 524320 | tf_op jit(solution)/shard_map/ppermute | solution.py:338
  164.7 10.1 %collective-permute-done.8.refs_0_ = bf16[2,4,128,256]{3,2,1,0:T(8,128)(2,1)S(1)} collective-permute-done((bf16[2,4,128,256]{3,2,1,0:T(8,128)(2,1)}, bf16[2,4,128,256]{3,2,1,0:T(8,128)(2,1)S(1)}, u32[]{:S(2)}, u32[]{:S(2)}) %collective-permute-start.8) | collective-permute-done | bytes 524320 | tf_op jit(solution)/shard_map/ppermute | solution.py:338
  174.8 1.7 collective-permute-done.9.refs_1_
  176.5 0.8 copy-done.10
  177.3 3.8 %add_parts.2 = (f32[4,128,256]{2,1,0:T(8,128)}, bf16[4,128,256]{2,1,0:T(8,128)(2,1)}, bf16[4,128,256]{2,1,0:T(8,128)(2,1)}) custom-call(s32[1]{0:T(128)} %bitcast.2.y_ref.place, f32[4,128,256]{2,1,0:T(8,128)} %get-tuple-element.46.own_ref, f32[4,128,256]{2,1,0:T(8,128)} %get-tuple-element.47.prev_ref, bf16[2,4,128,256]{3,2,1,0:T(8,128)(2,1)} %copy-done.9, ...), custom_call_target="tpu_custom_call" | custom-call | tf_op jit(solution)/shard_map/add_parts/pallas_call | solution.py:359
  181.1 1.1 collective-permute-start.12
  182.3 5.9 %collective-permute-done.11.refs_1_ = bf16[4,128,256]{2,1,0:T(8,128)(2,1)S(1)} collective-permute-done((bf16[4,128,256]{2,1,0:T(8,128)(2,1)}, bf16[4,128,256]{2,1,0:T(8,128)(2,1)S(1)}, u32[]{:S(2)}, u32[]{:S(2)}) %collective-permute-start.11) | collective-permute-done | bytes 262176 | tf_op jit(solution)/shard_map/ppermute | solution.py:333
  188.2 3.3 %collective-permute-done.12.refs_2_ = bf16[4,128,256]{2,1,0:T(8,128)(2,1)S(1)} collective-permute-done((bf16[4,128,256]{2,1,0:T(8,128)(2,1)}, bf16[4,128,256]{2,1,0:T(8,128)(2,1)S(1)}, u32[]{:S(2)}, u32[]{:S(2)}) %collective-permute-start.12) | collective-permute-done | bytes 262176 | tf_op jit(solution)/shard_map/ppermute | solution.py:333
  191.4 0.7 copy-done.13
  192.1 3.5 %add_home.1 = bf16[4,2,128,256]{3,2,1,0:T(8,128)(2,1)} custom-call(f32[4,128,256]{2,1,0:T(8,128)} %get-tuple-element.51.refs_0_, bf16[4,128,256]{2,1,0:T(8,128)(2,1)} %copy-done.12, bf16[4,128,256]{2,1,0:T(8,128)(2,1)} %copy-done.13, f32[4,128,256]{2,1,0:T(8,128)} %get-tuple-element.59.refs_3_, bf16[4,128,256]{2,1,0:T(8,128)(2,1)} %copy-done.11, ...), custom_call_target="tpu_custom_call" | custom-call | tf_op jit(solution)/shard_map/add_home/pallas_call | solution.py:382
  195.6 14.8 %all_to_all.30.got_ref = bf16[4,2,128,256]{3,2,1,0:T(8,128)(2,1)} all-to-all(bf16[4,2,128,256]{3,2,1,0:T(8,128)(2,1)} %add_home.1), channel_id=1, replica_groups=mesh['head'=4,'blk'=64] {'head'}, dimensions={0} | all-to-all | bytes 1048576 | tf_op jit(solution)/shard_map/all_to_all | solution.py:399
  210.4 30.4 %all_to_all.31.got_ref = bf16[4,2,128,1024]{3,2,1,0:T(8,128)(2,1)} all-to-all(bf16[4,2,128,1024]{3,2,1,0:T(8,128)(2,1)S(1)} %copy-done.2), channel_id=1, replica_groups=mesh['head'=4,'blk'=64] {'head'}, dimensions={0} | all-to-all | bytes 4194304 | tf_op jit(solution)/shard_map/all_to_all | solution.py:399
  240.8 3.6 %all-to-all-start.2 = ((bf16[4,2,128,1024]{3,2,1,0:T(8,128)(2,1)}), bf16[4,2,128,1024]{3,2,1,0:T(8,128)(2,1)S(1)}, u32[]{:S(2)}, u32[]{:S(2)}) async-start(bf16[4,2,128,1024]{3,2,1,0:T(8,128)(2,1)} %get-tuple-element.37), calls=%async_computation.2 | async-start | bytes 4194304 | tf_op jit(solution)/shard_map/all_to_all | solution.py:399
  244.5 2.0 unpack_keys.1
  246.4 3.8 %unpack_rows.2 = (bf16[128,8192]{1,0:T(8,128)(2,1)}, bf16[128,8192]{1,0:T(8,128)(2,1)}) custom-call(bf16[4,2,128,1024]{3,2,1,0:T(8,128)(2,1)} %all_to_all.31.got_ref), custom_call_target="tpu_custom_call" | custom-call | tf_op jit(solution)/shard_map/unpack_rows/pallas_call | solution.py:306
  250.2 21.4 %all-to-all-done.2.got_ref = bf16[4,2,128,1024]{3,2,1,0:T(8,128)(2,1)S(1)} async-done(((bf16[4,2,128,1024]{3,2,1,0:T(8,128)(2,1)}), bf16[4,2,128,1024]{3,2,1,0:T(8,128)(2,1)S(1)}, u32[]{:S(2)}, u32[]{:S(2)}) %all-to-all-start.2) | async-done | bytes 2097184 | tf_op jit(solution)/shard_map/all_to_all | solution.py:399
  271.6 1.3 copy-done
  272.9 3.8 %unpack_rows.3 = (bf16[128,8192]{1,0:T(8,128)(2,1)}, bf16[128,8192]{1,0:T(8,128)(2,1)}) custom-call(bf16[4,2,128,1024]{3,2,1,0:T(8,128)(2,1)} %copy-done, bf16[128,8192]{1,0:T(8,128)(2,1)} %get-tuple-element.42.refs_0_, bf16[128,8192]{1,0:T(8,128)(2,1)} %get-tuple-element.43.refs_1_), custom_call_target="tpu_custom_call", output_to_operand_aliasing={{0}: (1, {}), {1}: (2, {})} | custom-call | tf_op jit(solution)/shard_map/unpack_rows/pallas_call | solution.py:306
  (42 shorter events, 0.4 us)
Async XLA Ops:
  2.5 14.6 %all-to-all-start.1 = ((bf16[4,2,128,256]{3,2,1,0:T(8,128)(2,1)}), bf16[4,2,128,256]{3,2,1,0:T(8,128)(2,1)S(1)}, u32[]{:S(2)}, u32[]{:S(2)}) async-start(bf16[4,2,128,256]{3,2,1,0:T(8,128)(2,1)} %pack_keys.1), calls=%async_computation.1 | async-start | bytes 1048576 | tf_op jit(solution)/shard_map/all_to_all | solution.py:399
  17.2 5.4 %copy-start.3 = (bf16[4,2,128,256]{3,2,1,0:T(8,128)(2,1)}, bf16[4,2,128,256]{3,2,1,0:T(8,128)(2,1)S(1)}, u32[]{:S(2)}) copy-start(bf16[4,2,128,256]{3,2,1,0:T(8,128)(2,1)S(1)} %all-to-all-done.1.own_ref.own_in) | copy-start | bytes 1572868
  17.2 53.5 %all-to-all-start = ((bf16[4,2,128,1024]{3,2,1,0:T(8,128)(2,1)}), bf16[4,2,128,1024]{3,2,1,0:T(8,128)(2,1)S(1)}, u32[]{:S(2)}, u32[]{:S(2)}) async-start(bf16[4,2,128,1024]{3,2,1,0:T(8,128)(2,1)} %pack_rows.2), calls=%async_computation | async-start | bytes 4194304 | tf_op jit(solution)/shard_map/all_to_all | solution.py:399
  20.8 34.8 %collective-permute-start = (bf16[4,2,128,256]{3,2,1,0:T(8,128)(2,1)S(1)}, bf16[4,2,128,256]{3,2,1,0:T(8,128)(2,1)S(1)}, u32[]{:S(2)}, u32[]{:S(2)}) collective-permute-start(bf16[4,2,128,256]{3,2,1,0:T(8,128)(2,1)S(1)} %all-to-all-done.1.own_ref.own_in), channel_id=1, source_target_pairs={{60,0},{61,1},{62,2},{63,3},{0,4},{1,5},{2,6},{3,7},{4,8},{5,9},{6... | collective-permute-start | bytes 1572872 | tf_op jit(solution)/shard_map/ppermute | solution.py:333
  21.5 34.1 %collective-permute-start.1 = (bf16[4,2,128,256]{3,2,1,0:T(8,128)(2,1)S(1)}, bf16[4,2,128,256]{3,2,1,0:T(8,128)(2,1)}, u32[]{:S(2)}, u32[]{:S(2)}) collective-permute-start(bf16[4,2,128,256]{3,2,1,0:T(8,128)(2,1)S(1)} %all-to-all-done.1.own_ref.own_in), channel_id=1, source_target_pairs={{56,0},{57,1},{58,2},{59,3},{60,4},{61,5},{62,6},{63,7},{0,8},{1,9... | collective-permute-start | bytes 1572872 | tf_op jit(solution)/shard_map/ppermute | solution.py:333
  55.6 0.8 copy-start.4
  59.6 17.2 %collective-permute-start.2 = (bf16[2,4,128,256]{3,2,1,0:T(8,128)(2,1)}, bf16[2,4,128,256]{3,2,1,0:T(8,128)(2,1)}, u32[]{:S(2)}, u32[]{:S(2)}) collective-permute-start(bf16[2,4,128,256]{3,2,1,0:T(8,128)(2,1)} %get-tuple-element.34), channel_id=1, source_target_pairs={{0,1},{1,2},{2,3},{3,0},{4,5},{5,6},{6,7},{7,4},{8,9},{9,10},{10,1... | collective-permute-start | bytes 1572872 | tf_op jit(solution)/shard_map/ppermute | solution.py:338
  61.2 27.3 %collective-permute-start.3 = (bf16[2,4,128,256]{3,2,1,0:T(8,128)(2,1)}, bf16[2,4,128,256]{3,2,1,0:T(8,128)(2,1)}, u32[]{:S(2)}, u32[]{:S(2)}) collective-permute-start(bf16[2,4,128,256]{3,2,1,0:T(8,128)(2,1)} %get-tuple-element.35), channel_id=1, source_target_pairs={{0,2},{1,3},{2,0},{3,1},{4,6},{5,7},{6,4},{7,5},{8,10},{9,11},{10,... | collective-permute-start | bytes 1572872 | tf_op jit(solution)/shard_map/ppermute | solution.py:338
  64.1 24.4 %collective-permute-start.4 = (bf16[2,4,128,256]{3,2,1,0:T(8,128)(2,1)}, bf16[2,4,128,256]{3,2,1,0:T(8,128)(2,1)}, u32[]{:S(2)}, u32[]{:S(2)}) collective-permute-start(bf16[2,4,128,256]{3,2,1,0:T(8,128)(2,1)} %get-tuple-element.36), channel_id=1, source_target_pairs={{0,3},{1,0},{2,1},{3,2},{4,7},{5,4},{6,5},{7,6},{8,11},{9,8},{10,9... | collective-permute-start | bytes 1572872 | tf_op jit(solution)/shard_map/ppermute | solution.py:338
  69.2 50.7 %collective-permute-start.5 = (bf16[2,4,128,256]{3,2,1,0:T(8,128)(2,1)}, bf16[2,4,128,256]{3,2,1,0:T(8,128)(2,1)S(1)}, u32[]{:S(2)}, u32[]{:S(2)}) collective-permute-start(bf16[2,4,128,256]{3,2,1,0:T(8,128)(2,1)} %get-tuple-element.38), channel_id=1, source_target_pairs={{0,1},{1,2},{2,3},{3,0},{4,5},{5,6},{6,7},{7,4},{8,9},{9,10},{10,1... | collective-permute-start | bytes 1572872 | tf_op jit(solution)/shard_map/ppermute | solution.py:338
  69.9 7.0 %copy-start.14 = (bf16[2,4,128,256]{3,2,1,0:T(8,128)(2,1)S(1)}, bf16[2,4,128,256]{3,2,1,0:T(8,128)(2,1)}, u32[]{:S(2)}) copy-start(bf16[2,4,128,256]{3,2,1,0:T(8,128)(2,1)} %get-tuple-element.40) | copy-start | bytes 1572868
  69.9 51.0 %collective-permute-start.6 = (bf16[2,4,128,256]{3,2,1,0:T(8,128)(2,1)}, bf16[2,4,128,256]{3,2,1,0:T(8,128)(2,1)}, u32[]{:S(2)}, u32[]{:S(2)}) collective-permute-start(bf16[2,4,128,256]{3,2,1,0:T(8,128)(2,1)} %get-tuple-element.39), channel_id=1, source_target_pairs={{0,2},{1,3},{2,0},{3,1},{4,6},{5,7},{6,4},{7,5},{8,10},{9,11},{10,... | collective-permute-start | bytes 1572872 | tf_op jit(solution)/shard_map/ppermute | solution.py:338
  70.7 6.2 %copy-start.1 = (bf16[4,2,128,1024]{3,2,1,0:T(8,128)(2,1)}, bf16[4,2,128,1024]{3,2,1,0:T(8,128)(2,1)S(1)}, u32[]{:S(2)}) copy-start(bf16[4,2,128,1024]{3,2,1,0:T(8,128)(2,1)S(1)} %all-to-all-done.qd_ref) | copy-start | bytes 6291460
  70.7 50.2 %all-to-all-start.3 = ((bf16[4,2,128,1024]{3,2,1,0:T(8,128)(2,1)}), bf16[4,2,128,1024]{3,2,1,0:T(8,128)(2,1)}, u32[]{:S(2)}, u32[]{:S(2)}) async-start(bf16[4,2,128,1024]{3,2,1,0:T(8,128)(2,1)} %pack_rows.3), calls=%async_computation.3 | async-start | bytes 4194304 | tf_op jit(solution)/shard_map/all_to_all | solution.py:399
  76.8 44.0 %collective-permute-start.7 = (bf16[2,4,128,256]{3,2,1,0:T(8,128)(2,1)S(1)}, bf16[2,4,128,256]{3,2,1,0:T(8,128)(2,1)}, u32[]{:S(2)}, u32[]{:S(2)}) collective-permute-start(bf16[2,4,128,256]{3,2,1,0:T(8,128)(2,1)S(1)} %copy-done.14), channel_id=1, source_target_pairs={{0,3},{1,0},{2,1},{3,2},{4,7},{5,4},{6,5},{7,6},{8,11},{9,8},{10,9... | collective-permute-start | bytes 1572872 | tf_op jit(solution)/shard_map/ppermute | solution.py:338
  110.5 42.2 %collective-permute-start.13 = (bf16[2,4,128,256]{3,2,1,0:T(8,128)(2,1)}, bf16[2,4,128,256]{3,2,1,0:T(8,128)(2,1)S(1)}, u32[]{:S(2)}, u32[]{:S(2)}) collective-permute-start(bf16[2,4,128,256]{3,2,1,0:T(8,128)(2,1)} %get-tuple-element.56), channel_id=1, source_target_pairs={{0,3},{1,0},{2,1},{3,2},{4,7},{5,4},{6,5},{7,6},{8,11},{9,8},{10,9... | collective-permute-start | bytes 1572872 | tf_op jit(solution)/shard_map/ppermute | solution.py:338
  119.9 34.2 %collective-permute-start.14 = (bf16[2,4,128,256]{3,2,1,0:T(8,128)(2,1)}, bf16[2,4,128,256]{3,2,1,0:T(8,128)(2,1)S(1)}, u32[]{:S(2)}, u32[]{:S(2)}) collective-permute-start(bf16[2,4,128,256]{3,2,1,0:T(8,128)(2,1)} %get-tuple-element.57), channel_id=1, source_target_pairs={{0,2},{1,3},{2,0},{3,1},{4,6},{5,7},{6,4},{7,5},{8,10},{9,11},{10,... | collective-permute-start | bytes 1572872 | tf_op jit(solution)/shard_map/ppermute | solution.py:338
  119.9 1.0 copy-start.15
  119.9 34.2 %collective-permute-start.15 = (bf16[2,4,128,256]{3,2,1,0:T(8,128)(2,1)}, bf16[2,4,128,256]{3,2,1,0:T(8,128)(2,1)S(1)}, u32[]{:S(2)}, u32[]{:S(2)}) collective-permute-start(bf16[2,4,128,256]{3,2,1,0:T(8,128)(2,1)} %get-tuple-element.58), channel_id=1, source_target_pairs={{0,1},{1,2},{2,3},{3,0},{4,5},{5,6},{6,7},{7,4},{8,9},{9,10},{10,1... | collective-permute-start | bytes 1572872 | tf_op jit(solution)/shard_map/ppermute | solution.py:338
  143.0 21.7 %collective-permute-start.10 = (bf16[2,4,128,256]{3,2,1,0:T(8,128)(2,1)}, bf16[2,4,128,256]{3,2,1,0:T(8,128)(2,1)S(1)}, u32[]{:S(2)}, u32[]{:S(2)}) collective-permute-start(bf16[2,4,128,256]{3,2,1,0:T(8,128)(2,1)} %get-tuple-element.50), channel_id=1, source_target_pairs={{0,1},{1,2},{2,3},{3,0},{4,5},{5,6},{6,7},{7,4},{8,9},{9,10},{10,1... | collective-permute-start | bytes 1572872 | tf_op jit(solution)/shard_map/ppermute | solution.py:338
  148.4 26.4 %collective-permute-start.8 = (bf16[2,4,128,256]{3,2,1,0:T(8,128)(2,1)}, bf16[2,4,128,256]{3,2,1,0:T(8,128)(2,1)S(1)}, u32[]{:S(2)}, u32[]{:S(2)}) collective-permute-start(bf16[2,4,128,256]{3,2,1,0:T(8,128)(2,1)} %get-tuple-element.48), channel_id=1, source_target_pairs={{0,3},{1,0},{2,1},{3,2},{4,7},{5,4},{6,5},{7,6},{8,11},{9,8},{10,9... | collective-permute-start | bytes 1572872 | tf_op jit(solution)/shard_map/ppermute | solution.py:338
  152.7 1.5 copy-start.5
  152.7 23.8 %collective-permute-start.9 = (bf16[2,4,128,256]{3,2,1,0:T(8,128)(2,1)}, bf16[2,4,128,256]{3,2,1,0:T(8,128)(2,1)S(1)}, u32[]{:S(2)}, u32[]{:S(2)}) collective-permute-start(bf16[2,4,128,256]{3,2,1,0:T(8,128)(2,1)} %get-tuple-element.49), channel_id=1, source_target_pairs={{0,2},{1,3},{2,0},{3,1},{4,6},{5,7},{6,4},{7,5},{8,10},{9,11},{10,... | collective-permute-start | bytes 1572872 | tf_op jit(solution)/shard_map/ppermute | solution.py:338
  154.1 0.8 copy-start.6
  154.2 1.0 copy-start.7
  159.0 23.3 %collective-permute-start.16 = (bf16[4,128,256]{2,1,0:T(8,128)(2,1)}, bf16[4,128,256]{2,1,0:T(8,128)(2,1)S(1)}, u32[]{:S(2)}, u32[]{:S(2)}) collective-permute-start(bf16[4,128,256]{2,1,0:T(8,128)(2,1)} %get-tuple-element.60), channel_id=1, source_target_pairs={{4,0},{5,1},{6,2},{7,3},{8,4},{9,5},{10,6},{11,7},{12,8},{13,9},{1... | collective-permute-start | bytes 786440 | tf_op jit(solution)/shard_map/ppermute | solution.py:333
  159.0 23.3 %collective-permute-start.17 = (bf16[4,128,256]{2,1,0:T(8,128)(2,1)}, bf16[4,128,256]{2,1,0:T(8,128)(2,1)}, u32[]{:S(2)}, u32[]{:S(2)}) collective-permute-start(bf16[4,128,256]{2,1,0:T(8,128)(2,1)} %get-tuple-element.61), channel_id=1, source_target_pairs={{8,0},{9,1},{10,2},{11,3},{12,4},{13,5},{14,6},{15,7},{16,8},{17,9... | collective-permute-start | bytes 786440 | tf_op jit(solution)/shard_map/ppermute | solution.py:333
  164.7 11.8 %copy-start.8 = (bf16[2,4,128,256]{3,2,1,0:T(8,128)(2,1)}, bf16[2,4,128,256]{3,2,1,0:T(8,128)(2,1)S(1)}, u32[]{:S(2)}) copy-start(bf16[2,4,128,256]{3,2,1,0:T(8,128)(2,1)S(1)} %collective-permute-done.10.refs_2_) | copy-start | bytes 1572868
  174.8 1.7 copy-start.9
  176.5 0.8 copy-start.10
  181.1 29.4 %copy-start.2 = (bf16[4,2,128,1024]{3,2,1,0:T(8,128)(2,1)S(1)}, bf16[4,2,128,1024]{3,2,1,0:T(8,128)(2,1)}, u32[]{:S(2)}) copy-start(bf16[4,2,128,1024]{3,2,1,0:T(8,128)(2,1)} %get-tuple-element.41) | copy-start | bytes 6291460
  181.1 7.1 %collective-permute-start.11 = (bf16[4,128,256]{2,1,0:T(8,128)(2,1)}, bf16[4,128,256]{2,1,0:T(8,128)(2,1)S(1)}, u32[]{:S(2)}, u32[]{:S(2)}) collective-permute-start(bf16[4,128,256]{2,1,0:T(8,128)(2,1)} %get-tuple-element.52), channel_id=1, source_target_pairs={{4,0},{5,1},{6,2},{7,3},{8,4},{9,5},{10,6},{11,7},{12,8},{13,9},{1... | collective-permute-start | bytes 786440 | tf_op jit(solution)/shard_map/ppermute | solution.py:333
  181.1 10.3 %collective-permute-start.12 = (bf16[4,128,256]{2,1,0:T(8,128)(2,1)}, bf16[4,128,256]{2,1,0:T(8,128)(2,1)S(1)}, u32[]{:S(2)}, u32[]{:S(2)}) collective-permute-start(bf16[4,128,256]{2,1,0:T(8,128)(2,1)} %get-tuple-element.53), channel_id=1, source_target_pairs={{8,0},{9,1},{10,2},{11,3},{12,4},{13,5},{14,6},{15,7},{16,8},{17,9... | collective-permute-start | bytes 786440 | tf_op jit(solution)/shard_map/ppermute | solution.py:333
  182.3 9.2 %copy-start.11 = (bf16[4,128,256]{2,1,0:T(8,128)(2,1)}, bf16[4,128,256]{2,1,0:T(8,128)(2,1)S(1)}, u32[]{:S(2)}) copy-start(bf16[4,128,256]{2,1,0:T(8,128)(2,1)S(1)} %collective-permute-done.16.refs_4_) | copy-start | bytes 786436
  188.2 3.3 %copy-start.12 = (bf16[4,128,256]{2,1,0:T(8,128)(2,1)}, bf16[4,128,256]{2,1,0:T(8,128)(2,1)S(1)}, u32[]{:S(2)}) copy-start(bf16[4,128,256]{2,1,0:T(8,128)(2,1)S(1)} %collective-permute-done.11.refs_1_) | copy-start | bytes 786436
  191.4 0.7 copy-start.13
  240.8 30.8 %all-to-all-start.2 = ((bf16[4,2,128,1024]{3,2,1,0:T(8,128)(2,1)}), bf16[4,2,128,1024]{3,2,1,0:T(8,128)(2,1)S(1)}, u32[]{:S(2)}, u32[]{:S(2)}) async-start(bf16[4,2,128,1024]{3,2,1,0:T(8,128)(2,1)} %get-tuple-element.37), calls=%async_computation.2 | async-start | bytes 4194304 | tf_op jit(solution)/shard_map/all_to_all | solution.py:399
  271.6 1.3 copy-start

commit v3 on v2

--- a/solution.py
+++ b/solution.py
@@ -188,8 +188,7 @@
                     ref[m, c, :, right] = dkv[at, right].astype(BF16).T
 
 
-def attend_call(j, codes, counts, place, qd, own, prev, near):
-    mine = pl.BlockSpec((NB, None, BLOCK, 2 * HEAD_SIZE), lambda t, *_: (0, j, 0, 0))
+def attend_call(codes, counts, place, qd, own, prev, near):
     whole = pl.BlockSpec((2, NB, BLOCK, 2 * HEAD_SIZE), lambda t, *_: (0, 0, 0, 0))
     flat = pl.BlockSpec((NB, BLOCK, 2 * HEAD_SIZE), lambda t, *_: (0, 0, 0))
     block = pl.BlockSpec((None, 2, BLOCK, WIDE), lambda t, *_: (t, 0, 0, 0))
@@ -199,7 +198,7 @@
         grid_spec=pltpu.PrefetchScalarGridSpec(
             num_scalar_prefetch=3,
             grid=(NB,),
-            in_specs=[block, mine, mine, whole, whole, whole],
+            in_specs=[block, flat, flat, whole, whole, whole],
             out_specs=[block, flat, flat, whole, whole, whole],
             scratch_shapes=[
                 pltpu.SMEM((NB, MOST + 8), jnp.int32),
@@ -224,9 +223,7 @@
         ]
         + [jax.ShapeDtypeStruct((2, NB, BLOCK, 2 * HEAD_SIZE), BF16)] * 3,
         cost_estimate=pl.CostEstimate(flops=30_000_000_000, bytes_accessed=20_000_000, transcendentals=70_000_000),
-        compiler_params=pltpu.CompilerParams(
-            dimension_semantics=("arbitrary",), vmem_limit_bytes=58 * 1024 * 1024
-        ),
+        compiler_params=pltpu.CompilerParams(dimension_semantics=("arbitrary",), vmem_limit_bytes=58 * 1024 * 1024),
     )(codes, counts, place, qd, own, prev, *near)
 
 
@@ -267,30 +264,26 @@
 
 def pack_window(place, own, prev, back):
     def kernel(y_ref, own_ref, prev_ref, back_ref, *out_refs):
-        for d in range(1, QUAD):
-            for j in range(2):
-                out = out_refs[2 * (d - 1) + j]
-                out[0] = prev_ref[:, j]
-                pick = y_ref[0] + d < QUAD
-
-                @pl.when(pick)
-                def _(out=out, j=j):
-                    out[1] = own_ref[:, j]
-
-                @pl.when(jnp.logical_not(pick))
-                def _(out=out, j=j):
-                    out[1] = back_ref[:, j]
-
-    shape = (2,) + own.shape[:1] + own.shape[2:]
+        for d, out in enumerate(out_refs, 1):
+            out[0] = prev_ref[...]
+            pick = y_ref[0] + d < QUAD
+
+            @pl.when(pick)
+            def _(out=out):
+                out[1] = own_ref[...]
+
+            @pl.when(jnp.logical_not(pick))
+            def _(out=out):
+                out[1] = back_ref[...]
+
     vmem = pl.BlockSpec(memory_space=pltpu.VMEM)
-    outs = pl.pallas_call(
+    return pl.pallas_call(
         kernel,
         name="pack_window",
         in_specs=[pl.BlockSpec(memory_space=pltpu.SMEM), vmem, vmem, vmem],
-        out_specs=[vmem] * 6,
-        out_shape=[jax.ShapeDtypeStruct(shape, BF16)] * 6,
+        out_specs=[vmem] * 3,
+        out_shape=[jax.ShapeDtypeStruct((2,) + own.shape, BF16)] * 3,
     )(place, own, prev, back)
-    return [outs[j::2] for j in range(2)]
 
 
 def unpack_rows(j, got, filled):
@@ -403,17 +396,21 @@
     y = lax.axis_index("blk") % QUAD
     place = jnp.full((1,), y, jnp.int32)
     codes, counts = pair_codes[0], pair_counts[0]
-    own = swap(pack_keys(key, value))
-    prev, back = shifted(own, QUAD), shifted(own, 2 * QUAD)
-    sends = pack_window(place, own, prev, back)
-    near, rows = [], []
+    keys = swap(pack_keys(key, value))
+    packed = []
     for j in range(2):
-        near.append([turned_in_quad(sends[j][d - 1], d) for d in range(1, QUAD)])
-        packed = pack_rows(j, query, output_gradient)
-        rows.append(swap(packed))
+        packed.append(pack_rows(j, query, output_gradient))
+    own, prev, near, rows = [], [], [], []
+    for j in range(2):
+        own.append(keys[:, j])
+        prev.append(shifted(own[j], QUAD))
+        back = shifted(own[j], 2 * QUAD)
+        sends = pack_window(place, own[j], prev[j], back)
+        near.append([turned_in_quad(sends[d - 1], d) for d in range(1, QUAD)])
+        rows.append(swap(packed[j]))
     filled, sums = None, []
     for j in range(2):
-        both, own_sum, prev_sum, *parts = attend_call(j, codes, counts, place, rows[j], own, prev, near[j])
+        both, own_sum, prev_sum, *parts = attend_call(codes, counts, place, rows[j], own[j], prev[j], near[j])
         got = swap(both)
         filled = unpack_rows(j, got, filled)
         sums += gathered(place, own_sum, prev_sum, parts)

time: 282 us -> 282 us (level)
  the two profiles are of different devices: /device:TPU:192 before, /device:TPU:96 now
where the time goes in v3:
time: 282 us; the launch traced here: 281 us
  Pallas kernels  92.9 us (33%)
  waiting for transfers between devices  91.8 us (33%)
  blocking collectives  45.2 us (16%)
  starting transfers between devices  44.2 us (16%)
  local copies, waits for them, and re-layouts  6.08 us (2%)
    pallas_call x2, Pallas kernels, attend_call(): pl.pallas_call(attend, name='attend', grid_spec=pltpu.PrefetchScalarGridS...  58.1 us
    ppermute x8, waiting for transfers between devices, shifted(): return lax.ppermute(x, 'blk', [((i - distance) % n, i) for i in range(n)])  47.7 us
    all_to_all x2, blocking collectives, swap(): return lax.all_to_all(x, 'head', split_axis=0, concat_axis=0, tiled=True)  45.2 us
    all_to_all x4, waiting for transfers between devices, swap(): return lax.all_to_all(x, 'head', split_axis=0, concat_axis=0, tiled=True)  28 us
    ppermute x12, waiting for transfers between devices, turned_in_quad(): lax.ppermute(x, 'blk', [(i, i - i % QUAD + (i + d) % QUAD) for i in range...  16.2 us
    all_to_all x4, starting transfers between devices, swap(): return lax.all_to_all(x, 'head', split_axis=0, concat_axis=0, tiled=True)  16 us
    ppermute x8, starting transfers between devices, shifted(): return lax.ppermute(x, 'blk', [((i - distance) % n, i) for i in range(n)])  14.8 us
    ppermute x12, starting transfers between devices, turned_in_quad(): lax.ppermute(x, 'blk', [(i, i - i % QUAD + (i + d) % QUAD) for i in range...  13.4 us
  transfers between devices with their start and end apart: 24, of which 10 were waited for; matrix products, arithmetic and copies ran while one was open for 0% of the time, Pallas kernels for 30%

profile of v3, /device:TPU:96, one launch (start us, length us, event | category | flops | bytes accessed | tf_op | source)
XLA Modules:
  0.0 281.1 jit_solution(6279228471149696227)
XLA Ops:
  0.6 1.9 pack_keys.1
  2.5 4.3 %all-to-all-start.1 = ((bf16[4,2,128,256]{3,2,1,0:T(8,128)(2,1)}), bf16[4,2,128,256]{3,2,1,0:T(8,128)(2,1)S(1)}, u32[]{:S(2)}, u32[]{:S(2)}) async-start(bf16[4,2,128,256]{3,2,1,0:T(8,128)(2,1)} %pack_keys.1), calls=%async_computation.1 | async-start | bytes 1048576 | tf_op jit(solution)/shard_map/all_to_all | solution.py:392
  6.8 3.8 %pack_rows.3 = bf16[4,2,128,1024]{3,2,1,0:T(8,128)(2,1)} custom-call(bf16[128,8192]{1,0:T(8,128)(2,1)} %q_ref.3, bf16[128,8192]{1,0:T(8,128)(2,1)} %g_ref.3), custom_call_target="tpu_custom_call" | custom-call | tf_op jit(solution)/shard_map/pack_rows/pallas_call | solution.py:238
  10.6 6.6 %all-to-all-done.1 = bf16[4,2,128,256]{3,2,1,0:T(8,128)(2,1)S(1)} async-done(((bf16[4,2,128,256]{3,2,1,0:T(8,128)(2,1)}), bf16[4,2,128,256]{3,2,1,0:T(8,128)(2,1)S(1)}, u32[]{:S(2)}, u32[]{:S(2)}) %all-to-all-start.1) | async-done | bytes 524320 | tf_op jit(solution)/shard_map/all_to_all | solution.py:392
  17.2 3.6 %all-to-all-start.3 = ((bf16[4,2,128,1024]{3,2,1,0:T(8,128)(2,1)}), bf16[4,2,128,1024]{3,2,1,0:T(8,128)(2,1)S(1)}, u32[]{:S(2)}, u32[]{:S(2)}) async-start(bf16[4,2,128,1024]{3,2,1,0:T(8,128)(2,1)} %pack_rows.3), calls=%async_computation.3 | async-start | bytes 4194304 | tf_op jit(solution)/shard_map/all_to_all | solution.py:392
  20.8 3.2 %collective-permute-start.6 = (bf16[4,128,256]{2,1,0:T(8,128)(2,1)S(1)}, bf16[4,128,256]{2,1,0:T(8,128)(2,1)S(1)}, u32[]{:S(2)}, u32[]{:S(2)}) collective-permute-start(bf16[4,128,256]{2,1,0:T(8,128)(2,1)S(1)} %get-tuple-element.64.own_ref.own_in), channel_id=1, source_target_pairs={{56,0},{57,1},{58,2},{59,3},{60,4},{61,5},{62,6},{63,7},{0,8},{1,9... | collective-permute-start | bytes 786440 | tf_op jit(solution)/shard_map/ppermute | solution.py:326
  24.7 5.5 %collective-permute-done.6.back_ref = bf16[4,128,256]{2,1,0:T(8,128)(2,1)S(1)} collective-permute-done((bf16[4,128,256]{2,1,0:T(8,128)(2,1)S(1)}, bf16[4,128,256]{2,1,0:T(8,128)(2,1)S(1)}, u32[]{:S(2)}, u32[]{:S(2)}) %collective-permute-start.6) | collective-permute-done | bytes 262176 | tf_op jit(solution)/shard_map/ppermute | solution.py:326
  30.2 19.7 %collective-permute-done.5.prev_ref.prev_in = bf16[4,128,256]{2,1,0:T(8,128)(2,1)S(1)} collective-permute-done((bf16[4,128,256]{2,1,0:T(8,128)(2,1)S(1)}, bf16[4,128,256]{2,1,0:T(8,128)(2,1)S(1)}, u32[]{:S(2)}, u32[]{:S(2)}) %collective-permute-start.5) | collective-permute-done | bytes 262176 | tf_op jit(solution)/shard_map/ppermute | solution.py:326
  50.6 2.4 pack_window.3
  53.0 1.6 collective-permute-start.7
  54.6 2.9 %collective-permute-start.8 = (bf16[2,4,128,256]{3,2,1,0:T(8,128)(2,1)}, bf16[2,4,128,256]{3,2,1,0:T(8,128)(2,1)}, u32[]{:S(2)}, u32[]{:S(2)}) collective-permute-start(bf16[2,4,128,256]{3,2,1,0:T(8,128)(2,1)} %get-tuple-element.39), channel_id=1, source_target_pairs={{0,2},{1,3},{2,0},{3,1},{4,6},{5,7},{6,4},{7,5},{8,10},{9,11},{10,... | collective-permute-start | bytes 1572872 | tf_op jit(solution)/shard_map/ppermute | solution.py:331
  57.5 1.4 collective-permute-start.9
  58.8 3.1 %collective-permute-start.1 = (bf16[4,128,256]{2,1,0:T(8,128)(2,1)S(1)}, bf16[4,128,256]{2,1,0:T(8,128)(2,1)S(1)}, u32[]{:S(2)}, u32[]{:S(2)}) collective-permute-start(bf16[4,128,256]{2,1,0:T(8,128)(2,1)S(1)} %get-tuple-element.65.own_ref.own_in), channel_id=1, source_target_pairs={{56,0},{57,1},{58,2},{59,3},{60,4},{61,5},{62,6},{63,7},{0,8},{1,9... | collective-permute-start | bytes 786440 | tf_op jit(solution)/shard_map/ppermute | solution.py:326
  62.0 2.5 collective-permute-start
  64.5 3.8 %pack_rows.2 = bf16[4,2,128,1024]{3,2,1,0:T(8,128)(2,1)} custom-call(bf16[128,8192]{1,0:T(8,128)(2,1)} %q_ref.3, bf16[128,8192]{1,0:T(8,128)(2,1)} %g_ref.3), custom_call_target="tpu_custom_call" | custom-call | tf_op jit(solution)/shard_map/pack_rows/pallas_call | solution.py:238
  68.2 5.4 %collective-permute-done.prev_ref.prev_in = bf16[4,128,256]{2,1,0:T(8,128)(2,1)S(1)} collective-permute-done((bf16[4,128,256]{2,1,0:T(8,128)(2,1)S(1)}, bf16[4,128,256]{2,1,0:T(8,128)(2,1)S(1)}, u32[]{:S(2)}, u32[]{:S(2)}) %collective-permute-start) | collective-permute-done | bytes 262176 | tf_op jit(solution)/shard_map/ppermute | solution.py:326
  73.7 0.7 copy-done.15
  74.4 2.4 pack_window.2
  77.4 1.1 collective-permute-start.3
  78.5 4.5 %all-to-all-start = ((bf16[4,2,128,1024]{3,2,1,0:T(8,128)(2,1)}), bf16[4,2,128,1024]{3,2,1,0:T(8,128)(2,1)}, u32[]{:S(2)}, u32[]{:S(2)}) async-start(bf16[4,2,128,1024]{3,2,1,0:T(8,128)(2,1)} %pack_rows.2), calls=%async_computation | async-start | bytes 4194304 | tf_op jit(solution)/shard_map/all_to_all | solution.py:392
  83.0 1.7 collective-permute-start.4
  84.7 29.0 %attend.3 = (bf16[4,2,128,1024]{3,2,1,0:T(8,128)(2,1)}, f32[4,128,256]{2,1,0:T(8,128)}, f32[4,128,256]{2,1,0:T(8,128)}, bf16[2,4,128,256]{3,2,1,0:T(8,128)(2,1)}...) custom-call(s32[8,8]{1,0:T(8,128)} %bitcast.11, s32[8]{0:T(128)} %bitcast.13, s32[1]{0:T(128)} %bitcast.2.y_ref.place, ...), custom_call_target="tpu_custom_call" | custom-call | flops 30000001024 | bytes 20000000 | tf_op jit(solution)/shard_map/attend/pallas_call | solution.py:195
  114.1 1.8 collective-permute-start.12
  115.9 0.8 copy-done.19
  116.7 29.1 %attend.2 = (bf16[4,2,128,1024]{3,2,1,0:T(8,128)(2,1)}, f32[4,128,256]{2,1,0:T(8,128)}, f32[4,128,256]{2,1,0:T(8,128)}, bf16[2,4,128,256]{3,2,1,0:T(8,128)(2,1)}...) custom-call(s32[8,8]{1,0:T(8,128)} %bitcast.12, s32[8]{0:T(128)} %bitcast.14, s32[1]{0:T(128)} %bitcast.2.y_ref.place, ...), custom_call_target="tpu_custom_call" | custom-call | flops 30000001024 | bytes 20000000 | tf_op jit(solution)/shard_map/attend/pallas_call | solution.py:195
  145.8 0.9 collective-permute-start.16
  146.7 1.2 collective-permute-start.17
  147.9 0.8 copy-done.6
  148.9 3.8 %add_parts.2 = (f32[4,128,256]{2,1,0:T(8,128)}, bf16[4,128,256]{2,1,0:T(8,128)(2,1)}, bf16[4,128,256]{2,1,0:T(8,128)(2,1)}) custom-call(s32[1]{0:T(128)} %bitcast.2.y_ref.place, f32[4,128,256]{2,1,0:T(8,128)} %get-tuple-element.46.own_ref, f32[4,128,256]{2,1,0:T(8,128)} %get-tuple-element.47.prev_ref, bf16[2,4,128,256]{3,2,1,0:T(8,128)(2,1)} %copy-done.5, ...), custom_call_target="tpu_custom_call" | custom-call | tf_op jit(solution)/shard_map/add_parts/pallas_call | solution.py:352
  152.7 3.3 %collective-permute-start.13 = (bf16[4,128,256]{2,1,0:T(8,128)(2,1)}, bf16[4,128,256]{2,1,0:T(8,128)(2,1)S(1)}, u32[]{:S(2)}, u32[]{:S(2)}) collective-permute-start(bf16[4,128,256]{2,1,0:T(8,128)(2,1)} %get-tuple-element.52), channel_id=1, source_target_pairs={{4,0},{5,1},{6,2},{7,3},{8,4},{9,5},{10,6},{11,7},{12,8},{13,9},{1... | collective-permute-start | bytes 786440 | tf_op jit(solution)/shard_map/ppermute | solution.py:326
  156.0 4.8 %collective-permute-done.15.refs_0_ = bf16[2,4,128,256]{3,2,1,0:T(8,128)(2,1)S(1)} collective-permute-done((bf16[2,4,128,256]{3,2,1,0:T(8,128)(2,1)}, bf16[2,4,128,256]{3,2,1,0:T(8,128)(2,1)S(1)}, u32[]{:S(2)}, u32[]{:S(2)}) %collective-permute-start.15) | collective-permute-done | bytes 524320 | tf_op jit(solution)/shard_map/ppermute | solution.py:331
  160.8 1.6 collective-permute-done.16.refs_1_
  162.4 9.7 %collective-permute-done.17.refs_2_ = bf16[2,4,128,256]{3,2,1,0:T(8,128)(2,1)S(1)} collective-permute-done((bf16[2,4,128,256]{3,2,1,0:T(8,128)(2,1)}, bf16[2,4,128,256]{3,2,1,0:T(8,128)(2,1)S(1)}, u32[]{:S(2)}, u32[]{:S(2)}) %collective-permute-start.17) | collective-permute-done | bytes 524320 | tf_op jit(solution)/shard_map/ppermute | solution.py:331
  172.2 0.8 copy-done.10
  173.0 3.8 %add_parts.3 = (f32[4,128,256]{2,1,0:T(8,128)}, bf16[4,128,256]{2,1,0:T(8,128)(2,1)}, bf16[4,128,256]{2,1,0:T(8,128)(2,1)}) custom-call(s32[1]{0:T(128)} %bitcast.2.y_ref.place, f32[4,128,256]{2,1,0:T(8,128)} %get-tuple-element.54.own_ref, f32[4,128,256]{2,1,0:T(8,128)} %get-tuple-element.55.prev_ref, bf16[2,4,128,256]{3,2,1,0:T(8,128)(2,1)} %copy-done.8, ...), custom_call_target="tpu_custom_call" | custom-call | tf_op jit(solution)/shard_map/add_parts/pallas_call | solution.py:352
  176.8 1.9 collective-permute-start.18
  178.8 6.9 %collective-permute-done.18.refs_4_ = bf16[4,128,256]{2,1,0:T(8,128)(2,1)S(1)} collective-permute-done((bf16[4,128,256]{2,1,0:T(8,128)(2,1)}, bf16[4,128,256]{2,1,0:T(8,128)(2,1)S(1)}, u32[]{:S(2)}, u32[]{:S(2)}) %collective-permute-start.18) | collective-permute-done | bytes 262176 | tf_op jit(solution)/shard_map/ppermute | solution.py:326
  185.7 10.1 %collective-permute-done.19.refs_5_ = bf16[4,128,256]{2,1,0:T(8,128)(2,1)S(1)} collective-permute-done((bf16[4,128,256]{2,1,0:T(8,128)(2,1)}, bf16[4,128,256]{2,1,0:T(8,128)(2,1)S(1)}, u32[]{:S(2)}, u32[]{:S(2)}) %collective-permute-start.19) | collective-permute-done | bytes 262176 | tf_op jit(solution)/shard_map/ppermute | solution.py:326
  195.8 0.7 copy-done.13
  196.5 3.5 %add_home.1 = bf16[4,2,128,256]{3,2,1,0:T(8,128)(2,1)} custom-call(f32[4,128,256]{2,1,0:T(8,128)} %get-tuple-element.51.refs_0_, bf16[4,128,256]{2,1,0:T(8,128)(2,1)} %copy-done.11, bf16[4,128,256]{2,1,0:T(8,128)(2,1)} %collective-permute-done.14.refs_2_, f32[4,128,256]{2,1,0:T(8,128)} %get-tuple-element.59.refs_3_, bf16[4,128,256]{2,1,0:T(8,128)(2,1)} %copy-done.12, ...), custom_call_target="tpu_custom_call" | custom-call | tf_op jit(solution)/shard_map/add_home/pallas_call | solution.py:375
  200.0 14.8 %all_to_all.30.got_ref = bf16[4,2,128,256]{3,2,1,0:T(8,128)(2,1)} all-to-all(bf16[4,2,128,256]{3,2,1,0:T(8,128)(2,1)} %add_home.1), channel_id=1, replica_groups=mesh['head'=4,'blk'=64] {'head'}, dimensions={0} | all-to-all | bytes 1048576 | tf_op jit(solution)/shard_map/all_to_all | solution.py:392
  214.8 30.4 %all_to_all.31.got_ref = bf16[4,2,128,1024]{3,2,1,0:T(8,128)(2,1)} all-to-all(bf16[4,2,128,1024]{3,2,1,0:T(8,128)(2,1)S(1)} %copy-done.1), channel_id=1, replica_groups=mesh['head'=4,'blk'=64] {'head'}, dimensions={0} | all-to-all | bytes 4194304 | tf_op jit(solution)/shard_map/all_to_all | solution.py:392
  245.2 3.6 %all-to-all-start.2 = ((bf16[4,2,128,1024]{3,2,1,0:T(8,128)(2,1)}), bf16[4,2,128,1024]{3,2,1,0:T(8,128)(2,1)S(1)}, u32[]{:S(2)}, u32[]{:S(2)}) async-start(bf16[4,2,128,1024]{3,2,1,0:T(8,128)(2,1)} %get-tuple-element.37), calls=%async_computation.2 | async-start | bytes 4194304 | tf_op jit(solution)/shard_map/all_to_all | solution.py:392
  248.9 2.0 unpack_keys.1
  250.8 3.8 %unpack_rows.2 = (bf16[128,8192]{1,0:T(8,128)(2,1)}, bf16[128,8192]{1,0:T(8,128)(2,1)}) custom-call(bf16[4,2,128,1024]{3,2,1,0:T(8,128)(2,1)} %all_to_all.31.got_ref), custom_call_target="tpu_custom_call" | custom-call | tf_op jit(solution)/shard_map/unpack_rows/pallas_call | solution.py:299
  254.6 21.4 %all-to-all-done.2.got_ref = bf16[4,2,128,1024]{3,2,1,0:T(8,128)(2,1)S(1)} async-done(((bf16[4,2,128,1024]{3,2,1,0:T(8,128)(2,1)}), bf16[4,2,128,1024]{3,2,1,0:T(8,128)(2,1)S(1)}, u32[]{:S(2)}, u32[]{:S(2)}) %all-to-all-start.2) | async-done | bytes 2097184 | tf_op jit(solution)/shard_map/all_to_all | solution.py:392
  276.0 1.3 copy-done
  277.3 3.8 %unpack_rows.3 = (bf16[128,8192]{1,0:T(8,128)(2,1)}, bf16[128,8192]{1,0:T(8,128)(2,1)}) custom-call(bf16[4,2,128,1024]{3,2,1,0:T(8,128)(2,1)} %copy-done, bf16[128,8192]{1,0:T(8,128)(2,1)} %get-tuple-element.42.refs_0_, bf16[128,8192]{1,0:T(8,128)(2,1)} %get-tuple-element.43.refs_1_), custom_call_target="tpu_custom_call", output_to_operand_aliasing={{0}: (1, {}), {1}: (2, {})} | custom-call | tf_op jit(solution)/shard_map/unpack_rows/pallas_call | solution.py:299
  (56 shorter events, 2.7 us)
Async XLA Ops:
  2.5 14.6 %all-to-all-start.1 = ((bf16[4,2,128,256]{3,2,1,0:T(8,128)(2,1)}), bf16[4,2,128,256]{3,2,1,0:T(8,128)(2,1)S(1)}, u32[]{:S(2)}, u32[]{:S(2)}) async-start(bf16[4,2,128,256]{3,2,1,0:T(8,128)(2,1)} %pack_keys.1), calls=%async_computation.1 | async-start | bytes 1048576 | tf_op jit(solution)/shard_map/all_to_all | solution.py:392
  17.2 61.4 %all-to-all-start.3 = ((bf16[4,2,128,1024]{3,2,1,0:T(8,128)(2,1)}), bf16[4,2,128,1024]{3,2,1,0:T(8,128)(2,1)S(1)}, u32[]{:S(2)}, u32[]{:S(2)}) async-start(bf16[4,2,128,1024]{3,2,1,0:T(8,128)(2,1)} %pack_rows.3), calls=%async_computation.3 | async-start | bytes 4194304 | tf_op jit(solution)/shard_map/all_to_all | solution.py:392
  20.8 29.1 %copy-start.4 = (bf16[4,128,256]{2,1,0:T(8,128)(2,1)}, bf16[4,128,256]{2,1,0:T(8,128)(2,1)S(1)}, u32[]{:S(2)}) copy-start(bf16[4,128,256]{2,1,0:T(8,128)(2,1)S(1)} %get-tuple-element.64.own_ref.own_in) | copy-start | bytes 786436
  20.8 47.4 %copy-start.3 = (bf16[4,128,256]{2,1,0:T(8,128)(2,1)}, bf16[4,128,256]{2,1,0:T(8,128)(2,1)S(1)}, u32[]{:S(2)}) copy-start(bf16[4,128,256]{2,1,0:T(8,128)(2,1)S(1)} %get-tuple-element.65.own_ref.own_in) | copy-start | bytes 786436
  20.8 9.4 %collective-permute-start.6 = (bf16[4,128,256]{2,1,0:T(8,128)(2,1)S(1)}, bf16[4,128,256]{2,1,0:T(8,128)(2,1)S(1)}, u32[]{:S(2)}, u32[]{:S(2)}) collective-permute-start(bf16[4,128,256]{2,1,0:T(8,128)(2,1)S(1)} %get-tuple-element.64.own_ref.own_in), channel_id=1, source_target_pairs={{56,0},{57,1},{58,2},{59,3},{60,4},{61,5},{62,6},{63,7},{0,8},{1,9... | collective-permute-start | bytes 786440 | tf_op jit(solution)/shard_map/ppermute | solution.py:326
  24.0 25.9 %collective-permute-start.5 = (bf16[4,128,256]{2,1,0:T(8,128)(2,1)S(1)}, bf16[4,128,256]{2,1,0:T(8,128)(2,1)S(1)}, u32[]{:S(2)}, u32[]{:S(2)}) collective-permute-start(bf16[4,128,256]{2,1,0:T(8,128)(2,1)S(1)} %get-tuple-element.64.own_ref.own_in), channel_id=1, source_target_pairs={{60,0},{61,1},{62,2},{63,3},{0,4},{1,5},{2,6},{3,7},{4,8},{5,9},{6... | collective-permute-start | bytes 786440 | tf_op jit(solution)/shard_map/ppermute | solution.py:326
  30.2 19.7 %copy-start.16 = (bf16[4,128,256]{2,1,0:T(8,128)(2,1)}, bf16[4,128,256]{2,1,0:T(8,128)(2,1)S(1)}, u32[]{:S(2)}) copy-start(bf16[4,128,256]{2,1,0:T(8,128)(2,1)S(1)} %collective-permute-done.6.back_ref) | copy-start | bytes 786436
  49.9 0.7 copy-start.14
  53.0 30.0 %collective-permute-start.7 = (bf16[2,4,128,256]{3,2,1,0:T(8,128)(2,1)}, bf16[2,4,128,256]{3,2,1,0:T(8,128)(2,1)}, u32[]{:S(2)}, u32[]{:S(2)}) collective-permute-start(bf16[2,4,128,256]{3,2,1,0:T(8,128)(2,1)} %get-tuple-element.38), channel_id=1, source_target_pairs={{0,1},{1,2},{2,3},{3,0},{4,5},{5,6},{6,7},{7,4},{8,9},{9,10},{10,1... | collective-permute-start | bytes 1572872 | tf_op jit(solution)/shard_map/ppermute | solution.py:331
  54.6 30.1 %collective-permute-start.8 = (bf16[2,4,128,256]{3,2,1,0:T(8,128)(2,1)}, bf16[2,4,128,256]{3,2,1,0:T(8,128)(2,1)}, u32[]{:S(2)}, u32[]{:S(2)}) collective-permute-start(bf16[2,4,128,256]{3,2,1,0:T(8,128)(2,1)} %get-tuple-element.39), channel_id=1, source_target_pairs={{0,2},{1,3},{2,0},{3,1},{4,6},{5,7},{6,4},{7,5},{8,10},{9,11},{10,... | collective-permute-start | bytes 1572872 | tf_op jit(solution)/shard_map/ppermute | solution.py:331
  57.5 27.2 %collective-permute-start.9 = (bf16[2,4,128,256]{3,2,1,0:T(8,128)(2,1)}, bf16[2,4,128,256]{3,2,1,0:T(8,128)(2,1)}, u32[]{:S(2)}, u32[]{:S(2)}) collective-permute-start(bf16[2,4,128,256]{3,2,1,0:T(8,128)(2,1)} %get-tuple-element.40), channel_id=1, source_target_pairs={{0,3},{1,0},{2,1},{3,2},{4,7},{5,4},{6,5},{7,6},{8,11},{9,8},{10,9... | collective-permute-start | bytes 1572872 | tf_op jit(solution)/shard_map/ppermute | solution.py:331
  58.8 9.4 %collective-permute-start.1 = (bf16[4,128,256]{2,1,0:T(8,128)(2,1)S(1)}, bf16[4,128,256]{2,1,0:T(8,128)(2,1)S(1)}, u32[]{:S(2)}, u32[]{:S(2)}) collective-permute-start(bf16[4,128,256]{2,1,0:T(8,128)(2,1)S(1)} %get-tuple-element.65.own_ref.own_in), channel_id=1, source_target_pairs={{56,0},{57,1},{58,2},{59,3},{60,4},{61,5},{62,6},{63,7},{0,8},{1,9... | collective-permute-start | bytes 786440 | tf_op jit(solution)/shard_map/ppermute | solution.py:326
  62.0 11.7 %collective-permute-start = (bf16[4,128,256]{2,1,0:T(8,128)(2,1)S(1)}, bf16[4,128,256]{2,1,0:T(8,128)(2,1)S(1)}, u32[]{:S(2)}, u32[]{:S(2)}) collective-permute-start(bf16[4,128,256]{2,1,0:T(8,128)(2,1)S(1)} %get-tuple-element.65.own_ref.own_in), channel_id=1, source_target_pairs={{60,0},{61,1},{62,2},{63,3},{0,4},{1,5},{2,6},{3,7},{4,8},{5,9},{6... | collective-permute-start | bytes 786440 | tf_op jit(solution)/shard_map/ppermute | solution.py:326
  68.2 5.4 %copy-start.17 = (bf16[4,128,256]{2,1,0:T(8,128)(2,1)}, bf16[4,128,256]{2,1,0:T(8,128)(2,1)S(1)}, u32[]{:S(2)}) copy-start(bf16[4,128,256]{2,1,0:T(8,128)(2,1)S(1)} %collective-permute-done.1.back_ref) | copy-start | bytes 786436
  73.7 0.7 copy-start.15
  76.8 37.3 %collective-permute-start.2 = (bf16[2,4,128,256]{3,2,1,0:T(8,128)(2,1)}, bf16[2,4,128,256]{3,2,1,0:T(8,128)(2,1)S(1)}, u32[]{:S(2)}, u32[]{:S(2)}) collective-permute-start(bf16[2,4,128,256]{3,2,1,0:T(8,128)(2,1)} %get-tuple-element.34), channel_id=1, source_target_pairs={{0,1},{1,2},{2,3},{3,0},{4,5},{5,6},{6,7},{7,4},{8,9},{9,10},{10,1... | collective-permute-start | bytes 1572872 | tf_op jit(solution)/shard_map/ppermute | solution.py:331
  77.4 38.4 %collective-permute-start.3 = (bf16[2,4,128,256]{3,2,1,0:T(8,128)(2,1)}, bf16[2,4,128,256]{3,2,1,0:T(8,128)(2,1)S(1)}, u32[]{:S(2)}, u32[]{:S(2)}) collective-permute-start(bf16[2,4,128,256]{3,2,1,0:T(8,128)(2,1)} %get-tuple-element.35), channel_id=1, source_target_pairs={{0,2},{1,3},{2,0},{3,1},{4,6},{5,7},{6,4},{7,5},{8,10},{9,11},{10,... | collective-permute-start | bytes 1572872 | tf_op jit(solution)/shard_map/ppermute | solution.py:331
  78.5 4.5 %copy-start.2 = (bf16[4,2,128,1024]{3,2,1,0:T(8,128)(2,1)}, bf16[4,2,128,1024]{3,2,1,0:T(8,128)(2,1)S(1)}, u32[]{:S(2)}) copy-start(bf16[4,2,128,1024]{3,2,1,0:T(8,128)(2,1)S(1)} %all-to-all-done.3.qd_ref) | copy-start | bytes 6291460
  78.5 37.4 %all-to-all-start = ((bf16[4,2,128,1024]{3,2,1,0:T(8,128)(2,1)}), bf16[4,2,128,1024]{3,2,1,0:T(8,128)(2,1)}, u32[]{:S(2)}, u32[]{:S(2)}) async-start(bf16[4,2,128,1024]{3,2,1,0:T(8,128)(2,1)} %pack_rows.2), calls=%async_computation | async-start | bytes 4194304 | tf_op jit(solution)/shard_map/all_to_all | solution.py:392
  83.0 32.9 %collective-permute-start.4 = (bf16[2,4,128,256]{3,2,1,0:T(8,128)(2,1)}, bf16[2,4,128,256]{3,2,1,0:T(8,128)(2,1)}, u32[]{:S(2)}, u32[]{:S(2)}) collective-permute-start(bf16[2,4,128,256]{3,2,1,0:T(8,128)(2,1)} %get-tuple-element.36), channel_id=1, source_target_pairs={{0,3},{1,0},{2,1},{3,2},{4,7},{5,4},{6,5},{7,6},{8,11},{9,8},{10,9... | collective-permute-start | bytes 1572872 | tf_op jit(solution)/shard_map/ppermute | solution.py:331
  113.7 32.9 %collective-permute-start.10 = (bf16[2,4,128,256]{3,2,1,0:T(8,128)(2,1)}, bf16[2,4,128,256]{3,2,1,0:T(8,128)(2,1)S(1)}, u32[]{:S(2)}, u32[]{:S(2)}) collective-permute-start(bf16[2,4,128,256]{3,2,1,0:T(8,128)(2,1)} %get-tuple-element.48), channel_id=1, source_target_pairs={{0,3},{1,0},{2,1},{3,2},{4,7},{5,4},{6,5},{7,6},{8,11},{9,8},{10,9... | collective-permute-start | bytes 1572872 | tf_op jit(solution)/shard_map/ppermute | solution.py:331
  113.8 34.1 %collective-permute-start.11 = (bf16[2,4,128,256]{3,2,1,0:T(8,128)(2,1)}, bf16[2,4,128,256]{3,2,1,0:T(8,128)(2,1)S(1)}, u32[]{:S(2)}, u32[]{:S(2)}) collective-permute-start(bf16[2,4,128,256]{3,2,1,0:T(8,128)(2,1)} %get-tuple-element.49), channel_id=1, source_target_pairs={{0,2},{1,3},{2,0},{3,1},{4,6},{5,7},{6,4},{7,5},{8,10},{9,11},{10,... | collective-permute-start | bytes 1572872 | tf_op jit(solution)/shard_map/ppermute | solution.py:331
  114.1 1.8 copy-start.18
  114.1 33.8 %collective-permute-start.12 = (bf16[2,4,128,256]{3,2,1,0:T(8,128)(2,1)}, bf16[2,4,128,256]{3,2,1,0:T(8,128)(2,1)S(1)}, u32[]{:S(2)}, u32[]{:S(2)}) collective-permute-start(bf16[2,4,128,256]{3,2,1,0:T(8,128)(2,1)} %get-tuple-element.50), channel_id=1, source_target_pairs={{0,1},{1,2},{2,3},{3,0},{4,5},{5,6},{6,7},{7,4},{8,9},{9,10},{10,1... | collective-permute-start | bytes 1572872 | tf_op jit(solution)/shard_map/ppermute | solution.py:331
  115.9 0.8 copy-start.19
  145.8 15.0 %collective-permute-start.15 = (bf16[2,4,128,256]{3,2,1,0:T(8,128)(2,1)}, bf16[2,4,128,256]{3,2,1,0:T(8,128)(2,1)S(1)}, u32[]{:S(2)}, u32[]{:S(2)}) collective-permute-start(bf16[2,4,128,256]{3,2,1,0:T(8,128)(2,1)} %get-tuple-element.56), channel_id=1, source_target_pairs={{0,3},{1,0},{2,1},{3,2},{4,7},{5,4},{6,5},{7,6},{8,11},{9,8},{10,9... | collective-permute-start | bytes 1572872 | tf_op jit(solution)/shard_map/ppermute | solution.py:331
  145.8 16.6 %collective-permute-start.16 = (bf16[2,4,128,256]{3,2,1,0:T(8,128)(2,1)}, bf16[2,4,128,256]{3,2,1,0:T(8,128)(2,1)S(1)}, u32[]{:S(2)}, u32[]{:S(2)}) collective-permute-start(bf16[2,4,128,256]{3,2,1,0:T(8,128)(2,1)} %get-tuple-element.57), channel_id=1, source_target_pairs={{0,2},{1,3},{2,0},{3,1},{4,6},{5,7},{6,4},{7,5},{8,10},{9,11},{10,... | collective-permute-start | bytes 1572872 | tf_op jit(solution)/shard_map/ppermute | solution.py:331
  146.7 1.2 copy-start.5
  146.7 25.5 %collective-permute-start.17 = (bf16[2,4,128,256]{3,2,1,0:T(8,128)(2,1)}, bf16[2,4,128,256]{3,2,1,0:T(8,128)(2,1)S(1)}, u32[]{:S(2)}, u32[]{:S(2)}) collective-permute-start(bf16[2,4,128,256]{3,2,1,0:T(8,128)(2,1)} %get-tuple-element.58), channel_id=1, source_target_pairs={{0,1},{1,2},{2,3},{3,0},{4,5},{5,6},{6,7},{7,4},{8,9},{9,10},{10,1... | collective-permute-start | bytes 1572872 | tf_op jit(solution)/shard_map/ppermute | solution.py:331
  147.9 0.9 copy-start.6
  147.9 1.0 copy-start.7
  152.7 26.2 %collective-permute-start.13 = (bf16[4,128,256]{2,1,0:T(8,128)(2,1)}, bf16[4,128,256]{2,1,0:T(8,128)(2,1)S(1)}, u32[]{:S(2)}, u32[]{:S(2)}) collective-permute-start(bf16[4,128,256]{2,1,0:T(8,128)(2,1)} %get-tuple-element.52), channel_id=1, source_target_pairs={{4,0},{5,1},{6,2},{7,3},{8,4},{9,5},{10,6},{11,7},{12,8},{13,9},{1... | collective-permute-start | bytes 786440 | tf_op jit(solution)/shard_map/ppermute | solution.py:326
  156.0 22.8 %collective-permute-start.14 = (bf16[4,128,256]{2,1,0:T(8,128)(2,1)}, bf16[4,128,256]{2,1,0:T(8,128)(2,1)}, u32[]{:S(2)}, u32[]{:S(2)}) collective-permute-start(bf16[4,128,256]{2,1,0:T(8,128)(2,1)} %get-tuple-element.53), channel_id=1, source_target_pairs={{8,0},{9,1},{10,2},{11,3},{12,4},{13,5},{14,6},{15,7},{16,8},{17,9... | collective-permute-start | bytes 786440 | tf_op jit(solution)/shard_map/ppermute | solution.py:326
  160.8 11.4 %copy-start.8 = (bf16[2,4,128,256]{3,2,1,0:T(8,128)(2,1)}, bf16[2,4,128,256]{3,2,1,0:T(8,128)(2,1)S(1)}, u32[]{:S(2)}) copy-start(bf16[2,4,128,256]{3,2,1,0:T(8,128)(2,1)S(1)} %collective-permute-done.15.refs_0_) | copy-start | bytes 1572868
  162.4 9.8 %copy-start.9 = (bf16[2,4,128,256]{3,2,1,0:T(8,128)(2,1)}, bf16[2,4,128,256]{3,2,1,0:T(8,128)(2,1)S(1)}, u32[]{:S(2)}) copy-start(bf16[2,4,128,256]{3,2,1,0:T(8,128)(2,1)S(1)} %collective-permute-done.16.refs_1_) | copy-start | bytes 1572868
  172.2 0.8 copy-start.10
  176.8 38.1 %copy-start.1 = (bf16[4,2,128,1024]{3,2,1,0:T(8,128)(2,1)S(1)}, bf16[4,2,128,1024]{3,2,1,0:T(8,128)(2,1)}, u32[]{:S(2)}) copy-start(bf16[4,2,128,1024]{3,2,1,0:T(8,128)(2,1)} %get-tuple-element.41) | copy-start | bytes 6291460
  176.8 8.9 %collective-permute-start.18 = (bf16[4,128,256]{2,1,0:T(8,128)(2,1)}, bf16[4,128,256]{2,1,0:T(8,128)(2,1)S(1)}, u32[]{:S(2)}, u32[]{:S(2)}) collective-permute-start(bf16[4,128,256]{2,1,0:T(8,128)(2,1)} %get-tuple-element.60), channel_id=1, source_target_pairs={{4,0},{5,1},{6,2},{7,3},{8,4},{9,5},{10,6},{11,7},{12,8},{13,9},{1... | collective-permute-start | bytes 786440 | tf_op jit(solution)/shard_map/ppermute | solution.py:326
  178.7 17.1 %collective-permute-start.19 = (bf16[4,128,256]{2,1,0:T(8,128)(2,1)}, bf16[4,128,256]{2,1,0:T(8,128)(2,1)S(1)}, u32[]{:S(2)}, u32[]{:S(2)}) collective-permute-start(bf16[4,128,256]{2,1,0:T(8,128)(2,1)} %get-tuple-element.61), channel_id=1, source_target_pairs={{8,0},{9,1},{10,2},{11,3},{12,4},{13,5},{14,6},{15,7},{16,8},{17,9... | collective-permute-start | bytes 786440 | tf_op jit(solution)/shard_map/ppermute | solution.py:326
  178.8 17.0 %copy-start.11 = (bf16[4,128,256]{2,1,0:T(8,128)(2,1)}, bf16[4,128,256]{2,1,0:T(8,128)(2,1)S(1)}, u32[]{:S(2)}) copy-start(bf16[4,128,256]{2,1,0:T(8,128)(2,1)S(1)} %collective-permute-done.13.refs_1_) | copy-start | bytes 786436
  185.7 10.1 %copy-start.12 = (bf16[4,128,256]{2,1,0:T(8,128)(2,1)}, bf16[4,128,256]{2,1,0:T(8,128)(2,1)S(1)}, u32[]{:S(2)}) copy-start(bf16[4,128,256]{2,1,0:T(8,128)(2,1)S(1)} %collective-permute-done.18.refs_4_) | copy-start | bytes 786436
  195.8 0.7 copy-start.13
  245.2 30.8 %all-to-all-start.2 = ((bf16[4,2,128,1024]{3,2,1,0:T(8,128)(2,1)}), bf16[4,2,128,1024]{3,2,1,0:T(8,128)(2,1)S(1)}, u32[]{:S(2)}, u32[]{:S(2)}) async-start(bf16[4,2,128,1024]{3,2,1,0:T(8,128)(2,1)} %get-tuple-element.37), calls=%async_computation.2 | async-start | bytes 4194304 | tf_op jit(solution)/shard_map/all_to_all | solution.py:392
  276.0 1.3 copy-start

commit v4 on v3

--- a/solution.py
+++ b/solution.py
@@ -176,21 +176,23 @@
 
     @pl.when(t == NB - 1)
     def _():
-        left, right = pl.ds(0, HEAD_SIZE), pl.ds(HEAD_SIZE, HEAD_SIZE)
+        upper, lower = pl.ds(0, HEAD_SIZE), pl.ds(HEAD_SIZE, HEAD_SIZE)
         for c in range(NB):
             for at, ref in enumerate((own_out, prev_out)):
-                ref[c, :, left] = (dkv[at * NB + c, left] * SCALE).T
-                ref[c, :, right] = dkv[at * NB + c, right].T
+                ref[c, upper] = dkv[at * NB + c, upper] * SCALE
+                ref[c, lower] = dkv[at * NB + c, lower]
             for d, ref in enumerate((part_1, part_2, part_3), 1):
                 for m in range(2):
                     at = (2 * d + m) * NB + c
-                    ref[m, c, :, left] = (dkv[at, left] * SCALE).astype(BF16).T
-                    ref[m, c, :, right] = dkv[at, right].astype(BF16).T
+                    ref[m, c, upper] = (dkv[at, upper] * SCALE).astype(BF16)
+                    ref[m, c, lower] = dkv[at, lower].astype(BF16)
 
 
 def attend_call(codes, counts, place, qd, own, prev, near):
     whole = pl.BlockSpec((2, NB, BLOCK, 2 * HEAD_SIZE), lambda t, *_: (0, 0, 0, 0))
     flat = pl.BlockSpec((NB, BLOCK, 2 * HEAD_SIZE), lambda t, *_: (0, 0, 0))
+    whole_t = pl.BlockSpec((2, NB, 2 * HEAD_SIZE, BLOCK), lambda t, *_: (0, 0, 0, 0))
+    flat_t = pl.BlockSpec((NB, 2 * HEAD_SIZE, BLOCK), lambda t, *_: (0, 0, 0))
     block = pl.BlockSpec((None, 2, BLOCK, WIDE), lambda t, *_: (t, 0, 0, 0))
     return pl.pallas_call(
         attend,
@@ -199,7 +201,7 @@
             num_scalar_prefetch=3,
             grid=(NB,),
             in_specs=[block, flat, flat, whole, whole, whole],
-            out_specs=[block, flat, flat, whole, whole, whole],
+            out_specs=[block, flat_t, flat_t, whole_t, whole_t, whole_t],
             scratch_shapes=[
                 pltpu.SMEM((NB, MOST + 8), jnp.int32),
                 pltpu.SMEM((NB,), jnp.int32),
@@ -218,10 +220,10 @@
         ),
         out_shape=[
             jax.ShapeDtypeStruct(qd.shape, BF16),
-            jax.ShapeDtypeStruct((NB, BLOCK, 2 * HEAD_SIZE), F32),
-            jax.ShapeDtypeStruct((NB, BLOCK, 2 * HEAD_SIZE), F32),
+            jax.ShapeDtypeStruct((NB, 2 * HEAD_SIZE, BLOCK), F32),
+            jax.ShapeDtypeStruct((NB, 2 * HEAD_SIZE, BLOCK), F32),
         ]
-        + [jax.ShapeDtypeStruct((2, NB, BLOCK, 2 * HEAD_SIZE), BF16)] * 3,
+        + [jax.ShapeDtypeStruct((2, NB, 2 * HEAD_SIZE, BLOCK), BF16)] * 3,
         cost_estimate=pl.CostEstimate(flops=30_000_000_000, bytes_accessed=20_000_000, transcendentals=70_000_000),
         compiler_params=pltpu.CompilerParams(dimension_semantics=("arbitrary",), vmem_limit_bytes=58 * 1024 * 1024),
     )(codes, counts, place, qd, own, prev, *near)
@@ -346,7 +348,7 @@
         prev_out[...] = before.astype(BF16)
         back_out[...] = back.astype(BF16)
 
-    block = (BLOCK, 2 * HEAD_SIZE)
+    block = (2 * HEAD_SIZE, BLOCK)
     flat = pl.BlockSpec((None,) + block, lambda c: (c, 0, 0))
     pair = pl.BlockSpec((2, None) + block, lambda c: (0, c, 0, 0))
     return pl.pallas_call(
@@ -368,10 +370,12 @@
         out = refs[-1]
         for j in range(2):
             own, prev, back = (ref[...].astype(F32) for ref in refs[3 * j : 3 * j + 3])
-            out[j] = (own + prev + back).astype(BF16)
+            low = (own + prev + back).astype(BF16)
+            out[j, :, pl.ds(0, HEAD_SIZE)] = low[:HEAD_SIZE].T
+            out[j, :, pl.ds(HEAD_SIZE, HEAD_SIZE)] = low[HEAD_SIZE:].T
 
     block = (BLOCK, 2 * HEAD_SIZE)
-    flat = pl.BlockSpec((None,) + block, lambda c: (c, 0, 0))
+    flat = pl.BlockSpec((None, 2 * HEAD_SIZE, BLOCK), lambda c: (c, 0, 0))
     return pl.pallas_call(
         kernel,
         name="add_home",

time: 282 us -> 281 us (level)
  no operation moved by 1% of the time
where the time goes in v4:
time: 281 us; the launch traced here: 280 us
  Pallas kernels  92 us (33%)
  waiting for transfers between devices  91.8 us (33%)
  blocking collectives  45.2 us (16%)
  starting transfers between devices  44.2 us (16%)
  local copies, waits for them, and re-layouts  6.08 us (2%)
    pallas_call x2, Pallas kernels, attend_call(): pl.pallas_call(attend, name='attend', grid_spec=pltpu.PrefetchScalarGridS...  57.1 us
    ppermute x8, waiting for transfers between devices, shifted(): return lax.ppermute(x, 'blk', [((i - distance) % n, i) for i in range(n)])  47.7 us
    all_to_all x2, blocking collectives, swap(): return lax.all_to_all(x, 'head', split_axis=0, concat_axis=0, tiled=True)  45.2 us
    all_to_all x4, waiting for transfers between devices, swap(): return lax.all_to_all(x, 'head', split_axis=0, concat_axis=0, tiled=True)  28 us
    ppermute x12, waiting for transfers between devices, turned_in_quad(): lax.ppermute(x, 'blk', [(i, i - i % QUAD + (i + d) % QUAD) for i in range...  16.2 us
    all_to_all x4, starting transfers between devices, swap(): return lax.all_to_all(x, 'head', split_axis=0, concat_axis=0, tiled=True)  16 us
    ppermute x8, starting transfers between devices, shifted(): return lax.ppermute(x, 'blk', [((i - distance) % n, i) for i in range(n)])  14.8 us
    ppermute x12, starting transfers between devices, turned_in_quad(): lax.ppermute(x, 'blk', [(i, i - i % QUAD + (i + d) % QUAD) for i in range...  13.4 us
  transfers between devices with their start and end apart: 24, of which 10 were waited for; matrix products, arithmetic and copies ran while one was open for 0% of the time, Pallas kernels for 30%

profile of v4, /device:TPU:96, one launch (start us, length us, event | category | flops | bytes accessed | tf_op | source)
XLA Modules:
  0.0 280.2 jit_solution(2281836867713124074)
XLA Ops:
  0.6 1.9 pack_keys.1
  2.5 4.3 %all-to-all-start.1 = ((bf16[4,2,128,256]{3,2,1,0:T(8,128)(2,1)}), bf16[4,2,128,256]{3,2,1,0:T(8,128)(2,1)S(1)}, u32[]{:S(2)}, u32[]{:S(2)}) async-start(bf16[4,2,128,256]{3,2,1,0:T(8,128)(2,1)} %pack_keys.1), calls=%async_computation.1 | async-start | bytes 1048576 | tf_op jit(solution)/shard_map/all_to_all | solution.py:396
  6.8 3.8 %pack_rows.3 = bf16[4,2,128,1024]{3,2,1,0:T(8,128)(2,1)} custom-call(bf16[128,8192]{1,0:T(8,128)(2,1)} %q_ref.3, bf16[128,8192]{1,0:T(8,128)(2,1)} %g_ref.3), custom_call_target="tpu_custom_call" | custom-call | tf_op jit(solution)/shard_map/pack_rows/pallas_call | solution.py:240
  10.6 6.6 %all-to-all-done.1 = bf16[4,2,128,256]{3,2,1,0:T(8,128)(2,1)S(1)} async-done(((bf16[4,2,128,256]{3,2,1,0:T(8,128)(2,1)}), bf16[4,2,128,256]{3,2,1,0:T(8,128)(2,1)S(1)}, u32[]{:S(2)}, u32[]{:S(2)}) %all-to-all-start.1) | async-done | bytes 524320 | tf_op jit(solution)/shard_map/all_to_all | solution.py:396
  17.2 3.6 %all-to-all-start.3 = ((bf16[4,2,128,1024]{3,2,1,0:T(8,128)(2,1)}), bf16[4,2,128,1024]{3,2,1,0:T(8,128)(2,1)S(1)}, u32[]{:S(2)}, u32[]{:S(2)}) async-start(bf16[4,2,128,1024]{3,2,1,0:T(8,128)(2,1)} %pack_rows.3), calls=%async_computation.3 | async-start | bytes 4194304 | tf_op jit(solution)/shard_map/all_to_all | solution.py:396
  20.8 3.2 %collective-permute-start.6 = (bf16[4,128,256]{2,1,0:T(8,128)(2,1)S(1)}, bf16[4,128,256]{2,1,0:T(8,128)(2,1)S(1)}, u32[]{:S(2)}, u32[]{:S(2)}) collective-permute-start(bf16[4,128,256]{2,1,0:T(8,128)(2,1)S(1)} %get-tuple-element.64.own_ref.own_in), channel_id=1, source_target_pairs={{56,0},{57,1},{58,2},{59,3},{60,4},{61,5},{62,6},{63,7},{0,8},{1,9... | collective-permute-start | bytes 786440 | tf_op jit(solution)/shard_map/ppermute | solution.py:328
  24.7 5.5 %collective-permute-done.6.back_ref = bf16[4,128,256]{2,1,0:T(8,128)(2,1)S(1)} collective-permute-done((bf16[4,128,256]{2,1,0:T(8,128)(2,1)S(1)}, bf16[4,128,256]{2,1,0:T(8,128)(2,1)S(1)}, u32[]{:S(2)}, u32[]{:S(2)}) %collective-permute-start.6) | collective-permute-done | bytes 262176 | tf_op jit(solution)/shard_map/ppermute | solution.py:328
  30.2 19.7 %collective-permute-done.5.prev_ref.prev_in = bf16[4,128,256]{2,1,0:T(8,128)(2,1)S(1)} collective-permute-done((bf16[4,128,256]{2,1,0:T(8,128)(2,1)S(1)}, bf16[4,128,256]{2,1,0:T(8,128)(2,1)S(1)}, u32[]{:S(2)}, u32[]{:S(2)}) %collective-permute-start.5) | collective-permute-done | bytes 262176 | tf_op jit(solution)/shard_map/ppermute | solution.py:328
  50.6 2.4 pack_window.3
  53.0 1.6 collective-permute-start.7
  54.6 2.9 %collective-permute-start.8 = (bf16[2,4,128,256]{3,2,1,0:T(8,128)(2,1)}, bf16[2,4,128,256]{3,2,1,0:T(8,128)(2,1)}, u32[]{:S(2)}, u32[]{:S(2)}) collective-permute-start(bf16[2,4,128,256]{3,2,1,0:T(8,128)(2,1)} %get-tuple-element.39), channel_id=1, source_target_pairs={{0,2},{1,3},{2,0},{3,1},{4,6},{5,7},{6,4},{7,5},{8,10},{9,11},{10,... | collective-permute-start | bytes 1572872 | tf_op jit(solution)/shard_map/ppermute | solution.py:333
  57.5 1.4 collective-permute-start.9
  58.8 3.1 %collective-permute-start.1 = (bf16[4,128,256]{2,1,0:T(8,128)(2,1)S(1)}, bf16[4,128,256]{2,1,0:T(8,128)(2,1)S(1)}, u32[]{:S(2)}, u32[]{:S(2)}) collective-permute-start(bf16[4,128,256]{2,1,0:T(8,128)(2,1)S(1)} %get-tuple-element.65.own_ref.own_in), channel_id=1, source_target_pairs={{56,0},{57,1},{58,2},{59,3},{60,4},{61,5},{62,6},{63,7},{0,8},{1,9... | collective-permute-start | bytes 786440 | tf_op jit(solution)/shard_map/ppermute | solution.py:328
  62.0 2.5 collective-permute-start
  64.5 3.8 %pack_rows.2 = bf16[4,2,128,1024]{3,2,1,0:T(8,128)(2,1)} custom-call(bf16[128,8192]{1,0:T(8,128)(2,1)} %q_ref.3, bf16[128,8192]{1,0:T(8,128)(2,1)} %g_ref.3), custom_call_target="tpu_custom_call" | custom-call | tf_op jit(solution)/shard_map/pack_rows/pallas_call | solution.py:240
  68.2 5.4 %collective-permute-done.prev_ref.prev_in = bf16[4,128,256]{2,1,0:T(8,128)(2,1)S(1)} collective-permute-done((bf16[4,128,256]{2,1,0:T(8,128)(2,1)S(1)}, bf16[4,128,256]{2,1,0:T(8,128)(2,1)S(1)}, u32[]{:S(2)}, u32[]{:S(2)}) %collective-permute-start) | collective-permute-done | bytes 262176 | tf_op jit(solution)/shard_map/ppermute | solution.py:328
  73.7 0.7 copy-done.15
  74.4 2.4 pack_window.2
  77.4 1.1 collective-permute-start.3
  78.5 4.5 %all-to-all-start = ((bf16[4,2,128,1024]{3,2,1,0:T(8,128)(2,1)}), bf16[4,2,128,1024]{3,2,1,0:T(8,128)(2,1)}, u32[]{:S(2)}, u32[]{:S(2)}) async-start(bf16[4,2,128,1024]{3,2,1,0:T(8,128)(2,1)} %pack_rows.2), calls=%async_computation | async-start | bytes 4194304 | tf_op jit(solution)/shard_map/all_to_all | solution.py:396
  83.0 1.7 collective-permute-start.4
  84.7 28.5 %attend.3 = (bf16[4,2,128,1024]{3,2,1,0:T(8,128)(2,1)}, f32[4,256,128]{2,1,0:T(8,128)}, f32[4,256,128]{2,1,0:T(8,128)}, bf16[2,4,256,128]{3,2,1,0:T(8,128)(2,1)}...) custom-call(s32[8,8]{1,0:T(8,128)} %bitcast.11, s32[8]{0:T(128)} %bitcast.13, s32[1]{0:T(128)} %bitcast.2.y_ref.place, ...), custom_call_target="tpu_custom_call" | custom-call | flops 30000001024 | bytes 20000000 | tf_op jit(solution)/shard_map/attend/pallas_call | solution.py:197
  113.6 1.8 collective-permute-start.12
  115.4 0.8 copy-done.19
  116.2 28.5 %attend.2 = (bf16[4,2,128,1024]{3,2,1,0:T(8,128)(2,1)}, f32[4,256,128]{2,1,0:T(8,128)}, f32[4,256,128]{2,1,0:T(8,128)}, bf16[2,4,256,128]{3,2,1,0:T(8,128)(2,1)}...) custom-call(s32[8,8]{1,0:T(8,128)} %bitcast.12, s32[8]{0:T(128)} %bitcast.14, s32[1]{0:T(128)} %bitcast.2.y_ref.place, ...), custom_call_target="tpu_custom_call" | custom-call | flops 30000001024 | bytes 20000000 | tf_op jit(solution)/shard_map/attend/pallas_call | solution.py:197
  144.7 0.9 collective-permute-start.16
  145.6 1.2 collective-permute-start.17
  146.9 0.8 copy-done.6
  147.9 3.8 %add_parts.2 = (f32[4,256,128]{2,1,0:T(8,128)}, bf16[4,256,128]{2,1,0:T(8,128)(2,1)}, bf16[4,256,128]{2,1,0:T(8,128)(2,1)}) custom-call(s32[1]{0:T(128)} %bitcast.2.y_ref.place, f32[4,256,128]{2,1,0:T(8,128)} %get-tuple-element.46.own_ref, f32[4,256,128]{2,1,0:T(8,128)} %get-tuple-element.47.prev_ref, bf16[2,4,256,128]{3,2,1,0:T(8,128)(2,1)} %copy-done.5, ...), custom_call_target="tpu_custom_call" | custom-call | tf_op jit(solution)/shard_map/add_parts/pallas_call | solution.py:354
  151.6 3.3 %collective-permute-start.13 = (bf16[4,256,128]{2,1,0:T(8,128)(2,1)}, bf16[4,256,128]{2,1,0:T(8,128)(2,1)S(1)}, u32[]{:S(2)}, u32[]{:S(2)}) collective-permute-start(bf16[4,256,128]{2,1,0:T(8,128)(2,1)} %get-tuple-element.52), channel_id=1, source_target_pairs={{4,0},{5,1},{6,2},{7,3},{8,4},{9,5},{10,6},{11,7},{12,8},{13,9},{1... | collective-permute-start | bytes 786440 | tf_op jit(solution)/shard_map/ppermute | solution.py:328
  155.0 4.8 %collective-permute-done.15.refs_0_ = bf16[2,4,256,128]{3,2,1,0:T(8,128)(2,1)S(1)} collective-permute-done((bf16[2,4,256,128]{3,2,1,0:T(8,128)(2,1)}, bf16[2,4,256,128]{3,2,1,0:T(8,128)(2,1)S(1)}, u32[]{:S(2)}, u32[]{:S(2)}) %collective-permute-start.15) | collective-permute-done | bytes 524320 | tf_op jit(solution)/shard_map/ppermute | solution.py:333
  159.7 1.6 collective-permute-done.16.refs_1_
  161.4 9.7 %collective-permute-done.17.refs_2_ = bf16[2,4,256,128]{3,2,1,0:T(8,128)(2,1)S(1)} collective-permute-done((bf16[2,4,256,128]{3,2,1,0:T(8,128)(2,1)}, bf16[2,4,256,128]{3,2,1,0:T(8,128)(2,1)S(1)}, u32[]{:S(2)}, u32[]{:S(2)}) %collective-permute-start.17) | collective-permute-done | bytes 524320 | tf_op jit(solution)/shard_map/ppermute | solution.py:333
  171.1 0.8 copy-done.10
  171.9 3.8 %add_parts.3 = (f32[4,256,128]{2,1,0:T(8,128)}, bf16[4,256,128]{2,1,0:T(8,128)(2,1)}, bf16[4,256,128]{2,1,0:T(8,128)(2,1)}) custom-call(s32[1]{0:T(128)} %bitcast.2.y_ref.place, f32[4,256,128]{2,1,0:T(8,128)} %get-tuple-element.54.own_ref, f32[4,256,128]{2,1,0:T(8,128)} %get-tuple-element.55.prev_ref, bf16[2,4,256,128]{3,2,1,0:T(8,128)(2,1)} %copy-done.8, ...), custom_call_target="tpu_custom_call" | custom-call | tf_op jit(solution)/shard_map/add_parts/pallas_call | solution.py:354
  175.8 1.9 collective-permute-start.18
  177.8 6.9 %collective-permute-done.18.refs_4_ = bf16[4,256,128]{2,1,0:T(8,128)(2,1)S(1)} collective-permute-done((bf16[4,256,128]{2,1,0:T(8,128)(2,1)}, bf16[4,256,128]{2,1,0:T(8,128)(2,1)S(1)}, u32[]{:S(2)}, u32[]{:S(2)}) %collective-permute-start.18) | collective-permute-done | bytes 262176 | tf_op jit(solution)/shard_map/ppermute | solution.py:328
  184.7 10.1 %collective-permute-done.19.refs_5_ = bf16[4,256,128]{2,1,0:T(8,128)(2,1)S(1)} collective-permute-done((bf16[4,256,128]{2,1,0:T(8,128)(2,1)}, bf16[4,256,128]{2,1,0:T(8,128)(2,1)S(1)}, u32[]{:S(2)}, u32[]{:S(2)}) %collective-permute-start.19) | collective-permute-done | bytes 262176 | tf_op jit(solution)/shard_map/ppermute | solution.py:328
  194.8 0.7 copy-done.13
  195.5 3.6 %add_home.1 = bf16[4,2,128,256]{3,2,1,0:T(8,128)(2,1)} custom-call(f32[4,256,128]{2,1,0:T(8,128)} %get-tuple-element.51.refs_0_, bf16[4,256,128]{2,1,0:T(8,128)(2,1)} %copy-done.11, bf16[4,256,128]{2,1,0:T(8,128)(2,1)} %collective-permute-done.14.refs_2_, f32[4,256,128]{2,1,0:T(8,128)} %get-tuple-element.59.refs_3_, bf16[4,256,128]{2,1,0:T(8,128)(2,1)} %copy-done.12, ...), custom_call_target="tpu_custom_call" | custom-call | tf_op jit(solution)/shard_map/add_home/pallas_call | solution.py:379
  199.1 14.8 %all_to_all.30.got_ref = bf16[4,2,128,256]{3,2,1,0:T(8,128)(2,1)} all-to-all(bf16[4,2,128,256]{3,2,1,0:T(8,128)(2,1)} %add_home.1), channel_id=1, replica_groups=mesh['head'=4,'blk'=64] {'head'}, dimensions={0} | all-to-all | bytes 1048576 | tf_op jit(solution)/shard_map/all_to_all | solution.py:396
  213.9 30.4 %all_to_all.31.got_ref = bf16[4,2,128,1024]{3,2,1,0:T(8,128)(2,1)} all-to-all(bf16[4,2,128,1024]{3,2,1,0:T(8,128)(2,1)S(1)} %copy-done.1), channel_id=1, replica_groups=mesh['head'=4,'blk'=64] {'head'}, dimensions={0} | all-to-all | bytes 4194304 | tf_op jit(solution)/shard_map/all_to_all | solution.py:396
  244.3 3.6 %all-to-all-start.2 = ((bf16[4,2,128,1024]{3,2,1,0:T(8,128)(2,1)}), bf16[4,2,128,1024]{3,2,1,0:T(8,128)(2,1)S(1)}, u32[]{:S(2)}, u32[]{:S(2)}) async-start(bf16[4,2,128,1024]{3,2,1,0:T(8,128)(2,1)} %get-tuple-element.37), calls=%async_computation.2 | async-start | bytes 4194304 | tf_op jit(solution)/shard_map/all_to_all | solution.py:396
  247.9 2.0 unpack_keys.1
  249.9 3.8 %unpack_rows.2 = (bf16[128,8192]{1,0:T(8,128)(2,1)}, bf16[128,8192]{1,0:T(8,128)(2,1)}) custom-call(bf16[4,2,128,1024]{3,2,1,0:T(8,128)(2,1)} %all_to_all.31.got_ref), custom_call_target="tpu_custom_call" | custom-call | tf_op jit(solution)/shard_map/unpack_rows/pallas_call | solution.py:301
  253.7 21.4 %all-to-all-done.2.got_ref = bf16[4,2,128,1024]{3,2,1,0:T(8,128)(2,1)S(1)} async-done(((bf16[4,2,128,1024]{3,2,1,0:T(8,128)(2,1)}), bf16[4,2,128,1024]{3,2,1,0:T(8,128)(2,1)S(1)}, u32[]{:S(2)}, u32[]{:S(2)}) %all-to-all-start.2) | async-done | bytes 2097184 | tf_op jit(solution)/shard_map/all_to_all | solution.py:396
  275.1 1.3 copy-done
  276.4 3.8 %unpack_rows.3 = (bf16[128,8192]{1,0:T(8,128)(2,1)}, bf16[128,8192]{1,0:T(8,128)(2,1)}) custom-call(bf16[4,2,128,1024]{3,2,1,0:T(8,128)(2,1)} %copy-done, bf16[128,8192]{1,0:T(8,128)(2,1)} %get-tuple-element.42.refs_0_, bf16[128,8192]{1,0:T(8,128)(2,1)} %get-tuple-element.43.refs_1_), custom_call_target="tpu_custom_call", output_to_operand_aliasing={{0}: (1, {}), {1}: (2, {})} | custom-call | tf_op jit(solution)/shard_map/unpack_rows/pallas_call | solution.py:301
  (56 shorter events, 2.7 us)
Async XLA Ops:
  2.5 14.6 %all-to-all-start.1 = ((bf16[4,2,128,256]{3,2,1,0:T(8,128)(2,1)}), bf16[4,2,128,256]{3,2,1,0:T(8,128)(2,1)S(1)}, u32[]{:S(2)}, u32[]{:S(2)}) async-start(bf16[4,2,128,256]{3,2,1,0:T(8,128)(2,1)} %pack_keys.1), calls=%async_computation.1 | async-start | bytes 1048576 | tf_op jit(solution)/shard_map/all_to_all | solution.py:396
  17.2 61.4 %all-to-all-start.3 = ((bf16[4,2,128,1024]{3,2,1,0:T(8,128)(2,1)}), bf16[4,2,128,1024]{3,2,1,0:T(8,128)(2,1)S(1)}, u32[]{:S(2)}, u32[]{:S(2)}) async-start(bf16[4,2,128,1024]{3,2,1,0:T(8,128)(2,1)} %pack_rows.3), calls=%async_computation.3 | async-start | bytes 4194304 | tf_op jit(solution)/shard_map/all_to_all | solution.py:396
  20.8 29.1 %copy-start.4 = (bf16[4,128,256]{2,1,0:T(8,128)(2,1)}, bf16[4,128,256]{2,1,0:T(8,128)(2,1)S(1)}, u32[]{:S(2)}) copy-start(bf16[4,128,256]{2,1,0:T(8,128)(2,1)S(1)} %get-tuple-element.64.own_ref.own_in) | copy-start | bytes 786436
  20.8 47.4 %copy-start.3 = (bf16[4,128,256]{2,1,0:T(8,128)(2,1)}, bf16[4,128,256]{2,1,0:T(8,128)(2,1)S(1)}, u32[]{:S(2)}) copy-start(bf16[4,128,256]{2,1,0:T(8,128)(2,1)S(1)} %get-tuple-element.65.own_ref.own_in) | copy-start | bytes 786436
  20.8 9.4 %collective-permute-start.6 = (bf16[4,128,256]{2,1,0:T(8,128)(2,1)S(1)}, bf16[4,128,256]{2,1,0:T(8,128)(2,1)S(1)}, u32[]{:S(2)}, u32[]{:S(2)}) collective-permute-start(bf16[4,128,256]{2,1,0:T(8,128)(2,1)S(1)} %get-tuple-element.64.own_ref.own_in), channel_id=1, source_target_pairs={{56,0},{57,1},{58,2},{59,3},{60,4},{61,5},{62,6},{63,7},{0,8},{1,9... | collective-permute-start | bytes 786440 | tf_op jit(solution)/shard_map/ppermute | solution.py:328
  24.0 25.9 %collective-permute-start.5 = (bf16[4,128,256]{2,1,0:T(8,128)(2,1)S(1)}, bf16[4,128,256]{2,1,0:T(8,128)(2,1)S(1)}, u32[]{:S(2)}, u32[]{:S(2)}) collective-permute-start(bf16[4,128,256]{2,1,0:T(8,128)(2,1)S(1)} %get-tuple-element.64.own_ref.own_in), channel_id=1, source_target_pairs={{60,0},{61,1},{62,2},{63,3},{0,4},{1,5},{2,6},{3,7},{4,8},{5,9},{6... | collective-permute-start | bytes 786440 | tf_op jit(solution)/shard_map/ppermute | solution.py:328
  30.2 19.7 %copy-start.16 = (bf16[4,128,256]{2,1,0:T(8,128)(2,1)}, bf16[4,128,256]{2,1,0:T(8,128)(2,1)S(1)}, u32[]{:S(2)}) copy-start(bf16[4,128,256]{2,1,0:T(8,128)(2,1)S(1)} %collective-permute-done.6.back_ref) | copy-start | bytes 786436
  49.9 0.7 copy-start.14
  53.0 30.0 %collective-permute-start.7 = (bf16[2,4,128,256]{3,2,1,0:T(8,128)(2,1)}, bf16[2,4,128,256]{3,2,1,0:T(8,128)(2,1)}, u32[]{:S(2)}, u32[]{:S(2)}) collective-permute-start(bf16[2,4,128,256]{3,2,1,0:T(8,128)(2,1)} %get-tuple-element.38), channel_id=1, source_target_pairs={{0,1},{1,2},{2,3},{3,0},{4,5},{5,6},{6,7},{7,4},{8,9},{9,10},{10,1... | collective-permute-start | bytes 1572872 | tf_op jit(solution)/shard_map/ppermute | solution.py:333
  54.6 30.1 %collective-permute-start.8 = (bf16[2,4,128,256]{3,2,1,0:T(8,128)(2,1)}, bf16[2,4,128,256]{3,2,1,0:T(8,128)(2,1)}, u32[]{:S(2)}, u32[]{:S(2)}) collective-permute-start(bf16[2,4,128,256]{3,2,1,0:T(8,128)(2,1)} %get-tuple-element.39), channel_id=1, source_target_pairs={{0,2},{1,3},{2,0},{3,1},{4,6},{5,7},{6,4},{7,5},{8,10},{9,11},{10,... | collective-permute-start | bytes 1572872 | tf_op jit(solution)/shard_map/ppermute | solution.py:333
  57.5 27.2 %collective-permute-start.9 = (bf16[2,4,128,256]{3,2,1,0:T(8,128)(2,1)}, bf16[2,4,128,256]{3,2,1,0:T(8,128)(2,1)}, u32[]{:S(2)}, u32[]{:S(2)}) collective-permute-start(bf16[2,4,128,256]{3,2,1,0:T(8,128)(2,1)} %get-tuple-element.40), channel_id=1, source_target_pairs={{0,3},{1,0},{2,1},{3,2},{4,7},{5,4},{6,5},{7,6},{8,11},{9,8},{10,9... | collective-permute-start | bytes 1572872 | tf_op jit(solution)/shard_map/ppermute | solution.py:333
  58.8 9.4 %collective-permute-start.1 = (bf16[4,128,256]{2,1,0:T(8,128)(2,1)S(1)}, bf16[4,128,256]{2,1,0:T(8,128)(2,1)S(1)}, u32[]{:S(2)}, u32[]{:S(2)}) collective-permute-start(bf16[4,128,256]{2,1,0:T(8,128)(2,1)S(1)} %get-tuple-element.65.own_ref.own_in), channel_id=1, source_target_pairs={{56,0},{57,1},{58,2},{59,3},{60,4},{61,5},{62,6},{63,7},{0,8},{1,9... | collective-permute-start | bytes 786440 | tf_op jit(solution)/shard_map/ppermute | solution.py:328
  62.0 11.7 %collective-permute-start = (bf16[4,128,256]{2,1,0:T(8,128)(2,1)S(1)}, bf16[4,128,256]{2,1,0:T(8,128)(2,1)S(1)}, u32[]{:S(2)}, u32[]{:S(2)}) collective-permute-start(bf16[4,128,256]{2,1,0:T(8,128)(2,1)S(1)} %get-tuple-element.65.own_ref.own_in), channel_id=1, source_target_pairs={{60,0},{61,1},{62,2},{63,3},{0,4},{1,5},{2,6},{3,7},{4,8},{5,9},{6... | collective-permute-start | bytes 786440 | tf_op jit(solution)/shard_map/ppermute | solution.py:328
  68.2 5.4 %copy-start.17 = (bf16[4,128,256]{2,1,0:T(8,128)(2,1)}, bf16[4,128,256]{2,1,0:T(8,128)(2,1)S(1)}, u32[]{:S(2)}) copy-start(bf16[4,128,256]{2,1,0:T(8,128)(2,1)S(1)} %collective-permute-done.1.back_ref) | copy-start | bytes 786436
  73.7 0.7 copy-start.15
  76.8 36.8 %collective-permute-start.2 = (bf16[2,4,128,256]{3,2,1,0:T(8,128)(2,1)}, bf16[2,4,128,256]{3,2,1,0:T(8,128)(2,1)S(1)}, u32[]{:S(2)}, u32[]{:S(2)}) collective-permute-start(bf16[2,4,128,256]{3,2,1,0:T(8,128)(2,1)} %get-tuple-element.34), channel_id=1, source_target_pairs={{0,1},{1,2},{2,3},{3,0},{4,5},{5,6},{6,7},{7,4},{8,9},{9,10},{10,1... | collective-permute-start | bytes 1572872 | tf_op jit(solution)/shard_map/ppermute | solution.py:333
  77.4 37.9 %collective-permute-start.3 = (bf16[2,4,128,256]{3,2,1,0:T(8,128)(2,1)}, bf16[2,4,128,256]{3,2,1,0:T(8,128)(2,1)S(1)}, u32[]{:S(2)}, u32[]{:S(2)}) collective-permute-start(bf16[2,4,128,256]{3,2,1,0:T(8,128)(2,1)} %get-tuple-element.35), channel_id=1, source_target_pairs={{0,2},{1,3},{2,0},{3,1},{4,6},{5,7},{6,4},{7,5},{8,10},{9,11},{10,... | collective-permute-start | bytes 1572872 | tf_op jit(solution)/shard_map/ppermute | solution.py:333
  78.5 4.5 %copy-start.2 = (bf16[4,2,128,1024]{3,2,1,0:T(8,128)(2,1)}, bf16[4,2,128,1024]{3,2,1,0:T(8,128)(2,1)S(1)}, u32[]{:S(2)}) copy-start(bf16[4,2,128,1024]{3,2,1,0:T(8,128)(2,1)S(1)} %all-to-all-done.3.qd_ref) | copy-start | bytes 6291460
  78.5 36.9 %all-to-all-start = ((bf16[4,2,128,1024]{3,2,1,0:T(8,128)(2,1)}), bf16[4,2,128,1024]{3,2,1,0:T(8,128)(2,1)}, u32[]{:S(2)}, u32[]{:S(2)}) async-start(bf16[4,2,128,1024]{3,2,1,0:T(8,128)(2,1)} %pack_rows.2), calls=%async_computation | async-start | bytes 4194304 | tf_op jit(solution)/shard_map/all_to_all | solution.py:396
  83.0 32.4 %collective-permute-start.4 = (bf16[2,4,128,256]{3,2,1,0:T(8,128)(2,1)}, bf16[2,4,128,256]{3,2,1,0:T(8,128)(2,1)}, u32[]{:S(2)}, u32[]{:S(2)}) collective-permute-start(bf16[2,4,128,256]{3,2,1,0:T(8,128)(2,1)} %get-tuple-element.36), channel_id=1, source_target_pairs={{0,3},{1,0},{2,1},{3,2},{4,7},{5,4},{6,5},{7,6},{8,11},{9,8},{10,9... | collective-permute-start | bytes 1572872 | tf_op jit(solution)/shard_map/ppermute | solution.py:333
  113.2 32.4 %collective-permute-start.10 = (bf16[2,4,256,128]{3,2,1,0:T(8,128)(2,1)}, bf16[2,4,256,128]{3,2,1,0:T(8,128)(2,1)S(1)}, u32[]{:S(2)}, u32[]{:S(2)}) collective-permute-start(bf16[2,4,256,128]{3,2,1,0:T(8,128)(2,1)} %get-tuple-element.48), channel_id=1, source_target_pairs={{0,3},{1,0},{2,1},{3,2},{4,7},{5,4},{6,5},{7,6},{8,11},{9,8},{10,9... | collective-permute-start | bytes 1572872 | tf_op jit(solution)/shard_map/ppermute | solution.py:333
  113.3 33.6 %collective-permute-start.11 = (bf16[2,4,256,128]{3,2,1,0:T(8,128)(2,1)}, bf16[2,4,256,128]{3,2,1,0:T(8,128)(2,1)S(1)}, u32[]{:S(2)}, u32[]{:S(2)}) collective-permute-start(bf16[2,4,256,128]{3,2,1,0:T(8,128)(2,1)} %get-tuple-element.49), channel_id=1, source_target_pairs={{0,2},{1,3},{2,0},{3,1},{4,6},{5,7},{6,4},{7,5},{8,10},{9,11},{10,... | collective-permute-start | bytes 1572872 | tf_op jit(solution)/shard_map/ppermute | solution.py:333
  113.6 1.8 copy-start.18
  113.6 33.3 %collective-permute-start.12 = (bf16[2,4,256,128]{3,2,1,0:T(8,128)(2,1)}, bf16[2,4,256,128]{3,2,1,0:T(8,128)(2,1)S(1)}, u32[]{:S(2)}, u32[]{:S(2)}) collective-permute-start(bf16[2,4,256,128]{3,2,1,0:T(8,128)(2,1)} %get-tuple-element.50), channel_id=1, source_target_pairs={{0,1},{1,2},{2,3},{3,0},{4,5},{5,6},{6,7},{7,4},{8,9},{9,10},{10,1... | collective-permute-start | bytes 1572872 | tf_op jit(solution)/shard_map/ppermute | solution.py:333
  115.4 0.8 copy-start.19
  144.7 15.0 %collective-permute-start.15 = (bf16[2,4,256,128]{3,2,1,0:T(8,128)(2,1)}, bf16[2,4,256,128]{3,2,1,0:T(8,128)(2,1)S(1)}, u32[]{:S(2)}, u32[]{:S(2)}) collective-permute-start(bf16[2,4,256,128]{3,2,1,0:T(8,128)(2,1)} %get-tuple-element.56), channel_id=1, source_target_pairs={{0,3},{1,0},{2,1},{3,2},{4,7},{5,4},{6,5},{7,6},{8,11},{9,8},{10,9... | collective-permute-start | bytes 1572872 | tf_op jit(solution)/shard_map/ppermute | solution.py:333
  144.7 16.6 %collective-permute-start.16 = (bf16[2,4,256,128]{3,2,1,0:T(8,128)(2,1)}, bf16[2,4,256,128]{3,2,1,0:T(8,128)(2,1)S(1)}, u32[]{:S(2)}, u32[]{:S(2)}) collective-permute-start(bf16[2,4,256,128]{3,2,1,0:T(8,128)(2,1)} %get-tuple-element.57), channel_id=1, source_target_pairs={{0,2},{1,3},{2,0},{3,1},{4,6},{5,7},{6,4},{7,5},{8,10},{9,11},{10,... | collective-permute-start | bytes 1572872 | tf_op jit(solution)/shard_map/ppermute | solution.py:333
  145.6 1.2 copy-start.5
  145.6 25.5 %collective-permute-start.17 = (bf16[2,4,256,128]{3,2,1,0:T(8,128)(2,1)}, bf16[2,4,256,128]{3,2,1,0:T(8,128)(2,1)S(1)}, u32[]{:S(2)}, u32[]{:S(2)}) collective-permute-start(bf16[2,4,256,128]{3,2,1,0:T(8,128)(2,1)} %get-tuple-element.58), channel_id=1, source_target_pairs={{0,1},{1,2},{2,3},{3,0},{4,5},{5,6},{6,7},{7,4},{8,9},{9,10},{10,1... | collective-permute-start | bytes 1572872 | tf_op jit(solution)/shard_map/ppermute | solution.py:333
  146.8 0.9 copy-start.6
  146.9 1.0 copy-start.7
  151.6 26.2 %collective-permute-start.13 = (bf16[4,256,128]{2,1,0:T(8,128)(2,1)}, bf16[4,256,128]{2,1,0:T(8,128)(2,1)S(1)}, u32[]{:S(2)}, u32[]{:S(2)}) collective-permute-start(bf16[4,256,128]{2,1,0:T(8,128)(2,1)} %get-tuple-element.52), channel_id=1, source_target_pairs={{4,0},{5,1},{6,2},{7,3},{8,4},{9,5},{10,6},{11,7},{12,8},{13,9},{1... | collective-permute-start | bytes 786440 | tf_op jit(solution)/shard_map/ppermute | solution.py:328
  155.0 22.8 %collective-permute-start.14 = (bf16[4,256,128]{2,1,0:T(8,128)(2,1)}, bf16[4,256,128]{2,1,0:T(8,128)(2,1)}, u32[]{:S(2)}, u32[]{:S(2)}) collective-permute-start(bf16[4,256,128]{2,1,0:T(8,128)(2,1)} %get-tuple-element.53), channel_id=1, source_target_pairs={{8,0},{9,1},{10,2},{11,3},{12,4},{13,5},{14,6},{15,7},{16,8},{17,9... | collective-permute-start | bytes 786440 | tf_op jit(solution)/shard_map/ppermute | solution.py:328
  159.7 11.4 %copy-start.8 = (bf16[2,4,256,128]{3,2,1,0:T(8,128)(2,1)}, bf16[2,4,256,128]{3,2,1,0:T(8,128)(2,1)S(1)}, u32[]{:S(2)}) copy-start(bf16[2,4,256,128]{3,2,1,0:T(8,128)(2,1)S(1)} %collective-permute-done.15.refs_0_) | copy-start | bytes 1572868
  161.4 9.8 %copy-start.9 = (bf16[2,4,256,128]{3,2,1,0:T(8,128)(2,1)}, bf16[2,4,256,128]{3,2,1,0:T(8,128)(2,1)S(1)}, u32[]{:S(2)}) copy-start(bf16[2,4,256,128]{3,2,1,0:T(8,128)(2,1)S(1)} %collective-permute-done.16.refs_1_) | copy-start | bytes 1572868
  171.1 0.8 copy-start.10
  175.8 38.2 %copy-start.1 = (bf16[4,2,128,1024]{3,2,1,0:T(8,128)(2,1)S(1)}, bf16[4,2,128,1024]{3,2,1,0:T(8,128)(2,1)}, u32[]{:S(2)}) copy-start(bf16[4,2,128,1024]{3,2,1,0:T(8,128)(2,1)} %get-tuple-element.41) | copy-start | bytes 6291460
  175.8 8.9 %collective-permute-start.18 = (bf16[4,256,128]{2,1,0:T(8,128)(2,1)}, bf16[4,256,128]{2,1,0:T(8,128)(2,1)S(1)}, u32[]{:S(2)}, u32[]{:S(2)}) collective-permute-start(bf16[4,256,128]{2,1,0:T(8,128)(2,1)} %get-tuple-element.60), channel_id=1, source_target_pairs={{4,0},{5,1},{6,2},{7,3},{8,4},{9,5},{10,6},{11,7},{12,8},{13,9},{1... | collective-permute-start | bytes 786440 | tf_op jit(solution)/shard_map/ppermute | solution.py:328
  177.7 17.1 %collective-permute-start.19 = (bf16[4,256,128]{2,1,0:T(8,128)(2,1)}, bf16[4,256,128]{2,1,0:T(8,128)(2,1)S(1)}, u32[]{:S(2)}, u32[]{:S(2)}) collective-permute-start(bf16[4,256,128]{2,1,0:T(8,128)(2,1)} %get-tuple-element.61), channel_id=1, source_target_pairs={{8,0},{9,1},{10,2},{11,3},{12,4},{13,5},{14,6},{15,7},{16,8},{17,9... | collective-permute-start | bytes 786440 | tf_op jit(solution)/shard_map/ppermute | solution.py:328
  177.8 17.0 %copy-start.11 = (bf16[4,256,128]{2,1,0:T(8,128)(2,1)}, bf16[4,256,128]{2,1,0:T(8,128)(2,1)S(1)}, u32[]{:S(2)}) copy-start(bf16[4,256,128]{2,1,0:T(8,128)(2,1)S(1)} %collective-permute-done.13.refs_1_) | copy-start | bytes 786436
  184.7 10.1 %copy-start.12 = (bf16[4,256,128]{2,1,0:T(8,128)(2,1)}, bf16[4,256,128]{2,1,0:T(8,128)(2,1)S(1)}, u32[]{:S(2)}) copy-start(bf16[4,256,128]{2,1,0:T(8,128)(2,1)S(1)} %collective-permute-done.18.refs_4_) | copy-start | bytes 786436
  194.8 0.7 copy-start.13
  244.3 30.8 %all-to-all-start.2 = ((bf16[4,2,128,1024]{3,2,1,0:T(8,128)(2,1)}), bf16[4,2,128,1024]{3,2,1,0:T(8,128)(2,1)S(1)}, u32[]{:S(2)}, u32[]{:S(2)}) async-start(bf16[4,2,128,1024]{3,2,1,0:T(8,128)(2,1)} %get-tuple-element.37), calls=%async_computation.2 | async-start | bytes 4194304 | tf_op jit(solution)/shard_map/all_to_all | solution.py:396
  275.1 1.3 copy-start
